TPU v7x, 512 devices: a whole 4x4x16 slice. The times are simulated.
512 devices in a mesh: dp: 16 (over z), shard: 32 (over y, x, core).
Axes of the slice: x: 4, y: 4, z: 16, core: 2. Of those that a mesh axis runs over, the one named last changes fastest.
Arguments:
- hidden_in: bfloat16 [16384, 5120], P('dp', 'shard'), may hold values from -6 to 6
- context_in: bfloat16 [16384, 5120], P('dp', 'shard'), may hold values from -6 to 6
- query_cotan: bfloat16 [16384, 2560], P('dp', 'shard'), may hold values from -0.1875 to 0.1875
- output_cotan: bfloat16 [16384, 2560], P('dp', 'shard'), may hold values from -0.1875 to 0.1875
- query_error: bfloat16 [16, 5120, 2560], P('dp', 'shard'), may hold values from -3 to 3
- output_error: bfloat16 [16, 5120, 2560], P('dp', 'shard'), may hold values from -3 to 3
- query_weight: float32 [5120, 2560], P('shard', 'dp'), may hold values from -0.6 to 0.6
- output_weight: float32 [5120, 2560], P('shard', 'dp'), may hold values from -0.6 to 0.6
- start_factors: bfloat16 [2, 2560, 32], replicated, may hold values from -0.09863281 to 0.09863281
Outputs:
- query_error_new: bfloat16 [16, 5120, 2560], P('dp', 'shard')
- output_error_new: bfloat16 [16, 5120, 2560], P('dp', 'shard')
- query_weight_new: float32 [5120, 2560], P('shard', 'dp')
- output_weight_new: float32 [5120, 2560], P('shard', 'dp')
All inputs are finite; a program needn't handle non-finite values.
Results may differ from a plain program's by a relative error of at most 0.005.
Values may be sent and summed in bfloat16 or wider, within the bound.
No kernel may reach another device: no remote copies, remote signals or barrier semaphores. Data moves between devices by JAX's collectives and lax.ppermute only.
A program may use at most 64 MiB of HBM per device.

v0:
```python
import jax
import jax.numpy as jnp
from jax import lax
from jax.sharding import PartitionSpec as P

HIGH = lax.Precision.HIGHEST


def from_everyone(array, axis):
    copies = jnp.broadcast_to(array, (lax.axis_size(axis), *array.shape))
    return lax.all_to_all(copies, axis, split_axis=0, concat_axis=0, tiled=True)


def taken_together(array, axis):
    return from_everyone(array, axis).sum(axis=0)


def together(arrays, axis):
    line, at, finished = (jnp.concatenate([a.reshape(-1) for a in arrays]), 0, [])
    running = taken_together(line, axis)
    for a in arrays:
        finished.append(running[at : at + a.size].reshape(a.shape))
        at += a.size
    return tuple(finished)


def sent_together(arrays, axis, dim, along):
    ends, at = ([], 0)
    for a in arrays[:-1]:
        at += a.shape[along]
        ends.append(at)
    both = jnp.concatenate(arrays, axis=along)
    return tuple(jnp.split(lax.all_gather(both, axis, axis=dim, tiled=True), ends, axis=along))


def cut_along(array, dim, length):
    before, after = (array.shape[:dim], array.shape[dim + 1 :])
    return jnp.moveaxis(array.reshape(*before, length, -1, *after), dim, 0)


def summed_on_arrival(array, axis, dim):
    length = lax.axis_size(axis)
    tiles = lax.all_to_all(cut_along(array, dim, length), axis, 0, 0, tiled=True)
    return jnp.sum(tiles.astype(jnp.float32), axis=0)


def side_by_side(arrays, axis, dim, along):
    both = jnp.concatenate(arrays, axis=along)
    result, at, finished = (summed_on_arrival(both, axis, dim), 0, [])
    for a in arrays:
        finished.append(lax.slice_in_dim(result, at, at + a.shape[along], axis=along))
        at += a.shape[along]
    return tuple(finished)


def contract_tokens(left_op, right_op):
    return lax.dot_general(
        left_op, right_op, (((0,), (0,)), ((), ())), preferred_element_type=jnp.float32
    )


def form_grads(hidden_in, context_in, query_cotan, output_cotan):

    def query_part(piece, start):
        return contract_tokens(hidden_in, piece)

    def output_part(piece, start):
        return contract_tokens(context_in, piece)

    query_grad = query_part(lax.all_gather(query_cotan, "shard", axis=1, tiled=True), jnp.int32(0))
    output_grad = output_part(
        lax.all_gather(output_cotan, "shard", axis=1, tiled=True), jnp.int32(0)
    )
    return (query_grad, output_grad)


def orthonormal(left, gram):
    chol = jnp.linalg.cholesky(gram)
    return lax.linalg.triangular_solve(chol, left, left_side=False, lower=True, transpose_a=True)


def body(
    hidden_in,
    context_in,
    query_cotan,
    output_cotan,
    query_error,
    output_error,
    query_weight,
    output_weight,
    start_factors,
):
    replicas = lax.axis_size("dp")
    query_start = start_factors[0].astype(jnp.float32)
    output_start = start_factors[1].astype(jnp.float32)
    query_prior = query_error[0].astype(jnp.float32)
    output_prior = output_error[0].astype(jnp.float32)
    query_grad, output_grad = form_grads(hidden_in, context_in, query_cotan, output_cotan)
    query_full = query_grad + query_prior
    output_full = output_grad + output_prior
    query_left = jnp.dot(query_full, query_start, precision=HIGH)
    output_left = jnp.dot(output_full, output_start, precision=HIGH)
    query_left, output_left = together((query_left, output_left), "dp")
    query_left = query_left / jnp.float32(replicas)
    output_left = output_left / jnp.float32(replicas)
    query_whole, output_whole = tuple(
        (
            part.astype(jnp.float32)
            for part in sent_together(
                (query_left.astype(jnp.bfloat16), output_left.astype(jnp.bfloat16)), "shard", 0, 1
            )
        )
    )
    query_gram = jnp.dot(query_whole.T, query_whole, precision=HIGH)
    output_gram = jnp.dot(output_whole.T, output_whole, precision=HIGH)
    query_ortho = orthonormal(query_left, query_gram)
    output_ortho = orthonormal(output_left, output_gram)
    query_term = jnp.dot(query_full.T, query_ortho, precision=HIGH)
    output_term = jnp.dot(output_full.T, output_ortho, precision=HIGH)
    query_part, output_part = side_by_side(
        (query_term.astype(jnp.bfloat16), output_term.astype(jnp.bfloat16)), "shard", 0, 1
    )
    query_part, output_part = together((query_part, output_part), "dp")
    query_right, output_right = sent_together((query_part, output_part), "shard", 0, 1)
    query_right = query_right / jnp.float32(replicas)
    output_right = output_right / jnp.float32(replicas)
    query_approx = jnp.dot(query_ortho, query_right.T, precision=HIGH)
    output_approx = jnp.dot(output_ortho, output_right.T, precision=HIGH)
    query_error_new = (query_full - query_approx).astype(jnp.bfloat16)[None]
    output_error_new = (output_full - output_approx).astype(jnp.bfloat16)[None]
    weight_cols = query_weight.shape[1]
    col_start = lax.axis_index("dp") * weight_cols
    query_cols = lax.dynamic_slice_in_dim(query_approx, col_start, weight_cols, 1)
    output_cols = lax.dynamic_slice_in_dim(output_approx, col_start, weight_cols, 1)
    return (
        query_error_new,
        output_error_new,
        query_weight - query_cols,
        output_weight - output_cols,
    )


def solution(mesh):
    placed = (
        P("dp", "shard"),
        P("dp", "shard"),
        P("dp", "shard"),
        P("dp", "shard"),
        P("dp", "shard", None),
        P("dp", "shard", None),
        P("shard", "dp"),
        P("shard", "dp"),
        P(),
    )
    return jax.shard_map(
        body,
        mesh=mesh,
        in_specs=placed,
        out_specs=(
            P("dp", "shard", None),
            P("dp", "shard", None),
            P("shard", "dp"),
            P("shard", "dp"),
        ),
        check_vma=False,
    )
```

profile of v0, /device:TPU:1, one launch (start us, length us, event | category | flops | bytes accessed | tf_op | source)
XLA Modules:
  0.0 332.1 jit_solution(14758267442661580687)
XLA Ops:
  7.2 0.7 all-gather.7.cloned.1.call-update
  8.0 0.7 all-gather.5.cloned.1.call-update
  8.7 70.7 %all-gather.7.cloned.1.call-done = bf16[1024,2560]{0,1:T(8,128)(2,1)} async-done(((bf16[1024,80]{0,1:T(8,128)(2,1)}), bf16[1024,2560]{0,1:T(8,128)(2,1)}) %all-gather.7.cloned.1.call-update) | async-done | bytes 5242896 | tf_op jit(solution)/shard_map/all_gather | solution.py:72
  79.4 4.6 %convolution_add_fusion = f32[160,2560]{1,0:T(8,128)S(1)} fusion(bf16[1024,160]{0,1:T(8,128)(2,1)S(1)} %copy-done, bf16[1024,2560]{0,1:T(8,128)(2,1)} %all-gather.7.cloned.1.call-done, bf16[1,160,2560]{2,1,0:T(8,128)(2,1)} %param.17), kind=kOutput, calls=%fused_computation | convolution fusion | flops 839680000 | bytes 8028160 | tf_op jit(solution)/shard_map/dot_general | solution.py:57
  84.0 0.9 fusion.8
  85.0 59.4 %all-gather.5.cloned.1.call-done = bf16[1024,2560]{0,1:T(8,128)(2,1)} async-done(((bf16[1024,80]{0,1:T(8,128)(2,1)}), bf16[1024,2560]{0,1:T(8,128)(2,1)}) %all-gather.5.cloned.1.call-update) | async-done | bytes 5242896 | tf_op jit(solution)/shard_map/all_gather | solution.py:70
  144.5 4.4 %convolution_add_fusion.1 = f32[160,2560]{1,0:T(8,128)S(1)} fusion(bf16[1024,160]{0,1:T(8,128)(2,1)S(1)} %copy-done.5, bf16[1024,2560]{0,1:T(8,128)(2,1)} %all-gather.5.cloned.1.call-done, bf16[1,160,2560]{2,1,0:T(8,128)(2,1)S(1)} %copy-done.4), kind=kOutput, calls=%fused_computation.1 | convolution fusion | flops 839680000 | bytes 8028160 | tf_op jit(solution)/shard_map/dot_general | solution.py:57
  148.8 1.2 copy-done.1
  150.0 0.9 fusion.10
  151.0 0.3 broadcast_in_dim.13
  151.3 46.4 %all_to_all.17 = f32[16,1,10240]{2,1,0:T(1,128)S(1)} all-to-all(f32[16,1,10240]{2,1,0:T(1,128)S(1)} %broadcast_in_dim.13), channel_id=1, replica_groups=mesh['dp'=16,'shard'=32] {'dp'}, dimensions={0} | all-to-all | bytes 1310720 | tf_op jit(solution)/shard_map/all_to_all | solution.py:11
  197.7 0.4 reduce_sum.27
  198.3 0.1 maximum_bitcast_fusion
  198.4 0.1 copy.56
  198.5 27.0 %all-gather = bf16[32,160,64]{1,2,0:T(8,128)(2,1)S(1)} all-gather(bf16[1,160,64]{1,2,0:T(8,128)(2,1)S(1)} %copy.56), channel_id=1, replica_groups=mesh['dp'=16,'shard'=32] {'shard'}, dimensions={0}, use_global_device_ids=true | all-gather | bytes 675840 | tf_op jit(solution)/shard_map/all_gather | solution.py:33
  225.4 0.6 copy.57
  226.0 2.5 reshape.102
  228.6 1.3 fusion.6
  229.8 1.3 fusion.4
  231.2 2.9 cholesky.44
  234.2 0.6 compare_reduce_fusion.1
  234.8 0.7 fusion.16
  235.5 2.4 custom-call.6
  237.9 0.3 convolution_bitcast_fusion.1
  238.3 2.9 cholesky.55
  241.3 0.6 compare_reduce_fusion
  241.9 0.7 fusion.17
  242.6 2.4 custom-call.7
  245.0 0.3 convolution_bitcast_fusion
  245.4 1.0 convolution_convert_fusion
  246.4 0.1 copy-done.2
  246.5 1.0 convolution_convert_fusion.1
  247.5 0.6 reshape.92
  248.2 0.2 copy.60
  248.4 15.5 %all_to_all.18 = bf16[32,80,64]{1,2,0:T(8,128)(2,1)S(1)} all-to-all(bf16[32,80,64]{1,2,0:T(8,128)(2,1)S(1)} %copy.60), channel_id=1, replica_groups=mesh['dp'=16,'shard'=32] {'shard'}, dimensions={0} | all-to-all | bytes 655360 | tf_op jit(solution)/shard_map/all_to_all | solution.py:43
  263.9 0.1 convert_reduce_fusion
  264.3 0.9 broadcast_in_dim.14
  265.2 4.2 %all-to-all-start.2 = ((f32[16,1,5120]{2,1,0:T(1,128)}), f32[16,1,5120]{2,1,0:T(1,128)S(1)}, u32[]{:S(2)}, u32[]{:S(2)}) async-start(f32[16,1,5120]{2,1,0:T(1,128)} %broadcast_in_dim.14), calls=%async_computation.2 | async-start | bytes 655360 | tf_op jit(solution)/shard_map/all_to_all | solution.py:11
  269.5 15.4 %all-to-all-done.2 = f32[16,1,5120]{2,1,0:T(1,128)S(1)} async-done(((f32[16,1,5120]{2,1,0:T(1,128)}), f32[16,1,5120]{2,1,0:T(1,128)S(1)}, u32[]{:S(2)}, u32[]{:S(2)}) %all-to-all-start.2) | async-done | bytes 327712 | tf_op jit(solution)/shard_map/all_to_all | solution.py:11
  284.9 0.2 reduce_sum.29
  285.2 0.1 maximum_bitcast_fusion.1
  285.4 30.3 %all-gather.1 = f32[32,80,64]{1,2,0:T(8,128)S(1)} all-gather(f32[1,80,64]{1,2,0:T(8,128)S(1)} %copy.65), channel_id=1, replica_groups=mesh['dp'=16,'shard'=32] {'shard'}, dimensions={0}, use_global_device_ids=true | all-gather | bytes 675840 | tf_op jit(solution)/shard_map/all_gather | solution.py:33
  315.7 0.6 copy.66
  316.3 1.4 reshape.104
  317.8 2.6 fusion.3
  320.3 2.5 fusion.2
  322.8 1.6 fusion
  324.4 0.9 dynamic-slice_subtract_fusion
  (43 shorter events, 1.3 us)
Async XLA Ops:
  7.2 72.3 %copy-start = (bf16[1024,160]{0,1:T(8,128)(2,1)S(1)}, bf16[1024,160]{0,1:T(8,128)(2,1)}, u32[]{:S(2)}) copy-start(bf16[1024,160]{0,1:T(8,128)(2,1)} %param.13) | copy-start | bytes 983044
  7.2 72.2 %all-gather.7.cloned.1.call-start = ((), (), s32[]{:S(2)}) async-start(), calls=%async_computation.4 | async-start | bytes 5406720 | tf_op jit(solution)/shard_map/all_gather | solution.py:72
  7.9 136.5 %all-gather.5.cloned.1.call-start = ((), (), s32[]{:S(2)}) async-start(), calls=%async_computation.3 | async-start | bytes 5406720 | tf_op jit(solution)/shard_map/all_gather | solution.py:70
  8.7 75.3 %copy-start.6 = (bf16[2,2560,32]{1,2,0:T(8,128)(2,1)S(1)}, bf16[2,2560,32]{1,2,0:T(8,128)(2,1)}, u32[]{:S(2)}) copy-start(bf16[2,2560,32]{1,2,0:T(8,128)(2,1)} %param.20) | copy-start | bytes 983044
  84.0 60.4 %copy-start.4 = (bf16[1,160,2560]{2,1,0:T(8,128)(2,1)S(1)}, bf16[1,160,2560]{2,1,0:T(8,128)(2,1)}, u32[]{:S(2)}) copy-start(bf16[1,160,2560]{2,1,0:T(8,128)(2,1)} %param.16) | copy-start | bytes 2457604
  84.0 60.4 %copy-start.5 = (bf16[1024,160]{0,1:T(8,128)(2,1)S(1)}, bf16[1024,160]{0,1:T(8,128)(2,1)}, u32[]{:S(2)}) copy-start(bf16[1024,160]{0,1:T(8,128)(2,1)} %param.12) | copy-start | bytes 983044
  148.8 1.2 copy-start.1
  245.0 1.5 copy-start.2
  265.2 19.6 %all-to-all-start.2 = ((f32[16,1,5120]{2,1,0:T(1,128)}), f32[16,1,5120]{2,1,0:T(1,128)S(1)}, u32[]{:S(2)}, u32[]{:S(2)}) async-start(f32[16,1,5120]{2,1,0:T(1,128)} %broadcast_in_dim.14), calls=%async_computation.2 | async-start | bytes 655360 | tf_op jit(solution)/shard_map/all_to_all | solution.py:11
  317.8 5.0 %copy-start.3 = (f32[160,2560]{1,0:T(8,128)S(1)}, f32[160,2560]{1,0:T(8,128)}, u32[]{:S(2)}) copy-start(f32[160,2560]{1,0:T(8,128)} %copy-done.1) | copy-start | bytes 4915204
  322.8 1.6 copy-start.7
  322.8 1.6 copy-start.8
Sparse Core Ops, SparseCore 0:
  11.1 68.2 all-gather.6
  82.5 61.8 all-gather.4
where the time goes:
time: 333 us; the launch traced here: 332 us
  waiting for transfers between devices  147 us (44%)
  blocking collectives  119 us (36%)
  matrix products  20.9 us (6%)
  other arithmetic  16.8 us (5%)
  between operations  14.4 us (4%)
  local copies, waits for them, and re-layouts  9.68 us (3%)
  starting transfers between devices  4.29 us (1%)
    all_gather x1, waiting for transfers between devices, form_grads(): lax.all_gather(output_cotan, 'shard', axis=1, tiled=True)  70.7 us
    all_gather x1, waiting for transfers between devices, form_grads(): lax.all_gather(query_cotan, 'shard', axis=1, tiled=True)  59.4 us
    all_gather x2, blocking collectives, sent_together(): lax.all_gather(both, axis, axis=dim, tiled=True)  57.3 us
    all_to_all x1, blocking collectives, from_everyone(): return lax.all_to_all(copies, axis, split_axis=0, concat_axis=0, tiled=True)  46.4 us
    all_to_all x1, blocking collectives, summed_on_arrival(): lax.all_to_all(cut_along(array, dim, length), axis, 0, 0, tiled=True)  15.5 us
    all_to_all x1, waiting for transfers between devices, from_everyone(): return lax.all_to_all(copies, axis, split_axis=0, concat_axis=0, tiled=True)  15.4 us
    dot_general x2, matrix products, contract_tokens(): lax.dot_general(left_op, right_op, (((0,), (0,)), ((), ())), preferred_el...  8.94 us
    another operation x6, other arithmetic, orthonormal(): chol = jnp.linalg.cholesky(gram)  7.2 us
  transfers between devices with their start and end apart: 3, of which 3 were waited for; matrix products, arithmetic and copies ran while one was open for 2% of the time, Pallas kernels for 0%

commit v1 on v0

v1 whole, which is shorter than its diff:
```python
import jax
import jax.numpy as jnp
from jax import lax
from jax.sharding import PartitionSpec as P

HIGH = lax.Precision.HIGHEST
F32 = jnp.float32
BF16 = jnp.bfloat16


def copies(array, count):
    return jnp.broadcast_to(array, (count, *array.shape))


def exchange(array, axis, groups=None):
    return lax.all_to_all(array, axis, 0, 0, tiled=True, axis_index_groups=groups)


def from_everyone(array, axis):
    return exchange(copies(array, lax.axis_size(axis)), axis)


def split_high_low(array):
    high = array.astype(BF16)
    return high, (array - high.astype(F32)).astype(BF16)


def side_by_side(query, output):
    half = query.shape[-2] // 2
    return jnp.concatenate(
        [query[..., :half, :], output[..., :half, :], query[..., half:, :], output[..., half:, :]],
        axis=-1,
    )


def apart(both):
    rank = both.shape[-1] // 4
    parts = [both[..., i * rank : (i + 1) * rank] for i in range(4)]
    return (
        jnp.concatenate([parts[0], parts[2]], axis=-2),
        jnp.concatenate([parts[1], parts[3]], axis=-2),
    )


def all_columns(cotan):
    shards = lax.axis_size("shard")
    chips = shards // 2
    same_core = [[2 * chip + core for chip in range(chips)] for core in range(2)]
    swap = [(i, i ^ 1) for i in range(shards)]
    mine = exchange(copies(cotan.T, chips), "shard", same_core)
    theirs = lax.ppermute(mine, "shard", swap)
    first = lax.axis_index("shard") % 2 == 0
    both = jnp.stack(
        [jnp.where(first, mine, theirs), jnp.where(first, theirs, mine)], axis=1
    )
    return both.reshape(-1, cotan.shape[0])


def contract(a, b, dims):
    return lax.dot_general(a, b, ((dims[:1], dims[1:]), ((), ())), preferred_element_type=F32)


def full_gradient(inputs, columns, error):
    return contract(inputs.T, columns, (1, 1)) + error[0].astype(F32)


def inverse_factor(gram):
    chol = jnp.linalg.cholesky(gram)
    eye = jnp.eye(gram.shape[0], dtype=F32)
    return lax.linalg.triangular_solve(chol, eye, left_side=True, lower=True)


def body(
    hidden_in,
    context_in,
    query_cotan,
    output_cotan,
    query_error,
    output_error,
    query_weight,
    output_weight,
    start_factors,
):
    replicas = lax.axis_size("dp")
    shards = lax.axis_size("shard")
    start = start_factors.astype(F32)

    query_full = full_gradient(hidden_in, all_columns(query_cotan), query_error)
    output_full = full_gradient(context_in, all_columns(output_cotan), output_error)
    query_left = jnp.dot(query_full, start[0], precision=HIGH)
    output_left = jnp.dot(output_full, start[1], precision=HIGH)

    lefts = from_everyone(side_by_side(query_left, output_left).astype(BF16), "dp")
    query_left, output_left = apart(lefts.astype(F32).sum(axis=0) / F32(replicas))

    def term(full, left):
        product = lax.dot_general(full, left, (((0,), (0,)), ((), ())), precision=HIGH)
        return product.reshape(shards, -1, product.shape[-1])

    def gram_of(left):
        return lax.dot_general(left, left, (((0,), (0,)), ((), ())), precision=HIGH)

    terms = side_by_side(term(query_full, query_left), term(output_full, output_left))
    rows = terms.shape[1]
    grams = jnp.concatenate(
        [*split_high_low(gram_of(query_left)), *split_high_low(gram_of(output_left))], axis=1
    )
    rank = grams.shape[0]
    sent = jnp.concatenate([terms.astype(BF16), copies(grams, shards)], axis=1)
    arrived = exchange(sent, "shard").astype(F32).sum(axis=0)
    share = arrived[:rows]
    gram_parts = arrived[rows:]

    shares = from_everyone(share.astype(BF16), "dp")
    share = shares.astype(F32).sum(axis=0) / F32(replicas)

    query_inverse = inverse_factor(gram_parts[:, :rank] + gram_parts[:, rank : 2 * rank])
    output_inverse = inverse_factor(gram_parts[:, 2 * rank : 3 * rank] + gram_parts[:, 3 * rank :])

    def weighted(left, inverse):
        ortho = lax.dot_general(left, inverse, (((1,), (1,)), ((), ())), precision=HIGH)
        high, low = split_high_low(jnp.dot(ortho, inverse, precision=HIGH))
        return jnp.concatenate([high, low], axis=1)

    query_rows = weighted(query_left, query_inverse)
    output_rows = weighted(output_left, output_inverse)

    query_cols, output_cols = apart(from_everyone(share.astype(BF16), "shard"))

    def finish(rows, cols, full, weight):
        cols = cols.reshape(-1, cols.shape[-1])
        cols = jnp.concatenate([cols, cols], axis=1)
        width = weight.shape[1]
        own = lax.dynamic_slice_in_dim(cols, lax.axis_index("dp") * width, width, 0)
        error_new = (full - contract(rows, cols, (1, 1))).astype(BF16)[None]
        return error_new, weight - contract(rows, own, (1, 1))

    query_error_new, query_weight_new = finish(query_rows, query_cols, query_full, query_weight)
    output_error_new, output_weight_new = finish(
        output_rows, output_cols, output_full, output_weight
    )
    return query_error_new, output_error_new, query_weight_new, output_weight_new


def solution(mesh):
    placed = (
        P("dp", "shard"),
        P("dp", "shard"),
        P("dp", "shard"),
        P("dp", "shard"),
        P("dp", "shard", None),
        P("dp", "shard", None),
        P("shard", "dp"),
        P("shard", "dp"),
        P(),
    )
    return jax.shard_map(
        body,
        mesh=mesh,
        in_specs=placed,
        out_specs=(
            P("dp", "shard", None),
            P("dp", "shard", None),
            P("shard", "dp"),
            P("shard", "dp"),
        ),
        check_vma=False,
    )
```

time: 333 us -> 213 us (0.64)
  waiting for transfers between devices: 147 us -> 54.4 us
  blocking collectives: 119 us -> 71.5 us
  starting transfers between devices: 4.29 us -> 38.7 us
  between operations: 14.4 us -> 1.07 us
  matrix products: 20.9 us -> 15.5 us
  other arithmetic: 16.8 us -> 21.1 us
    all_gather x2 -> x0, waiting for transfers between devices: 130 us -> none  [the longest x1 70.7 us: form_grads(): lax.all_gather(output_cotan, 'shard', axis=1, tiled=True)]
    all_gather x2 -> x0, blocking collectives: 57.3 us -> none  [sent_together(): lax.all_gather(both, axis, axis=dim, tiled=True)]
    all_to_all x1 -> x4, waiting for transfers between devices: 15.4 us -> 54.4 us  [exchange(): lax.all_to_all(array, axis, 0, 0, tiled=True, axis_index_groups=groups)]
    all_to_all x1 -> x4, starting transfers between devices: 4.22 us -> 27.2 us  [exchange(): lax.all_to_all(array, axis, 0, 0, tiled=True, axis_index_groups=groups)]
    ppermute x0 -> x2, starting transfers between devices: none -> 11.4 us  [all_columns(): theirs = lax.ppermute(mine, 'shard', swap)]
    all_to_all x2, blocking collectives: 61.8 us -> 71.5 us  [exchange(): lax.all_to_all(array, axis, 0, 0, tiled=True, axis_index_groups=groups)]
    another operation x10 -> x14, other arithmetic: 13.4 us -> 19.3 us  [the longest x6 7.2 us: inverse_factor(): chol = jnp.linalg.cholesky(gram)]
    dot_general x10 -> x16, matrix products: 20.3 us -> 15 us  [the longest x6 8.16 us: contract(): lax.dot_general(a, b, ((dims[:1], dims[1:]), ((), ())), preferred_element...]
  transfers between devices with their start and end apart: 3 -> 6, of which waited for: 3 -> 4; matrix products, arithmetic and copies ran while one was open for 2% -> 7% of each run, Pallas kernels for 0% -> 0%
where the time goes in v1:
time: 213 us
  blocking collectives  71.5 us (34%)
  waiting for transfers between devices  54.4 us (26%)
  starting transfers between devices  38.7 us (18%)
  other arithmetic  21.1 us (10%)
  matrix products  15.5 us (7%)
  local copies, waits for them, and re-layouts  10.3 us (5%)
    all_to_all x2, blocking collectives, exchange(): lax.all_to_all(array, axis, 0, 0, tiled=True, axis_index_groups=groups)  71.5 us
    all_to_all x4, waiting for transfers between devices, exchange(): lax.all_to_all(array, axis, 0, 0, tiled=True, axis_index_groups=groups)  54.4 us
    all_to_all x4, starting transfers between devices, exchange(): lax.all_to_all(array, axis, 0, 0, tiled=True, axis_index_groups=groups)  27.2 us
    ppermute x2, starting transfers between devices, all_columns(): theirs = lax.ppermute(mine, 'shard', swap)  11.4 us
    dot_general x6, matrix products, contract(): lax.dot_general(a, b, ((dims[:1], dims[1:]), ((), ())), preferred_element...  8.16 us
    another operation x6, other arithmetic, inverse_factor(): chol = jnp.linalg.cholesky(gram)  7.2 us
    another operation x4, other arithmetic, inverse_factor(): return lax.linalg.triangular_solve(chol, eye, left_side=True, lower=True)  6.17 us
    another operation x4, other arithmetic, all_columns(): jnp.stack([jnp.where(first, mine, theirs), jnp.where(first, theirs, mine)...  5.92 us
  transfers between devices with their start and end apart: 6, of which 4 were waited for; matrix products, arithmetic and copies ran while one was open for 7% of the time, Pallas kernels for 0%

profile of v1, /device:TPU:1, one launch (start us, length us, event | category | flops | bytes accessed | tf_op | source)
XLA Modules:
  0.0 212.5 jit_solution(17913795610806751824)
XLA Ops:
  0.6 1.3 broadcast_in_dim.26
  1.9 40.4 %all_to_all.30 = bf16[16,80,1024]{2,1,0:T(8,128)(2,1)S(1)} all-to-all(bf16[16,80,1024]{2,1,0:T(8,128)(2,1)S(1)} %broadcast_in_dim.26), channel_id=1, replica_groups={{0,2,4,6,8,10,12,14,16,18,20,22,24,26,28,30},{1,3,5,7,9,11,13,15,17,19,..., dimensions={0} | all-to-all | bytes 5242880 | tf_op jit(solution)/shard_map/all_to_all | solution.py:16
  42.4 1.8 broadcast_in_dim.25
  44.2 4.5 %all-to-all-start = ((bf16[16,80,1024]{2,1,0:T(8,128)(2,1)}), bf16[16,80,1024]{2,1,0:T(8,128)(2,1)}, u32[]{:S(2)}, u32[]{:S(2)}) async-start(bf16[16,80,1024]{2,1,0:T(8,128)(2,1)} %broadcast_in_dim.25), calls=%async_computation | async-start | bytes 5242880 | tf_op jit(solution)/shard_map/all_to_all | solution.py:16
  48.7 4.6 %collective-permute-start.1 = (bf16[16,80,1024]{2,1,0:T(8,128)(2,1)S(1)}, bf16[16,80,1024]{2,1,0:T(8,128)(2,1)}, u32[]{:S(2)}, u32[]{:S(2)}) collective-permute-start(bf16[16,80,1024]{2,1,0:T(8,128)(2,1)S(1)} %all_to_all.30), channel_id=1, source_target_pairs={{0,1},{1,0},{2,3},{3,2},{4,5},{5,4},{6,7},{7,6},{8,9},{9,8},{10,11... | collective-permute-start | bytes 7864328 | tf_op jit(solution)/shard_map/ppermute | solution.py:51
  53.3 28.4 %all-to-all-done = bf16[16,80,1024]{2,1,0:T(8,128)(2,1)} async-done(((bf16[16,80,1024]{2,1,0:T(8,128)(2,1)}), bf16[16,80,1024]{2,1,0:T(8,128)(2,1)}, u32[]{:S(2)}, u32[]{:S(2)}) %all-to-all-start) | async-done | bytes 2621472 | tf_op jit(solution)/shard_map/all_to_all | solution.py:16
  81.7 6.8 %collective-permute-start = (bf16[16,80,1024]{2,1,0:T(8,128)(2,1)}, bf16[16,80,1024]{2,1,0:T(8,128)(2,1)}, u32[]{:S(2)}, u32[]{:S(2)}) collective-permute-start(bf16[16,80,1024]{2,1,0:T(8,128)(2,1)} %all-to-all-done), channel_id=1, source_target_pairs={{0,1},{1,0},{2,3},{3,2},{4,5},{5,4},{6,7},{7,6},{8,9},{9,8},{10,11... | collective-permute-start | bytes 7864328 | tf_op jit(solution)/shard_map/ppermute | solution.py:51
  88.6 2.1 select_bitcast_fusion.1
  90.7 0.5 pad_maximum_fusion.1
  91.2 0.9 copy.67
  92.3 1.9 fusion
  94.2 1.0 convolution_convert_fusion.2
  95.2 2.9 %select_bitcast_fusion.3 = (bf16[16,1,80,1024]{3,2,1,0:T(8,128)(2,1)S(1)}, bf16[16,1,80,1024]{3,2,1,0:T(8,128)(2,1)S(1)}) fusion(bf16[16,80,1024]{2,1,0:T(8,128)(2,1)} %all-to-all-done, bf16[16,80,1024]{2,1,0:T(8,128)(2,1)} %collective-permute-done, pred[]{:T(512)S(6)} %eq.13), kind=kLoop, calls=%fused_computation.17 | loop fusion | flops 2621440 | bytes 10485761 | tf_op jit(solution)/shard_map/stack | solution.py:53
  98.1 0.5 pad_maximum_fusion
  98.6 0.6 copy-done.4
  99.3 1.9 fusion.1
  101.2 1.2 copy-done.1
  102.4 1.0 convolution_convert_fusion.3
  103.6 31.0 %all_to_all.31 = bf16[16,80,128]{2,1,0:T(8,128)(2,1)S(1)} all-to-all(bf16[16,80,128]{2,1,0:T(8,128)(2,1)S(1)} %broadcast_in_dim.27), channel_id=1, replica_groups=mesh['dp'=16,'shard'=32] {'dp'}, dimensions={0} | all-to-all | bytes 655360 | tf_op jit(solution)/shard_map/all_to_all | solution.py:16
  134.9 2.5 %convolution_convert_fusion.1 = bf16[2560,32]{0,1:T(8,128)(2,1)S(1)} fusion(f32[160,2560]{1,0:T(8,128)} %copy-done.1, f32[80,32]{0,1:T(8,128)S(1)} %copy.70, f32[80,32]{0,1:T(8,128)S(1)} %copy.69), kind=kOutput, calls=%fused_computation.13 | convolution fusion | flops 157373440 | bytes 1822720 | tf_op jit(solution)/shard_map/dot_general | solution.py:97
  137.8 1.0 convolution_convert_fusion
  139.1 0.3 copy.87
  139.5 0.3 copy.88
  140.0 1.3 pad_maximum_fusion.4
  141.3 9.7 %all-to-all-start.3 = ((bf16[32,72,128]{2,1,0:T(8,128)(2,1)}), bf16[32,72,128]{2,1,0:T(8,128)(2,1)S(1)}, u32[]{:S(2)}, u32[]{:S(2)}) async-start(bf16[32,72,128]{2,1,0:T(8,128)(2,1)} %pad_maximum_fusion.4), calls=%async_computation.3 | async-start | bytes 1179648 | tf_op jit(solution)/shard_map/all_to_all | solution.py:16
  151.0 12.2 %all-to-all-done.3 = bf16[32,72,128]{2,1,0:T(8,128)(2,1)S(1)} async-done(((bf16[32,72,128]{2,1,0:T(8,128)(2,1)}), bf16[32,72,128]{2,1,0:T(8,128)(2,1)S(1)}, u32[]{:S(2)}, u32[]{:S(2)}) %all-to-all-start.3) | async-done | bytes 589856 | tf_op jit(solution)/shard_map/all_to_all | solution.py:16
  163.6 2.9 %cholesky.55 = f32[32,32]{1,0:T(8,128)S(1)} custom-call(f32[32,32]{1,0:T(8,128)S(1)} %fusion.25), custom_call_target="Cholesky" | custom-call | tf_op jit(solution)/shard_map/jit(cholesky)/cholesky | solution.py:68
  166.6 0.6 compare_reduce_fusion
  167.2 0.7 fusion.23
  167.9 2.4 %custom-call.7 = f32[1,32,32]{1,2,0:T(8,128)S(1)} custom-call(f32[1,32,32]{2,1,0:T(8,128)S(1)} %fusion.23), custom_call_target="InvertDiagBlocksLowerTriangular" | custom-call | tf_op jit(solution)/shard_map/triangular_solve/custom-call.0 | solution.py:70
  170.3 0.2 fusion.14
  170.5 0.7 broadcast_in_dim.29
  171.2 5.7 %all-to-all-start.4 = ((bf16[16,40,128]{2,1,0:T(8,128)(2,1)}), bf16[16,40,128]{2,1,0:T(8,128)(2,1)S(1)}, u32[]{:S(2)}, u32[]{:S(2)}) async-start(bf16[16,40,128]{2,1,0:T(8,128)(2,1)} %broadcast_in_dim.29), calls=%async_computation.4 | async-start | bytes 327680 | tf_op jit(solution)/shard_map/all_to_all | solution.py:16
  177.2 2.9 %cholesky.44 = f32[32,32]{1,0:T(8,128)S(1)} custom-call(f32[32,32]{1,0:T(8,128)S(1)} %fusion.27), custom_call_target="Cholesky" | custom-call | tf_op jit(solution)/shard_map/jit(cholesky)/cholesky | solution.py:68
  180.2 0.6 compare_reduce_fusion.1
  180.8 0.7 fusion.22
  181.5 2.4 %custom-call.6 = f32[1,32,32]{1,2,0:T(8,128)S(1)} custom-call(f32[1,32,32]{2,1,0:T(8,128)S(1)} %fusion.22), custom_call_target="InvertDiagBlocksLowerTriangular" | custom-call | tf_op jit(solution)/shard_map/triangular_solve/custom-call.0 | solution.py:70
  183.9 0.2 fusion.16
  184.1 0.2 fusion.18
  184.6 4.7 %all-to-all-done.4 = bf16[16,40,128]{2,1,0:T(8,128)(2,1)S(1)} async-done(((bf16[16,40,128]{2,1,0:T(8,128)(2,1)}), bf16[16,40,128]{2,1,0:T(8,128)(2,1)S(1)}, u32[]{:S(2)}, u32[]{:S(2)}) %all-to-all-start.4) | async-done | bytes 163872 | tf_op jit(solution)/shard_map/all_to_all | solution.py:16
  189.3 0.8 broadcast_in_dim.30
  190.1 7.4 %all-to-all-start.5 = ((bf16[32,40,128]{2,1,0:T(8,128)(2,1)}), bf16[32,40,128]{2,1,0:T(8,128)(2,1)S(1)}, u32[]{:S(2)}, u32[]{:S(2)}) async-start(bf16[32,40,128]{2,1,0:T(8,128)(2,1)} %broadcast_in_dim.30), calls=%async_computation.5 | async-start | bytes 655360 | tf_op jit(solution)/shard_map/all_to_all | solution.py:16
  198.0 9.0 %all-to-all-done.5 = bf16[32,40,128]{2,1,0:T(8,128)(2,1)S(1)} async-done(((bf16[32,40,128]{2,1,0:T(8,128)(2,1)}), bf16[32,40,128]{2,1,0:T(8,128)(2,1)S(1)}, u32[]{:S(2)}, u32[]{:S(2)}) %all-to-all-start.5) | async-done | bytes 327712 | tf_op jit(solution)/shard_map/all_to_all | solution.py:16
  207.0 0.3 fusion.42
  208.1 1.3 fusion.4
  209.4 0.9 convolution_subtract_fusion.2
  210.3 1.3 fusion.5
  211.6 0.9 convolution_subtract_fusion.3
  (61 shorter events, 3.8 us)
Async XLA Ops:
  0.6 91.5 %copy-start = (bf16[1024,160]{0,1:T(8,128)(2,1)S(1)}, bf16[1024,160]{0,1:T(8,128)(2,1)}, u32[]{:S(2)}) copy-start(bf16[1024,160]{0,1:T(8,128)(2,1)} %param.13) | copy-start | bytes 983044
  1.9 40.5 %copy-start.9 = (bf16[1024,80]{0,1:T(8,128)(2,1)S(1)}, bf16[1024,80]{0,1:T(8,128)(2,1)}, u32[]{:S(2)}) copy-start(bf16[1024,80]{0,1:T(8,128)(2,1)} %param.14) | copy-start | bytes 491524
  44.2 37.5 %all-to-all-start = ((bf16[16,80,1024]{2,1,0:T(8,128)(2,1)}), bf16[16,80,1024]{2,1,0:T(8,128)(2,1)}, u32[]{:S(2)}, u32[]{:S(2)}) async-start(bf16[16,80,1024]{2,1,0:T(8,128)(2,1)} %broadcast_in_dim.25), calls=%async_computation | async-start | bytes 5242880 | tf_op jit(solution)/shard_map/all_to_all | solution.py:16
  48.7 39.9 %collective-permute-start.1 = (bf16[16,80,1024]{2,1,0:T(8,128)(2,1)S(1)}, bf16[16,80,1024]{2,1,0:T(8,128)(2,1)}, u32[]{:S(2)}, u32[]{:S(2)}) collective-permute-start(bf16[16,80,1024]{2,1,0:T(8,128)(2,1)S(1)} %all_to_all.30), channel_id=1, source_target_pairs={{0,1},{1,0},{2,3},{3,2},{4,5},{5,4},{6,7},{7,6},{8,9},{9,8},{10,11... | collective-permute-start | bytes 7864328 | tf_op jit(solution)/shard_map/ppermute | solution.py:51
  81.7 13.4 %collective-permute-start = (bf16[16,80,1024]{2,1,0:T(8,128)(2,1)}, bf16[16,80,1024]{2,1,0:T(8,128)(2,1)}, u32[]{:S(2)}, u32[]{:S(2)}) collective-permute-start(bf16[16,80,1024]{2,1,0:T(8,128)(2,1)} %all-to-all-done), channel_id=1, source_target_pairs={{0,1},{1,0},{2,3},{3,2},{4,5},{5,4},{6,7},{7,6},{8,9},{9,8},{10,11... | collective-permute-start | bytes 7864328 | tf_op jit(solution)/shard_map/ppermute | solution.py:51
  91.1 1.1 copy-start.3
  92.3 1.9 copy-start.6
  98.1 1.1 copy-start.4
  98.1 1.2 copy-start.5
  101.2 1.2 copy-start.1
  141.3 21.9 %all-to-all-start.3 = ((bf16[32,72,128]{2,1,0:T(8,128)(2,1)}), bf16[32,72,128]{2,1,0:T(8,128)(2,1)S(1)}, u32[]{:S(2)}, u32[]{:S(2)}) async-start(bf16[32,72,128]{2,1,0:T(8,128)(2,1)} %pad_maximum_fusion.4), calls=%async_computation.3 | async-start | bytes 1179648 | tf_op jit(solution)/shard_map/all_to_all | solution.py:16
  171.2 18.1 %all-to-all-start.4 = ((bf16[16,40,128]{2,1,0:T(8,128)(2,1)}), bf16[16,40,128]{2,1,0:T(8,128)(2,1)S(1)}, u32[]{:S(2)}, u32[]{:S(2)}) async-start(bf16[16,40,128]{2,1,0:T(8,128)(2,1)} %broadcast_in_dim.29), calls=%async_computation.4 | async-start | bytes 327680 | tf_op jit(solution)/shard_map/all_to_all | solution.py:16
  190.1 16.9 %all-to-all-start.5 = ((bf16[32,40,128]{2,1,0:T(8,128)(2,1)}), bf16[32,40,128]{2,1,0:T(8,128)(2,1)S(1)}, u32[]{:S(2)}, u32[]{:S(2)}) async-start(bf16[32,40,128]{2,1,0:T(8,128)(2,1)} %broadcast_in_dim.30), calls=%async_computation.5 | async-start | bytes 655360 | tf_op jit(solution)/shard_map/all_to_all | solution.py:16
  207.8 1.5 copy-start.7
  208.1 2.2 %copy-start.2 = (f32[160,2560]{1,0:T(8,128)S(1)}, f32[160,2560]{1,0:T(8,128)}, u32[]{:S(2)}) copy-start(f32[160,2560]{1,0:T(8,128)} %copy-done.1) | copy-start | bytes 4915204
  209.4 2.2 %copy-start.8 = (f32[160,160]{1,0:T(8,128)S(1)}, f32[160,160]{1,0:T(8,128)}, u32[]{:S(2)}) copy-start(f32[160,160]{1,0:T(8,128)} %param.18) | copy-start | bytes 307204

commit v2 on v1

--- a/solution.py
+++ b/solution.py
@@ -2,6 +2,7 @@
 import jax.numpy as jnp
 from jax import lax
 from jax.sharding import PartitionSpec as P
+
 
 HIGH = lax.Precision.HIGHEST
 F32 = jnp.float32
@@ -42,18 +43,57 @@
     )
 
 
-def all_columns(cotan):
-    shards = lax.axis_size("shard")
-    chips = shards // 2
+def in_plane(rows, cols, core):
+    side = 4
+    pairs = []
+    for y in range(side):
+        for x in range(side):
+            for c in range(2):
+                to = ((y + rows) % side * side + (x + cols) % side) * 2 + (c + core) % 2
+                pairs.append(((y * side + x) * 2 + c, to))
+    return pairs
+
+
+def send(array, rows, cols, core=0):
+    return lax.ppermute(array, "shard", in_plane(rows, cols, core))
+
+
+def in_order(pieces, position):
+    count = len(pieces)
+    result = jnp.zeros((count, *pieces[0].shape), pieces[0].dtype)
+    for k, piece in enumerate(pieces):
+        at = (position + k) % count
+        result = lax.dynamic_update_slice_in_dim(result, piece[None], at, 0)
+    return result
+
+
+def by_exchange(cotan):
+    chips = lax.axis_size("shard") // 2
     same_core = [[2 * chip + core for chip in range(chips)] for core in range(2)]
-    swap = [(i, i ^ 1) for i in range(shards)]
-    mine = exchange(copies(cotan.T, chips), "shard", same_core)
-    theirs = lax.ppermute(mine, "shard", swap)
-    first = lax.axis_index("shard") % 2 == 0
-    both = jnp.stack(
-        [jnp.where(first, mine, theirs), jnp.where(first, theirs, mine)], axis=1
-    )
-    return both.reshape(-1, cotan.shape[0])
+    return exchange(copies(cotan.T, chips), "shard", same_core)
+
+
+def by_rings(cotan):
+    shard = lax.axis_index("shard")
+    y, x = shard // 8, shard // 2 % 4
+    block = cotan.T
+    below, above, across = send(block, 1, 0), send(block, 3, 0), send(block, 2, 0)
+    column = in_order([block, above, across, below], y)
+    left, right = send(column, 0, 1), send(column, 0, 3)
+    half = column.shape[0] // 2
+    far = jnp.concatenate([send(left[:half], 0, 1), send(right[half:], 0, 3)])
+    return jnp.swapaxes(in_order([column, right, far, left], x), 0, 1)
+
+
+def all_columns(mine):
+    theirs = send(mine, 0, 0, 1)
+    tokens = mine.shape[-1]
+    core = lax.axis_index("shard") % 2
+    both = jnp.zeros((mine.size // mine.shape[-2] // tokens, 2, *mine.shape[-2:]), mine.dtype)
+    for array, at in ((mine, core), (theirs, 1 - core)):
+        array = array.reshape(-1, 1, *mine.shape[-2:])
+        both = lax.dynamic_update_slice_in_dim(both, array, at, 1)
+    return both.reshape(-1, tokens)
 
 
 def contract(a, b, dims):
@@ -70,7 +110,7 @@
     return lax.linalg.triangular_solve(chol, eye, left_side=True, lower=True)
 
 
-def body(
+def step(
     hidden_in,
     context_in,
     query_cotan,
@@ -85,8 +125,11 @@
     shards = lax.axis_size("shard")
     start = start_factors.astype(F32)
 
-    query_full = full_gradient(hidden_in, all_columns(query_cotan), query_error)
-    output_full = full_gradient(context_in, all_columns(output_cotan), output_error)
+    query_blocks = by_exchange(query_cotan)
+    query_columns = all_columns(query_blocks)
+    output_columns = all_columns(by_rings(output_cotan))
+    query_full = full_gradient(hidden_in, query_columns, query_error)
+    output_full = full_gradient(context_in, output_columns, output_error)
     query_left = jnp.dot(query_full, start[0], precision=HIGH)
     output_left = jnp.dot(output_full, start[1], precision=HIGH)
 
@@ -155,7 +198,7 @@
         P(),
     )
     return jax.shard_map(
-        body,
+        step,
         mesh=mesh,
         in_specs=placed,
         out_specs=(

time: 213 us -> 232 us (1.089)
  blocking collectives: 71.5 us -> 31.4 us
  starting transfers between devices: 38.7 us -> 62.1 us
  local copies, waits for them, and re-layouts: 10.3 us -> 30.4 us
  waiting for transfers between devices: 54.4 us -> 73.6 us
  other arithmetic: 21.1 us -> 17.1 us
    ppermute x2 -> x9, waiting for transfers between devices: 0.01 us -> 40.8 us  [send(): return lax.ppermute(array, 'shard', in_plane(rows, cols, core))]
    all_to_all x2 -> x1, blocking collectives: 71.5 us -> 31.4 us  [exchange(): lax.all_to_all(array, axis, 0, 0, tiled=True, axis_index_groups=groups)]
    all_to_all x4, waiting for transfers between devices: 54.4 us -> 32.8 us  [exchange(): lax.all_to_all(array, axis, 0, 0, tiled=True, axis_index_groups=groups)]
    ppermute x2 -> x9, starting transfers between devices: 11.4 us -> 29.2 us  [send(): return lax.ppermute(array, 'shard', in_plane(rows, cols, core))]
    dynamic_update_slice x0 -> x10, local copies, waits for them, and re-layouts: none -> 15.3 us  [the longest x7 9.56 us: in_order(): result = lax.dynamic_update_slice_in_dim(result, piece[None], at, 0)]
    another operation x4 -> x0, other arithmetic: 5.92 us -> none  [all_columns(): jnp.stack([jnp.where(first, mine, theirs), jnp.where(first, theirs, mine)...]
    all_to_all x4, starting transfers between devices: 27.2 us -> 32.9 us  [exchange(): lax.all_to_all(array, axis, 0, 0, tiled=True, axis_index_groups=groups)]
    broadcast_in_dim x0 -> x2, local copies, waits for them, and re-layouts: none -> 2.72 us  [in_order(): result = jnp.zeros((count, *pieces[0].shape), pieces[0].dtype)]
  transfers between devices with their start and end apart: 6 -> 13, of which waited for: 4 -> 6; matrix products, arithmetic and copies ran while one was open for 7% -> 10% of each run, Pallas kernels for 0% -> 0%
where the time goes in v2:
time: 232 us; the launch traced here: 231 us
  waiting for transfers between devices  73.6 us (32%)
  starting transfers between devices  62.1 us (27%)
  blocking collectives  31.4 us (14%)
  local copies, waits for them, and re-layouts  30.4 us (13%)
  other arithmetic  17.1 us (7%)
  matrix products  15.5 us (7%)
    ppermute x9, waiting for transfers between devices, send(): return lax.ppermute(array, 'shard', in_plane(rows, cols, core))  40.8 us
    all_to_all x4, starting transfers between devices, exchange(): lax.all_to_all(array, axis, 0, 0, tiled=True, axis_index_groups=groups)  32.9 us
    all_to_all x4, waiting for transfers between devices, exchange(): lax.all_to_all(array, axis, 0, 0, tiled=True, axis_index_groups=groups)  32.8 us
    all_to_all x1, blocking collectives, exchange(): lax.all_to_all(array, axis, 0, 0, tiled=True, axis_index_groups=groups)  31.4 us
    ppermute x9, starting transfers between devices, send(): return lax.ppermute(array, 'shard', in_plane(rows, cols, core))  29.2 us
    dynamic_update_slice x7, local copies, waits for them, and re-layouts, in_order(): result = lax.dynamic_update_slice_in_dim(result, piece[None], at, 0)  9.56 us
    dot_general x6, matrix products, contract(): lax.dot_general(a, b, ((dims[:1], dims[1:]), ((), ())), preferred_element...  8.22 us
    another operation x6, other arithmetic, inverse_factor(): chol = jnp.linalg.cholesky(gram)  7.2 us
  transfers between devices with their start and end apart: 13, of which 6 were waited for; matrix products, arithmetic and copies ran while one was open for 10% of the time, Pallas kernels for 0%

profile of v2, /device:TPU:1, one launch (start us, length us, event | category | flops | bytes accessed | tf_op | source)
XLA Modules:
  0.0 231.4 jit_solution(10960598844590045365)
XLA Ops:
  0.6 5.8 %collective-permute-start.2 = (bf16[80,1024]{1,0:T(8,128)(2,1)}, bf16[80,1024]{1,0:T(8,128)(2,1)S(1)}, u32[]{:S(2)}, u32[]{:S(2)}) collective-permute-start(bf16[80,1024]{1,0:T(8,128)(2,1)} %bitcast.109), channel_id=1, source_target_pairs={{0,16},{1,17},{2,18},{3,19},{4,20},{5,21},{6,22},{7,23},{8,24},{9,... | collective-permute-start | bytes 491528 | tf_op jit(solution)/shard_map/ppermute | solution.py:58
  6.4 2.7 %collective-permute-start.1 = (bf16[80,1024]{1,0:T(8,128)(2,1)}, bf16[80,1024]{1,0:T(8,128)(2,1)}, u32[]{:S(2)}, u32[]{:S(2)}) collective-permute-start(bf16[80,1024]{1,0:T(8,128)(2,1)} %bitcast.110), channel_id=1, source_target_pairs={{0,24},{1,25},{2,26},{3,27},{4,28},{5,29},{6,30},{7,31},{8,0},{9,1... | collective-permute-start | bytes 491528 | tf_op jit(solution)/shard_map/ppermute | solution.py:58
  9.1 2.6 %collective-permute-start.3 = (bf16[80,1024]{1,0:T(8,128)(2,1)}, bf16[80,1024]{1,0:T(8,128)(2,1)S(1)}, u32[]{:S(2)}, u32[]{:S(2)}) collective-permute-start(bf16[80,1024]{1,0:T(8,128)(2,1)} %bitcast.111), channel_id=1, source_target_pairs={{0,8},{1,9},{2,10},{3,11},{4,12},{5,13},{6,14},{7,15},{8,16},{9,17... | collective-permute-start | bytes 491528 | tf_op jit(solution)/shard_map/ppermute | solution.py:58
  11.7 2.7 %broadcast_in_dim.52 = bf16[16,80,1024]{2,1,0:T(8,128)(2,1)} broadcast(bf16[80,1024]{1,0:T(8,128)(2,1)} %bitcast.112), dimensions={1,2} | broadcast | bytes 2785280 | tf_op jit(solution)/shard_map/broadcast_in_dim | solution.py:13
  14.5 6.0 %all-to-all-start = ((bf16[16,80,1024]{2,1,0:T(8,128)(2,1)}), bf16[16,80,1024]{2,1,0:T(8,128)(2,1)S(1)}, u32[]{:S(2)}, u32[]{:S(2)}) async-start(bf16[16,80,1024]{2,1,0:T(8,128)(2,1)} %broadcast_in_dim.52), calls=%async_computation | async-start | bytes 5242880 | tf_op jit(solution)/shard_map/all_to_all | solution.py:17
  22.1 1.6 bitcast_dynamic-update-slice_fusion.8
  25.1 3.2 %collective-permute-start.5 = (bf16[4,80,1024]{2,1,0:T(8,128)(2,1)}, bf16[4,80,1024]{2,1,0:T(8,128)(2,1)}, u32[]{:S(2)}, u32[]{:S(2)}) collective-permute-start(bf16[4,80,1024]{2,1,0:T(8,128)(2,1)} %bitcast_dynamic-update-slice_fusion.6), channel_id=1, source_target_pairs={{0,2},{1,3},{2,4},{3,5},{4,6},{5,7},{6,0},{7,1},{8,10},{9,11},{10,... | collective-permute-start | bytes 1966088 | tf_op jit(solution)/shard_map/ppermute | solution.py:58
  28.3 3.3 %collective-permute-start.4 = (bf16[4,80,1024]{2,1,0:T(8,128)(2,1)}, bf16[4,80,1024]{2,1,0:T(8,128)(2,1)}, u32[]{:S(2)}, u32[]{:S(2)}) collective-permute-start(bf16[4,80,1024]{2,1,0:T(8,128)(2,1)} %bitcast_dynamic-update-slice_fusion.6), channel_id=1, source_target_pairs={{0,6},{1,7},{2,0},{3,1},{4,2},{5,3},{6,4},{7,5},{8,14},{9,15},{10,... | collective-permute-start | bytes 1966088 | tf_op jit(solution)/shard_map/ppermute | solution.py:58
  31.7 36.6 %collective-permute-done.5 = bf16[4,80,1024]{2,1,0:T(8,128)(2,1)} collective-permute-done((bf16[4,80,1024]{2,1,0:T(8,128)(2,1)}, bf16[4,80,1024]{2,1,0:T(8,128)(2,1)}, u32[]{:S(2)}, u32[]{:S(2)}) %collective-permute-start.5) | collective-permute-done | bytes 655392 | tf_op jit(solution)/shard_map/ppermute | solution.py:58
  68.3 1.0 slice.121
  69.3 2.2 collective-permute-start.6
  71.5 1.0 slice.122
  72.5 4.3 %collective-permute-start.7 = (bf16[2,80,1024]{2,1,0:T(8,128)(2,1)S(1)}, bf16[2,80,1024]{2,1,0:T(8,128)(2,1)S(1)}, u32[]{:S(2)}, u32[]{:S(2)}) collective-permute-start(bf16[2,80,1024]{2,1,0:T(8,128)(2,1)S(1)} %slice.122), channel_id=1, source_target_pairs={{0,6},{1,7},{2,0},{3,1},{4,2},{5,3},{6,4},{7,5},{8,14},{9,15},{10,... | collective-permute-start | bytes 983048 | tf_op jit(solution)/shard_map/ppermute | solution.py:58
  76.8 1.8 broadcast_in_dim.53
  78.6 2.0 bitcast_dynamic-update-slice_fusion.3
  80.6 2.0 bitcast_dynamic-update-slice_fusion.2
  82.6 1.3 collective-permute-done.7
  84.8 2.0 bitcast_dynamic-update-slice_fusion.4
  86.8 3.2 %collective-permute-start.8 = (bf16[4,4,80,1024]{3,2,1,0:T(8,128)(2,1)}, bf16[4,4,80,1024]{3,2,1,0:T(8,128)(2,1)}, u32[]{:S(2)}, u32[]{:S(2)}) collective-permute-start(bf16[4,4,80,1024]{3,2,1,0:T(8,128)(2,1)} %bitcast.20), channel_id=1, source_target_pairs={{0,1},{1,0},{2,3},{3,2},{4,5},{5,4},{6,7},{7,6},{8,9},{9,8},{10,11... | collective-permute-start | bytes 7864328 | tf_op jit(solution)/shard_map/ppermute | solution.py:58
  90.1 1.9 collective-permute-start
  92.7 2.1 constant_dynamic-update-slice_fusion.1
  95.8 2.8 %collective-permute-done = bf16[16,80,1024]{2,1,0:T(8,128)(2,1)} collective-permute-done((bf16[16,80,1024]{2,1,0:T(8,128)(2,1)S(1)}, bf16[16,80,1024]{2,1,0:T(8,128)(2,1)}, u32[]{:S(2)}, u32[]{:S(2)}) %collective-permute-start) | collective-permute-done | bytes 2621472 | tf_op jit(solution)/shard_map/ppermute | solution.py:58
  98.7 3.3 %bitcast_dynamic-update-slice_fusion.1 = (bf16[16,2,80,1024]{3,2,1,0:T(8,128)(2,1)S(1)}, bf16[16,2,80,1024]{3,2,1,0:T(8,128)(2,1)S(1)}) fusion(bf16[16,2,80,1024]{3,2,1,0:T(8,128)(2,1)S(1)} %bitcast_dynamic-update-slice_fusion, s32[]{:T(128)S(6)} %select_n.93, bf16[16,80,1024]{2,1,0:T(8,128)(2,1)} %collective-permute-done, ...), kind=kLoop, calls=%fused_computation.13 | loop fusion | bytes 10485764 | tf_op jit(solution)/shard_map/dynamic_update_slice | solution.py:95
  102.0 1.9 fusion
  104.0 1.0 convolution_convert_fusion.2
  105.2 1.9 fusion.1
  107.1 1.2 copy-done.1
  108.3 1.0 convolution_convert_fusion.3
  109.5 31.4 %all_to_all.25 = bf16[16,80,128]{2,1,0:T(8,128)(2,1)S(1)} all-to-all(bf16[16,80,128]{2,1,0:T(8,128)(2,1)S(1)} %broadcast_in_dim.63), channel_id=1, replica_groups=mesh['dp'=16,'shard'=32] {'dp'}, dimensions={0} | all-to-all | bytes 655360 | tf_op jit(solution)/shard_map/all_to_all | solution.py:17
  141.4 2.5 %convolution_convert_fusion.1 = bf16[2560,32]{0,1:T(8,128)(2,1)S(1)} fusion(f32[160,2560]{1,0:T(8,128)} %copy-done.1, f32[80,32]{0,1:T(8,128)S(1)} %copy.99, f32[80,32]{0,1:T(8,128)S(1)} %copy.98), kind=kOutput, calls=%fused_computation.11 | convolution fusion | flops 157373440 | bytes 1822720 | tf_op jit(solution)/shard_map/dot_general | solution.py:140
  144.3 1.0 convolution_convert_fusion
  146.2 1.3 pad_maximum_fusion.2
  147.5 13.9 %all-to-all-start.2 = ((bf16[32,72,128]{2,1,0:T(8,128)(2,1)}), bf16[32,72,128]{2,1,0:T(8,128)(2,1)S(1)}, u32[]{:S(2)}, u32[]{:S(2)}) async-start(bf16[32,72,128]{2,1,0:T(8,128)(2,1)} %pad_maximum_fusion.2), calls=%async_computation.2 | async-start | bytes 1179648 | tf_op jit(solution)/shard_map/all_to_all | solution.py:17
  161.4 12.1 %all-to-all-done.2 = bf16[32,72,128]{2,1,0:T(8,128)(2,1)S(1)} async-done(((bf16[32,72,128]{2,1,0:T(8,128)(2,1)}), bf16[32,72,128]{2,1,0:T(8,128)(2,1)S(1)}, u32[]{:S(2)}, u32[]{:S(2)}) %all-to-all-start.2) | async-done | bytes 589856 | tf_op jit(solution)/shard_map/all_to_all | solution.py:17
  174.0 2.9 %cholesky.55 = f32[32,32]{1,0:T(8,128)S(1)} custom-call(f32[32,32]{1,0:T(8,128)S(1)} %fusion.26), custom_call_target="Cholesky" | custom-call | tf_op jit(solution)/shard_map/jit(cholesky)/cholesky | solution.py:108
  178.2 2.4 %custom-call.7 = f32[1,32,32]{1,2,0:T(8,128)S(1)} custom-call(f32[1,32,32]{2,1,0:T(8,128)S(1)} %fusion.24), custom_call_target="InvertDiagBlocksLowerTriangular" | custom-call | tf_op jit(solution)/shard_map/triangular_solve/custom-call.0 | solution.py:110
  181.2 2.9 %cholesky.44 = f32[32,32]{1,0:T(8,128)S(1)} custom-call(f32[32,32]{1,0:T(8,128)S(1)} %fusion.28), custom_call_target="Cholesky" | custom-call | tf_op jit(solution)/shard_map/jit(cholesky)/cholesky | solution.py:108
  185.4 2.4 %custom-call.6 = f32[1,32,32]{1,2,0:T(8,128)S(1)} custom-call(f32[1,32,32]{2,1,0:T(8,128)S(1)} %fusion.23), custom_call_target="InvertDiagBlocksLowerTriangular" | custom-call | tf_op jit(solution)/shard_map/triangular_solve/custom-call.0 | solution.py:110
  188.6 5.6 %all-to-all-start.3 = ((bf16[16,40,128]{2,1,0:T(8,128)(2,1)}), bf16[16,40,128]{2,1,0:T(8,128)(2,1)S(1)}, u32[]{:S(2)}, u32[]{:S(2)}) async-start(bf16[16,40,128]{2,1,0:T(8,128)(2,1)} %broadcast_in_dim.65), calls=%async_computation.3 | async-start | bytes 327680 | tf_op jit(solution)/shard_map/all_to_all | solution.py:17
  194.9 11.6 %all-to-all-done.3 = bf16[16,40,128]{2,1,0:T(8,128)(2,1)S(1)} async-done(((bf16[16,40,128]{2,1,0:T(8,128)(2,1)}), bf16[16,40,128]{2,1,0:T(8,128)(2,1)S(1)}, u32[]{:S(2)}, u32[]{:S(2)}) %all-to-all-start.3) | async-done | bytes 163872 | tf_op jit(solution)/shard_map/all_to_all | solution.py:17
  207.3 7.4 %all-to-all-start.4 = ((bf16[32,40,128]{2,1,0:T(8,128)(2,1)}), bf16[32,40,128]{2,1,0:T(8,128)(2,1)S(1)}, u32[]{:S(2)}, u32[]{:S(2)}) async-start(bf16[32,40,128]{2,1,0:T(8,128)(2,1)} %broadcast_in_dim.66), calls=%async_computation.4 | async-start | bytes 655360 | tf_op jit(solution)/shard_map/all_to_all | solution.py:17
  215.2 9.0 %all-to-all-done.4 = bf16[32,40,128]{2,1,0:T(8,128)(2,1)S(1)} async-done(((bf16[32,40,128]{2,1,0:T(8,128)(2,1)}), bf16[32,40,128]{2,1,0:T(8,128)(2,1)S(1)}, u32[]{:S(2)}, u32[]{:S(2)}) %all-to-all-start.4) | async-done | bytes 327712 | tf_op jit(solution)/shard_map/all_to_all | solution.py:17
  224.3 1.0 fusion.43
  225.6 1.1 pad_maximum_fusion
  227.0 1.3 fusion.4
  228.3 0.9 convolution_subtract_fusion.2
  229.2 1.3 fusion.5
  230.5 0.9 convolution_subtract_fusion.3
  (86 shorter events, 14.6 us)
Async XLA Ops:
  0.6 101.4 %copy-start = (bf16[1024,160]{0,1:T(8,128)(2,1)S(1)}, bf16[1024,160]{0,1:T(8,128)(2,1)}, u32[]{:S(2)}) copy-start(bf16[1024,160]{0,1:T(8,128)(2,1)} %param.13) | copy-start | bytes 983044
  0.6 23.1 %collective-permute-start.2 = (bf16[80,1024]{1,0:T(8,128)(2,1)}, bf16[80,1024]{1,0:T(8,128)(2,1)S(1)}, u32[]{:S(2)}, u32[]{:S(2)}) collective-permute-start(bf16[80,1024]{1,0:T(8,128)(2,1)} %bitcast.109), channel_id=1, source_target_pairs={{0,16},{1,17},{2,18},{3,19},{4,20},{5,21},{6,22},{7,23},{8,24},{9,... | collective-permute-start | bytes 491528 | tf_op jit(solution)/shard_map/ppermute | solution.py:58
  6.4 15.7 %collective-permute-start.1 = (bf16[80,1024]{1,0:T(8,128)(2,1)}, bf16[80,1024]{1,0:T(8,128)(2,1)}, u32[]{:S(2)}, u32[]{:S(2)}) collective-permute-start(bf16[80,1024]{1,0:T(8,128)(2,1)} %bitcast.110), channel_id=1, source_target_pairs={{0,24},{1,25},{2,26},{3,27},{4,28},{5,29},{6,30},{7,31},{8,0},{9,1... | collective-permute-start | bytes 491528 | tf_op jit(solution)/shard_map/ppermute | solution.py:58
  9.1 15.3 %collective-permute-start.3 = (bf16[80,1024]{1,0:T(8,128)(2,1)}, bf16[80,1024]{1,0:T(8,128)(2,1)S(1)}, u32[]{:S(2)}, u32[]{:S(2)}) collective-permute-start(bf16[80,1024]{1,0:T(8,128)(2,1)} %bitcast.111), channel_id=1, source_target_pairs={{0,8},{1,9},{2,10},{3,11},{4,12},{5,13},{6,14},{7,15},{8,16},{9,17... | collective-permute-start | bytes 491528 | tf_op jit(solution)/shard_map/ppermute | solution.py:58
  14.5 7.0 %copy-start.9 = (bf16[1024,80]{0,1:T(8,128)(2,1)S(1)}, bf16[1024,80]{0,1:T(8,128)(2,1)}, u32[]{:S(2)}) copy-start(bf16[1024,80]{0,1:T(8,128)(2,1)} %param.15) | copy-start | bytes 491524
  14.5 75.6 %all-to-all-start = ((bf16[16,80,1024]{2,1,0:T(8,128)(2,1)}), bf16[16,80,1024]{2,1,0:T(8,128)(2,1)S(1)}, u32[]{:S(2)}, u32[]{:S(2)}) async-start(bf16[16,80,1024]{2,1,0:T(8,128)(2,1)} %broadcast_in_dim.52), calls=%async_computation | async-start | bytes 5242880 | tf_op jit(solution)/shard_map/all_to_all | solution.py:17
  25.1 43.2 %collective-permute-start.5 = (bf16[4,80,1024]{2,1,0:T(8,128)(2,1)}, bf16[4,80,1024]{2,1,0:T(8,128)(2,1)}, u32[]{:S(2)}, u32[]{:S(2)}) collective-permute-start(bf16[4,80,1024]{2,1,0:T(8,128)(2,1)} %bitcast_dynamic-update-slice_fusion.6), channel_id=1, source_target_pairs={{0,2},{1,3},{2,4},{3,5},{4,6},{5,7},{6,0},{7,1},{8,10},{9,11},{10,... | collective-permute-start | bytes 1966088 | tf_op jit(solution)/shard_map/ppermute | solution.py:58
  28.3 43.2 %collective-permute-start.4 = (bf16[4,80,1024]{2,1,0:T(8,128)(2,1)}, bf16[4,80,1024]{2,1,0:T(8,128)(2,1)}, u32[]{:S(2)}, u32[]{:S(2)}) collective-permute-start(bf16[4,80,1024]{2,1,0:T(8,128)(2,1)} %bitcast_dynamic-update-slice_fusion.6), channel_id=1, source_target_pairs={{0,6},{1,7},{2,0},{3,1},{4,2},{5,3},{6,4},{7,5},{8,14},{9,15},{10,... | collective-permute-start | bytes 1966088 | tf_op jit(solution)/shard_map/ppermute | solution.py:58
  69.3 13.3 %collective-permute-start.6 = (bf16[2,80,1024]{2,1,0:T(8,128)(2,1)S(1)}, bf16[2,80,1024]{2,1,0:T(8,128)(2,1)S(1)}, u32[]{:S(2)}, u32[]{:S(2)}) collective-permute-start(bf16[2,80,1024]{2,1,0:T(8,128)(2,1)S(1)} %slice.121), channel_id=1, source_target_pairs={{0,2},{1,3},{2,4},{3,5},{4,6},{5,7},{6,0},{7,1},{8,10},{9,11},{10,... | collective-permute-start | bytes 983048 | tf_op jit(solution)/shard_map/ppermute | solution.py:58
  72.5 11.4 %collective-permute-start.7 = (bf16[2,80,1024]{2,1,0:T(8,128)(2,1)S(1)}, bf16[2,80,1024]{2,1,0:T(8,128)(2,1)S(1)}, u32[]{:S(2)}, u32[]{:S(2)}) collective-permute-start(bf16[2,80,1024]{2,1,0:T(8,128)(2,1)S(1)} %slice.122), channel_id=1, source_target_pairs={{0,6},{1,7},{2,0},{3,1},{4,2},{5,3},{6,4},{7,5},{8,14},{9,15},{10,... | collective-permute-start | bytes 983048 | tf_op jit(solution)/shard_map/ppermute | solution.py:58
  86.8 9.0 %collective-permute-start.8 = (bf16[4,4,80,1024]{3,2,1,0:T(8,128)(2,1)}, bf16[4,4,80,1024]{3,2,1,0:T(8,128)(2,1)}, u32[]{:S(2)}, u32[]{:S(2)}) collective-permute-start(bf16[4,4,80,1024]{3,2,1,0:T(8,128)(2,1)} %bitcast.20), channel_id=1, source_target_pairs={{0,1},{1,0},{2,3},{3,2},{4,5},{5,4},{6,7},{7,6},{8,9},{9,8},{10,11... | collective-permute-start | bytes 7864328 | tf_op jit(solution)/shard_map/ppermute | solution.py:58
  90.1 8.6 %collective-permute-start = (bf16[16,80,1024]{2,1,0:T(8,128)(2,1)S(1)}, bf16[16,80,1024]{2,1,0:T(8,128)(2,1)}, u32[]{:S(2)}, u32[]{:S(2)}) collective-permute-start(bf16[16,80,1024]{2,1,0:T(8,128)(2,1)S(1)} %all-to-all-done), channel_id=1, source_target_pairs={{0,1},{1,0},{2,3},{3,2},{4,5},{5,4},{6,7},{7,6},{8,9},{9,8},{10,11... | collective-permute-start | bytes 7864328 | tf_op jit(solution)/shard_map/ppermute | solution.py:58
  98.7 3.4 %copy-start.3 = (bf16[1,160,2560]{2,1,0:T(8,128)(2,1)S(1)}, bf16[1,160,2560]{2,1,0:T(8,128)(2,1)}, u32[]{:S(2)}) copy-start(bf16[1,160,2560]{2,1,0:T(8,128)(2,1)} %param.17) | copy-start | bytes 2457604
  102.0 1.9 copy-start.6
  104.0 1.1 copy-start.4
  104.0 1.2 copy-start.5
  107.1 1.2 copy-start.1
  147.5 26.1 %all-to-all-start.2 = ((bf16[32,72,128]{2,1,0:T(8,128)(2,1)}), bf16[32,72,128]{2,1,0:T(8,128)(2,1)S(1)}, u32[]{:S(2)}, u32[]{:S(2)}) async-start(bf16[32,72,128]{2,1,0:T(8,128)(2,1)} %pad_maximum_fusion.2), calls=%async_computation.2 | async-start | bytes 1179648 | tf_op jit(solution)/shard_map/all_to_all | solution.py:17
  188.6 18.0 %all-to-all-start.3 = ((bf16[16,40,128]{2,1,0:T(8,128)(2,1)}), bf16[16,40,128]{2,1,0:T(8,128)(2,1)S(1)}, u32[]{:S(2)}, u32[]{:S(2)}) async-start(bf16[16,40,128]{2,1,0:T(8,128)(2,1)} %broadcast_in_dim.65), calls=%async_computation.3 | async-start | bytes 327680 | tf_op jit(solution)/shard_map/all_to_all | solution.py:17
  207.3 16.9 %all-to-all-start.4 = ((bf16[32,40,128]{2,1,0:T(8,128)(2,1)}), bf16[32,40,128]{2,1,0:T(8,128)(2,1)S(1)}, u32[]{:S(2)}, u32[]{:S(2)}) async-start(bf16[32,40,128]{2,1,0:T(8,128)(2,1)} %broadcast_in_dim.66), calls=%async_computation.4 | async-start | bytes 655360 | tf_op jit(solution)/shard_map/all_to_all | solution.py:17
  226.7 1.5 copy-start.7
  227.0 2.2 copy-start.2
  228.3 2.2 copy-start.8

commit v3 on v2

--- a/solution.py
+++ b/solution.py
@@ -1,6 +1,10 @@
+import functools
+
 import jax
 import jax.numpy as jnp
 from jax import lax
+from jax.experimental import pallas as pl
+from jax.experimental.pallas import tpu as pltpu
 from jax.sharding import PartitionSpec as P
 
 
@@ -58,50 +62,87 @@
     return lax.ppermute(array, "shard", in_plane(rows, cols, core))
 
 
-def in_order(pieces, position):
-    count = len(pieces)
-    result = jnp.zeros((count, *pieces[0].shape), pieces[0].dtype)
-    for k, piece in enumerate(pieces):
-        at = (position + k) % count
-        result = lax.dynamic_update_slice_in_dim(result, piece[None], at, 0)
-    return result
-
-
 def by_exchange(cotan):
-    chips = lax.axis_size("shard") // 2
-    same_core = [[2 * chip + core for chip in range(chips)] for core in range(2)]
-    return exchange(copies(cotan.T, chips), "shard", same_core)
+    side = 4
+    rows = [[(y * side + x) * 2 + c for x in range(side)] for y in range(side) for c in range(2)]
+    cols = [[(y * side + x) * 2 + c for y in range(side)] for x in range(side) for c in range(2)]
+    row = exchange(copies(cotan.T, side), "shard", rows)
+    return exchange(copies(row, side), "shard", cols)
 
 
 def by_rings(cotan):
-    shard = lax.axis_index("shard")
-    y, x = shard // 8, shard // 2 % 4
     block = cotan.T
     below, above, across = send(block, 1, 0), send(block, 3, 0), send(block, 2, 0)
-    column = in_order([block, above, across, below], y)
+    column = jnp.stack([block, above, across, below])
     left, right = send(column, 0, 1), send(column, 0, 3)
     half = column.shape[0] // 2
     far = jnp.concatenate([send(left[:half], 0, 1), send(right[half:], 0, 3)])
-    return jnp.swapaxes(in_order([column, right, far, left], x), 0, 1)
-
-
-def all_columns(mine):
-    theirs = send(mine, 0, 0, 1)
-    tokens = mine.shape[-1]
-    core = lax.axis_index("shard") % 2
-    both = jnp.zeros((mine.size // mine.shape[-2] // tokens, 2, *mine.shape[-2:]), mine.dtype)
-    for array, at in ((mine, core), (theirs, 1 - core)):
-        array = array.reshape(-1, 1, *mine.shape[-2:])
-        both = lax.dynamic_update_slice_in_dim(both, array, at, 1)
-    return both.reshape(-1, tokens)
+    return column, right, far, left
+
+
+def partner(array):
+    return send(array, 0, 0, 1)
+
+
+def gradient_kernel(blocks, place, acts, error, start, *refs):
+    sources, (full, left, columns, done) = refs[:-4], refs[-4:]
+    mine, theirs = sources[: len(sources) // 2], sources[len(sources) // 2 :]
+    side, each = 4, columns.shape[1] // 8
+    y0, x0, core = place[0], place[1], place[2]
+
+    def fetch(j, k, other):
+        source = blocks(theirs if other else mine, j, k)
+        at = ((x0 + k) % side * 2 + (1 - core if other else core)) * each
+        return pltpu.make_async_copy(
+            source,
+            columns.at[j, pl.ds(pl.multiple_of(at, 16), each), :],
+            done.at[j, k * 2 + other],
+        )
+
+    steps = [(k, other) for k in range(side) for other in range(2)]
+    for j in range(side):
+        for k, other in steps:
+            fetch(j, k, other).start()
+    total = jnp.zeros(left.shape, F32)
+    for j in range(side):
+        for k, other in steps:
+            fetch(j, k, other).wait()
+        here = pl.ds(pl.multiple_of((y0 + j) % side * (8 * each), 128), 8 * each)
+        part = contract(acts[...], columns[j], (1, 1)) + error[:, here].astype(F32)
+        full[:, here] = part
+        high, low = split_high_low(part)
+        factor = start[:, here]
+        total += contract(high, factor, (1, 1)) + contract(low, factor, (1, 1))
+    left[...] = total
+
+
+def full_gradient(inputs, error, start, mine, theirs, blocks, place):
+    rows, tokens = inputs.shape[::-1]
+    width, rank = error.shape[-1], start.shape[-1]
+    vmem = pl.BlockSpec(memory_space=pltpu.VMEM)
+    return pl.pallas_call(
+        functools.partial(gradient_kernel, blocks),
+        out_shape=(
+            jax.ShapeDtypeStruct((rows, width), F32),
+            jax.ShapeDtypeStruct((rows, rank), F32),
+        ),
+        in_specs=[
+            pl.BlockSpec(memory_space=pltpu.SMEM),
+            vmem,
+            vmem,
+            vmem,
+            *[pl.BlockSpec(memory_space=pl.ANY)] * (len(mine) + len(theirs)),
+        ],
+        out_specs=(vmem, vmem),
+        scratch_shapes=[
+            pltpu.VMEM((4, width // 4, tokens), BF16),
+            pltpu.SemaphoreType.DMA((4, 8)),
+        ],
+    )(place, inputs.T, error[0], start.T, *mine, *theirs)
 
 
 def contract(a, b, dims):
     return lax.dot_general(a, b, ((dims[:1], dims[1:]), ((), ())), preferred_element_type=F32)
-
-
-def full_gradient(inputs, columns, error):
-    return contract(inputs.T, columns, (1, 1)) + error[0].astype(F32)
 
 
 def inverse_factor(gram):
@@ -123,15 +164,31 @@
 ):
     replicas = lax.axis_size("dp")
     shards = lax.axis_size("shard")
-    start = start_factors.astype(F32)
-
-    query_blocks = by_exchange(query_cotan)
-    query_columns = all_columns(query_blocks)
-    output_columns = all_columns(by_rings(output_cotan))
-    query_full = full_gradient(hidden_in, query_columns, query_error)
-    output_full = full_gradient(context_in, output_columns, output_error)
-    query_left = jnp.dot(query_full, start[0], precision=HIGH)
-    output_left = jnp.dot(output_full, start[1], precision=HIGH)
+    shard = lax.axis_index("shard")
+    y, x, core = shard // 8, shard // 2 % 4, shard % 2
+    query_mine = (by_exchange(query_cotan),)
+    query_theirs = [partner(a) for a in query_mine]
+    output_mine = by_rings(output_cotan)
+    query_full, query_left = full_gradient(
+        hidden_in,
+        query_error,
+        start_factors[0],
+        query_mine,
+        query_theirs,
+        lambda refs, j, k: refs[0].at[j, k],
+        jnp.stack([0 * core, 0 * core, core]),
+    )
+    column, right, far, left = output_mine
+    far = partner(far)
+    output_full, output_left = full_gradient(
+        context_in,
+        output_error,
+        start_factors[1],
+        output_mine,
+        [partner(column), partner(right), far, partner(left)],
+        lambda refs, j, k: refs[k].at[j],
+        jnp.stack([y, x, core]),
+    )
 
     lefts = from_everyone(side_by_side(query_left, output_left).astype(BF16), "dp")
     query_left, output_left = apart(lefts.astype(F32).sum(axis=0) / F32(replicas))

time: 232 us -> 247 us (1.065)
  blocking collectives: 31.4 us -> 78.5 us
  waiting for transfers between devices: 73.6 us -> 51 us
  local copies, waits for them, and re-layouts: 30.4 us -> 12.8 us
  Pallas kernels: 0 us -> 15.1 us
  matrix products: 15.5 us -> 8.3 us
    all_to_all x1 -> x3, blocking collectives: 31.4 us -> 78.5 us  [exchange(): lax.all_to_all(array, axis, 0, 0, tiled=True, axis_index_groups=groups)]
    ppermute x9 -> x12, waiting for transfers between devices: 40.8 us -> 18.1 us  [send(): return lax.ppermute(array, 'shard', in_plane(rows, cols, core))]
    dynamic_update_slice x10 -> x0, local copies, waits for them, and re-layouts: 15.3 us -> none  [the longest x7 9.56 us: in_order(): result = lax.dynamic_update_slice_in_dim(result, piece[None], at, 0)]
    pallas_call x0 -> x2, Pallas kernels: none -> 15.1 us  [full_gradient(): pl.pallas_call(functools.partial(gradient_kernel, blocks), out_shape=(jax...]
    all_to_all x4 -> x3, starting transfers between devices: 32.9 us -> 23.3 us  [exchange(): lax.all_to_all(array, axis, 0, 0, tiled=True, axis_index_groups=groups)]
    ppermute x9 -> x12, starting transfers between devices: 29.2 us -> 37.5 us  [send(): return lax.ppermute(array, 'shard', in_plane(rows, cols, core))]
    dot_general x6 -> x4, matrix products: 8.22 us -> 4.41 us  [contract(): lax.dot_general(a, b, ((dims[:1], dims[1:]), ((), ())), preferred_element...]
    broadcast_in_dim x2 -> x0, local copies, waits for them, and re-layouts: 2.72 us -> none  [in_order(): result = jnp.zeros((count, *pieces[0].shape), pieces[0].dtype)]
  transfers between devices with their start and end apart: 13 -> 15, of which waited for: 6 -> 8; matrix products, arithmetic and copies ran while one was open for 10% -> 4% of each run, Pallas kernels for 0% -> 3%
where the time goes in v3:
time: 247 us; the launch traced here: 246 us
  blocking collectives  78.5 us (32%)
  starting transfers between devices  60.8 us (25%)
  waiting for transfers between devices  51 us (21%)
  other arithmetic  17.9 us (7%)
  Pallas kernels  15.1 us (6%)
  local copies, waits for them, and re-layouts  12.8 us (5%)
  matrix products  8.3 us (3%)
    all_to_all x3, blocking collectives, exchange(): lax.all_to_all(array, axis, 0, 0, tiled=True, axis_index_groups=groups)  78.5 us
    ppermute x12, starting transfers between devices, send(): return lax.ppermute(array, 'shard', in_plane(rows, cols, core))  37.5 us
    all_to_all x3, waiting for transfers between devices, exchange(): lax.all_to_all(array, axis, 0, 0, tiled=True, axis_index_groups=groups)  32.9 us
    all_to_all x3, starting transfers between devices, exchange(): lax.all_to_all(array, axis, 0, 0, tiled=True, axis_index_groups=groups)  23.3 us
    ppermute x12, waiting for transfers between devices, send(): return lax.ppermute(array, 'shard', in_plane(rows, cols, core))  18.1 us
    pallas_call x2, Pallas kernels, full_gradient(): pl.pallas_call(functools.partial(gradient_kernel, blocks), out_shape=(jax...  15.1 us
    another operation x6, other arithmetic, inverse_factor(): chol = jnp.linalg.cholesky(gram)  7.2 us
    another operation x4, other arithmetic, inverse_factor(): return lax.linalg.triangular_solve(chol, eye, left_side=True, lower=True)  6.17 us
  transfers between devices with their start and end apart: 15, of which 8 were waited for; matrix products, arithmetic and copies ran while one was open for 4% of the time, Pallas kernels for 3%

profile of v3, /device:TPU:1, one launch (start us, length us, event | category | flops | bytes accessed | tf_op | source)
XLA Modules:
  0.0 245.6 jit_solution(766911660298098514)
XLA Ops:
  0.6 1.0 broadcast_in_dim.25
  1.6 12.3 %all_to_all.30 = bf16[4,80,1024]{2,1,0:T(8,128)(2,1)S(1)} all-to-all(bf16[4,80,1024]{2,1,0:T(8,128)(2,1)S(1)} %broadcast_in_dim.25), channel_id=1, replica_groups={{0,2,4,6},{1,3,5,7},{8,10,12,14},{9,11,13,15},{16,18,20,22},{17,19,21,2..., dimensions={0} | all-to-all | bytes 1310720 | tf_op jit(solution)/shard_map/all_to_all | solution.py:21
  14.2 36.2 %all_to_all.31.refs_0_ = bf16[4,4,80,1024]{3,2,1,0:T(8,128)(2,1)S(1)} all-to-all(bf16[4,4,80,1024]{3,2,1,0:T(8,128)(2,1)S(1)} %broadcast_in_dim.26), channel_id=1, replica_groups={{0,8,16,24},{1,9,17,25},{2,10,18,26},{3,11,19,27},{4,12,20,28},{5,13,21..., dimensions={0} | all-to-all | bytes 5242880 | tf_op jit(solution)/shard_map/all_to_all | solution.py:21
  50.4 5.1 %collective-permute-start = (bf16[4,4,80,1024]{3,2,1,0:T(8,128)(2,1)S(1)}, bf16[4,4,80,1024]{3,2,1,0:T(8,128)(2,1)}, u32[]{:S(2)}, u32[]{:S(2)}) collective-permute-start(bf16[4,4,80,1024]{3,2,1,0:T(8,128)(2,1)S(1)} %all_to_all.31.refs_0_), channel_id=1, source_target_pairs={{0,1},{1,0},{2,3},{3,2},{4,5},{5,4},{6,7},{7,6},{8,9},{9,8},{10,11... | collective-permute-start | bytes 7864328 | tf_op jit(solution)/shard_map/ppermute | solution.py:62
  55.6 2.4 collective-permute-start.2
  58.0 4.0 %collective-permute-start.1 = (bf16[80,1024]{1,0:T(8,128)(2,1)S(1)}, bf16[80,1024]{1,0:T(8,128)(2,1)S(1)}, u32[]{:S(2)}, u32[]{:S(2)}) collective-permute-start(bf16[80,1024]{1,0:T(8,128)(2,1)S(1)} %bitcast.65), channel_id=1, source_target_pairs={{0,24},{1,25},{2,26},{3,27},{4,28},{5,29},{6,30},{7,31},{8,0},{9,1... | collective-permute-start | bytes 491528 | tf_op jit(solution)/shard_map/ppermute | solution.py:62
  62.1 1.9 collective-permute-start.3
  64.0 0.7 collective-permute-done.2
  64.7 2.0 collective-permute-done.1
  66.7 3.6 %collective-permute-done.3 = bf16[80,1024]{1,0:T(8,128)(2,1)S(1)} collective-permute-done((bf16[80,1024]{1,0:T(8,128)(2,1)S(1)}, bf16[80,1024]{1,0:T(8,128)(2,1)S(1)}, u32[]{:S(2)}, u32[]{:S(2)}) %collective-permute-start.3) | collective-permute-done | bytes 163872 | tf_op jit(solution)/shard_map/ppermute | solution.py:62
  70.5 2.2 collective-permute-start.5
  72.7 4.3 %collective-permute-start.4 = (bf16[4,80,1024]{2,1,0:T(8,128)(2,1)S(1)}, bf16[4,80,1024]{2,1,0:T(8,128)(2,1)S(1)}, u32[]{:S(2)}, u32[]{:S(2)}) collective-permute-start(bf16[4,80,1024]{2,1,0:T(8,128)(2,1)S(1)} %pad_maximum_fusion.refs_0_), channel_id=1, source_target_pairs={{0,6},{1,7},{2,0},{3,1},{4,2},{5,3},{6,4},{7,5},{8,14},{9,15},{10,... | collective-permute-start | bytes 1966088 | tf_op jit(solution)/shard_map/ppermute | solution.py:62
  77.0 11.5 %collective-permute-done.5.refs_3_ = bf16[4,80,1024]{2,1,0:T(8,128)(2,1)S(1)} collective-permute-done((bf16[4,80,1024]{2,1,0:T(8,128)(2,1)S(1)}, bf16[4,80,1024]{2,1,0:T(8,128)(2,1)S(1)}, u32[]{:S(2)}, u32[]{:S(2)}) %collective-permute-start.5) | collective-permute-done | bytes 655392 | tf_op jit(solution)/shard_map/ppermute | solution.py:62
  88.4 0.8 slice.121
  89.2 1.9 collective-permute-start.6
  91.2 0.8 slice.122
  92.1 4.6 %collective-permute-start.7 = (bf16[2,80,1024]{2,1,0:T(8,128)(2,1)}, bf16[2,80,1024]{2,1,0:T(8,128)(2,1)}, u32[]{:S(2)}, u32[]{:S(2)}) collective-permute-start(bf16[2,80,1024]{2,1,0:T(8,128)(2,1)} %slice.122), channel_id=1, source_target_pairs={{0,6},{1,7},{2,0},{3,1},{4,2},{5,3},{6,4},{7,5},{8,14},{9,15},{10,... | collective-permute-start | bytes 983048 | tf_op jit(solution)/shard_map/ppermute | solution.py:62
  97.9 4.7 %collective-permute-start.8 = (bf16[4,80,1024]{2,1,0:T(8,128)(2,1)S(1)}, bf16[4,80,1024]{2,1,0:T(8,128)(2,1)S(1)}, u32[]{:S(2)}, u32[]{:S(2)}) collective-permute-start(bf16[4,80,1024]{2,1,0:T(8,128)(2,1)S(1)} %pad_maximum_fusion.refs_0_), channel_id=1, source_target_pairs={{0,1},{1,0},{2,3},{3,2},{4,5},{5,4},{6,7},{7,6},{8,9},{9,8},{10,11... | collective-permute-start | bytes 1966088 | tf_op jit(solution)/shard_map/ppermute | solution.py:62
  102.7 1.9 collective-permute-start.11
  104.6 2.4 collective-permute-start.9
  107.0 1.0 constant_dynamic-update-slice_fusion.1
  108.1 1.0 constant_dynamic-update-slice_fusion.refs_2_
  109.1 1.9 collective-permute-start.10
  111.0 1.7 slice_bitcast_fusion
  114.5 7.6 %shard_map.121 = (f32[160,2560]{1,0:T(8,128)}, f32[160,32]{1,0:T(8,128)}) custom-call(s32[3]{0:T(128)} %add_add_fusion.place, bf16[160,1024]{1,0:T(8,128)(2,1)} %bitcast.62, bf16[160,2560]{1,0:T(8,128)(2,1)} %bitcast.60, bf16[32,2560]{1,0:T(8,128)(2,1)} %get-tuple-element.26.start, bf16[4,80,1024]{2,1,0:T(8,128)(2,1)} %copy-done.4, ...), custom_call_target="tpu_custom_call" | custom-call | tf_op jit(solution)/shard_map/pallas_call | solution.py:123
  122.0 0.9 convert.28
  122.9 7.6 %shard_map.120 = (f32[160,2560]{1,0:T(8,128)}, f32[160,32]{1,0:T(8,128)}) custom-call(s32[3]{0:T(128)} %stack.32.place, bf16[160,1024]{1,0:T(8,128)(2,1)} %bitcast.63, bf16[160,2560]{1,0:T(8,128)(2,1)} %bitcast.61, bf16[32,2560]{1,0:T(8,128)(2,1)} %get-tuple-element.27.start, bf16[4,4,80,1024]{3,2,1,0:T(8,128)(2,1)} %copy-done, ...), custom_call_target="tpu_custom_call" | custom-call | tf_op jit(solution)/shard_map/pallas_call | solution.py:123
  130.5 1.0 convert.27
  131.7 30.0 %all_to_all.32 = bf16[16,80,128]{2,1,0:T(8,128)(2,1)S(1)} all-to-all(bf16[16,80,128]{2,1,0:T(8,128)(2,1)S(1)} %broadcast_in_dim.27), channel_id=1, replica_groups=mesh['dp'=16,'shard'=32] {'dp'}, dimensions={0} | all-to-all | bytes 655360 | tf_op jit(solution)/shard_map/all_to_all | solution.py:21
  162.5 1.0 convolution_convert_fusion.1
  163.7 1.0 convolution_convert_fusion
  165.7 1.3 pad_maximum_fusion.3
  166.9 10.2 %all-to-all-start.3 = ((bf16[32,72,128]{2,1,0:T(8,128)(2,1)}), bf16[32,72,128]{2,1,0:T(8,128)(2,1)S(1)}, u32[]{:S(2)}, u32[]{:S(2)}) async-start(bf16[32,72,128]{2,1,0:T(8,128)(2,1)} %pad_maximum_fusion.3), calls=%async_computation.3 | async-start | bytes 1179648 | tf_op jit(solution)/shard_map/all_to_all | solution.py:21
  177.1 12.2 %all-to-all-done.3 = bf16[32,72,128]{2,1,0:T(8,128)(2,1)S(1)} async-done(((bf16[32,72,128]{2,1,0:T(8,128)(2,1)}), bf16[32,72,128]{2,1,0:T(8,128)(2,1)S(1)}, u32[]{:S(2)}, u32[]{:S(2)}) %all-to-all-start.3) | async-done | bytes 589856 | tf_op jit(solution)/shard_map/all_to_all | solution.py:21
  189.8 2.9 %cholesky.55 = f32[32,32]{1,0:T(8,128)S(1)} custom-call(f32[32,32]{1,0:T(8,128)S(1)} %fusion.19), custom_call_target="Cholesky" | custom-call | tf_op jit(solution)/shard_map/jit(cholesky)/cholesky | solution.py:149
  194.1 2.4 custom-call.7
  197.0 2.9 %cholesky.44 = f32[32,32]{1,0:T(8,128)S(1)} custom-call(f32[32,32]{1,0:T(8,128)S(1)} %fusion.21), custom_call_target="Cholesky" | custom-call | tf_op jit(solution)/shard_map/jit(cholesky)/cholesky | solution.py:149
  201.2 2.4 custom-call.6
  203.7 0.7 broadcast_in_dim.29
  204.4 5.7 %all-to-all-start.4 = ((bf16[16,40,128]{2,1,0:T(8,128)(2,1)}), bf16[16,40,128]{2,1,0:T(8,128)(2,1)S(1)}, u32[]{:S(2)}, u32[]{:S(2)}) async-start(bf16[16,40,128]{2,1,0:T(8,128)(2,1)} %broadcast_in_dim.29), calls=%async_computation.4 | async-start | bytes 327680 | tf_op jit(solution)/shard_map/all_to_all | solution.py:21
  210.8 11.6 %all-to-all-done.4 = bf16[16,40,128]{2,1,0:T(8,128)(2,1)S(1)} async-done(((bf16[16,40,128]{2,1,0:T(8,128)(2,1)}), bf16[16,40,128]{2,1,0:T(8,128)(2,1)S(1)}, u32[]{:S(2)}, u32[]{:S(2)}) %all-to-all-start.4) | async-done | bytes 163872 | tf_op jit(solution)/shard_map/all_to_all | solution.py:21
  222.4 0.8 broadcast_in_dim.30
  223.2 7.4 %all-to-all-start.5 = ((bf16[32,40,128]{2,1,0:T(8,128)(2,1)}), bf16[32,40,128]{2,1,0:T(8,128)(2,1)S(1)}, u32[]{:S(2)}, u32[]{:S(2)}) async-start(bf16[32,40,128]{2,1,0:T(8,128)(2,1)} %broadcast_in_dim.30), calls=%async_computation.5 | async-start | bytes 655360 | tf_op jit(solution)/shard_map/all_to_all | solution.py:21
  231.1 9.0 %all-to-all-done.5 = bf16[32,40,128]{2,1,0:T(8,128)(2,1)S(1)} async-done(((bf16[32,40,128]{2,1,0:T(8,128)(2,1)}), bf16[32,40,128]{2,1,0:T(8,128)(2,1)S(1)}, u32[]{:S(2)}, u32[]{:S(2)}) %all-to-all-start.5) | async-done | bytes 327712 | tf_op jit(solution)/shard_map/all_to_all | solution.py:21
  241.2 1.3 fusion.2
  242.5 0.9 convolution_subtract_fusion.2
  243.4 1.3 fusion.3
  244.7 0.9 convolution_subtract_fusion.3
  (92 shorter events, 11.1 us)
Async XLA Ops:
  14.2 41.3 %copy-start.12 = (bf16[1024,80]{0,1:T(8,128)(2,1)S(1)}, bf16[1024,80]{0,1:T(8,128)(2,1)}, u32[]{:S(2)}) copy-start(bf16[1024,80]{0,1:T(8,128)(2,1)} %param.15) | copy-start | bytes 491524
  50.4 57.6 %copy-start = (bf16[4,4,80,1024]{3,2,1,0:T(8,128)(2,1)}, bf16[4,4,80,1024]{3,2,1,0:T(8,128)(2,1)S(1)}, u32[]{:S(2)}) copy-start(bf16[4,4,80,1024]{3,2,1,0:T(8,128)(2,1)S(1)} %all_to_all.31.refs_0_) | copy-start | bytes 7864324
  50.4 72.5 %collective-permute-start = (bf16[4,4,80,1024]{3,2,1,0:T(8,128)(2,1)S(1)}, bf16[4,4,80,1024]{3,2,1,0:T(8,128)(2,1)}, u32[]{:S(2)}, u32[]{:S(2)}) collective-permute-start(bf16[4,4,80,1024]{3,2,1,0:T(8,128)(2,1)S(1)} %all_to_all.31.refs_0_), channel_id=1, source_target_pairs={{0,1},{1,0},{2,3},{3,2},{4,5},{5,4},{6,7},{7,6},{8,9},{9,8},{10,11... | collective-permute-start | bytes 7864328 | tf_op jit(solution)/shard_map/ppermute | solution.py:62
  55.6 9.1 %collective-permute-start.2 = (bf16[80,1024]{1,0:T(8,128)(2,1)S(1)}, bf16[80,1024]{1,0:T(8,128)(2,1)S(1)}, u32[]{:S(2)}, u32[]{:S(2)}) collective-permute-start(bf16[80,1024]{1,0:T(8,128)(2,1)S(1)} %bitcast.64), channel_id=1, source_target_pairs={{0,16},{1,17},{2,18},{3,19},{4,20},{5,21},{6,22},{7,23},{8,24},{9,... | collective-permute-start | bytes 491528 | tf_op jit(solution)/shard_map/ppermute | solution.py:62
  58.0 8.7 %collective-permute-start.1 = (bf16[80,1024]{1,0:T(8,128)(2,1)S(1)}, bf16[80,1024]{1,0:T(8,128)(2,1)S(1)}, u32[]{:S(2)}, u32[]{:S(2)}) collective-permute-start(bf16[80,1024]{1,0:T(8,128)(2,1)S(1)} %bitcast.65), channel_id=1, source_target_pairs={{0,24},{1,25},{2,26},{3,27},{4,28},{5,29},{6,30},{7,31},{8,0},{9,1... | collective-permute-start | bytes 491528 | tf_op jit(solution)/shard_map/ppermute | solution.py:62
  62.1 8.3 %collective-permute-start.3 = (bf16[80,1024]{1,0:T(8,128)(2,1)S(1)}, bf16[80,1024]{1,0:T(8,128)(2,1)S(1)}, u32[]{:S(2)}, u32[]{:S(2)}) collective-permute-start(bf16[80,1024]{1,0:T(8,128)(2,1)S(1)} %bitcast.66), channel_id=1, source_target_pairs={{0,8},{1,9},{2,10},{3,11},{4,12},{5,13},{6,14},{7,15},{8,16},{9,17... | collective-permute-start | bytes 491528 | tf_op jit(solution)/shard_map/ppermute | solution.py:62
  70.4 42.3 %copy-start.4 = (bf16[4,80,1024]{2,1,0:T(8,128)(2,1)}, bf16[4,80,1024]{2,1,0:T(8,128)(2,1)S(1)}, u32[]{:S(2)}) copy-start(bf16[4,80,1024]{2,1,0:T(8,128)(2,1)S(1)} %pad_maximum_fusion.refs_0_) | copy-start | bytes 1966084
  70.5 18.0 %collective-permute-start.5 = (bf16[4,80,1024]{2,1,0:T(8,128)(2,1)S(1)}, bf16[4,80,1024]{2,1,0:T(8,128)(2,1)S(1)}, u32[]{:S(2)}, u32[]{:S(2)}) collective-permute-start(bf16[4,80,1024]{2,1,0:T(8,128)(2,1)S(1)} %pad_maximum_fusion.refs_0_), channel_id=1, source_target_pairs={{0,2},{1,3},{2,4},{3,5},{4,6},{5,7},{6,0},{7,1},{8,10},{9,11},{10,... | collective-permute-start | bytes 1966088 | tf_op jit(solution)/shard_map/ppermute | solution.py:62
  72.7 18.5 %collective-permute-start.4 = (bf16[4,80,1024]{2,1,0:T(8,128)(2,1)S(1)}, bf16[4,80,1024]{2,1,0:T(8,128)(2,1)S(1)}, u32[]{:S(2)}, u32[]{:S(2)}) collective-permute-start(bf16[4,80,1024]{2,1,0:T(8,128)(2,1)S(1)} %pad_maximum_fusion.refs_0_), channel_id=1, source_target_pairs={{0,6},{1,7},{2,0},{3,1},{4,2},{5,3},{6,4},{7,5},{8,14},{9,15},{10,... | collective-permute-start | bytes 1966088 | tf_op jit(solution)/shard_map/ppermute | solution.py:62
  88.4 2.7 %copy-start.5 = (bf16[4,80,1024]{2,1,0:T(8,128)(2,1)}, bf16[4,80,1024]{2,1,0:T(8,128)(2,1)S(1)}, u32[]{:S(2)}) copy-start(bf16[4,80,1024]{2,1,0:T(8,128)(2,1)S(1)} %collective-permute-done.5.refs_3_) | copy-start | bytes 1966084
  89.2 15.4 %collective-permute-start.6 = (bf16[2,80,1024]{2,1,0:T(8,128)(2,1)}, bf16[2,80,1024]{2,1,0:T(8,128)(2,1)}, u32[]{:S(2)}, u32[]{:S(2)}) collective-permute-start(bf16[2,80,1024]{2,1,0:T(8,128)(2,1)} %slice.121), channel_id=1, source_target_pairs={{0,2},{1,3},{2,4},{3,5},{4,6},{5,7},{6,0},{7,1},{8,10},{9,11},{10,... | collective-permute-start | bytes 983048 | tf_op jit(solution)/shard_map/ppermute | solution.py:62
  91.2 0.9 copy-start.6
  92.1 15.9 %collective-permute-start.7 = (bf16[2,80,1024]{2,1,0:T(8,128)(2,1)}, bf16[2,80,1024]{2,1,0:T(8,128)(2,1)}, u32[]{:S(2)}, u32[]{:S(2)}) collective-permute-start(bf16[2,80,1024]{2,1,0:T(8,128)(2,1)} %slice.122), channel_id=1, source_target_pairs={{0,6},{1,7},{2,0},{3,1},{4,2},{5,3},{6,4},{7,5},{8,14},{9,15},{10,... | collective-permute-start | bytes 983048 | tf_op jit(solution)/shard_map/ppermute | solution.py:62
  97.9 14.8 %collective-permute-start.8 = (bf16[4,80,1024]{2,1,0:T(8,128)(2,1)S(1)}, bf16[4,80,1024]{2,1,0:T(8,128)(2,1)S(1)}, u32[]{:S(2)}, u32[]{:S(2)}) collective-permute-start(bf16[4,80,1024]{2,1,0:T(8,128)(2,1)S(1)} %pad_maximum_fusion.refs_0_), channel_id=1, source_target_pairs={{0,1},{1,0},{2,3},{3,2},{4,5},{5,4},{6,7},{7,6},{8,9},{9,8},{10,11... | collective-permute-start | bytes 1966088 | tf_op jit(solution)/shard_map/ppermute | solution.py:62
  102.7 10.1 %collective-permute-start.11 = (bf16[4,80,1024]{2,1,0:T(8,128)(2,1)}, bf16[4,80,1024]{2,1,0:T(8,128)(2,1)S(1)}, u32[]{:S(2)}, u32[]{:S(2)}) collective-permute-start(bf16[4,80,1024]{2,1,0:T(8,128)(2,1)} %copy-done.5), channel_id=1, source_target_pairs={{0,1},{1,0},{2,3},{3,2},{4,5},{5,4},{6,7},{7,6},{8,9},{9,8},{10,11... | collective-permute-start | bytes 1966088 | tf_op jit(solution)/shard_map/ppermute | solution.py:62
  104.6 8.2 %collective-permute-start.9 = (bf16[4,80,1024]{2,1,0:T(8,128)(2,1)}, bf16[4,80,1024]{2,1,0:T(8,128)(2,1)S(1)}, u32[]{:S(2)}, u32[]{:S(2)}) collective-permute-start(bf16[4,80,1024]{2,1,0:T(8,128)(2,1)} %copy-done.6), channel_id=1, source_target_pairs={{0,1},{1,0},{2,3},{3,2},{4,5},{5,4},{6,7},{7,6},{8,9},{9,8},{10,11... | collective-permute-start | bytes 1966088 | tf_op jit(solution)/shard_map/ppermute | solution.py:62
  109.1 3.7 %copy-start.7 = (bf16[4,80,1024]{2,1,0:T(8,128)(2,1)}, bf16[4,80,1024]{2,1,0:T(8,128)(2,1)S(1)}, u32[]{:S(2)}) copy-start(bf16[4,80,1024]{2,1,0:T(8,128)(2,1)S(1)} %constant_dynamic-update-slice_fusion.refs_2_) | copy-start | bytes 1966084
  109.1 4.0 %collective-permute-start.10 = (bf16[4,80,1024]{2,1,0:T(8,128)(2,1)S(1)}, bf16[4,80,1024]{2,1,0:T(8,128)(2,1)S(1)}, u32[]{:S(2)}, u32[]{:S(2)}) collective-permute-start(bf16[4,80,1024]{2,1,0:T(8,128)(2,1)S(1)} %constant_dynamic-update-slice_fusion.refs_2_), channel_id=1, source_target_pairs={{0,1},{1,0},{2,3},{3,2},{4,5},{5,4},{6,7},{7,6},{8,9},{9,8},{10,11... | collective-permute-start | bytes 1966088 | tf_op jit(solution)/shard_map/ppermute | solution.py:62
  112.7 0.9 copy-start.8
  112.8 1.1 copy-start.9
  112.8 1.3 copy-start.10
  113.6 0.8 copy-start.11
  130.5 31.9 %copy-start.2 = (f32[160,2560]{1,0:T(8,128)S(1)}, f32[160,2560]{1,0:T(8,128)}, u32[]{:S(2)}) copy-start(f32[160,2560]{1,0:T(8,128)} %get-tuple-element.10) | copy-start | bytes 4915204
  161.7 2.0 copy-start.1
  166.9 22.4 %all-to-all-start.3 = ((bf16[32,72,128]{2,1,0:T(8,128)(2,1)}), bf16[32,72,128]{2,1,0:T(8,128)(2,1)S(1)}, u32[]{:S(2)}, u32[]{:S(2)}) async-start(bf16[32,72,128]{2,1,0:T(8,128)(2,1)} %pad_maximum_fusion.3), calls=%async_computation.3 | async-start | bytes 1179648 | tf_op jit(solution)/shard_map/all_to_all | solution.py:21
  204.4 18.0 %all-to-all-start.4 = ((bf16[16,40,128]{2,1,0:T(8,128)(2,1)}), bf16[16,40,128]{2,1,0:T(8,128)(2,1)S(1)}, u32[]{:S(2)}, u32[]{:S(2)}) async-start(bf16[16,40,128]{2,1,0:T(8,128)(2,1)} %broadcast_in_dim.29), calls=%async_computation.4 | async-start | bytes 327680 | tf_op jit(solution)/shard_map/all_to_all | solution.py:21
  223.2 16.9 %all-to-all-start.5 = ((bf16[32,40,128]{2,1,0:T(8,128)(2,1)}), bf16[32,40,128]{2,1,0:T(8,128)(2,1)S(1)}, u32[]{:S(2)}, u32[]{:S(2)}) async-start(bf16[32,40,128]{2,1,0:T(8,128)(2,1)} %broadcast_in_dim.30), calls=%async_computation.5 | async-start | bytes 655360 | tf_op jit(solution)/shard_map/all_to_all | solution.py:21
  240.9 1.5 copy-start.13
  241.2 2.2 copy-start.3
  242.5 2.2 copy-start.14

commit v4 on v3

v4 whole, which is shorter than its diff:
```python
import functools

import jax
import jax.numpy as jnp
from jax import lax
from jax.experimental import pallas as pl
from jax.experimental.pallas import tpu as pltpu
from jax.sharding import PartitionSpec as P


HIGH = lax.Precision.HIGHEST
F32 = jnp.float32
BF16 = jnp.bfloat16


def copies(array, count):
    return jnp.broadcast_to(array, (count, *array.shape))


def exchange(array, axis, groups=None):
    return lax.all_to_all(array, axis, 0, 0, tiled=True, axis_index_groups=groups)


def from_everyone(array, axis):
    return exchange(copies(array, lax.axis_size(axis)), axis)


def split_high_low(array):
    high = array.astype(BF16)
    return high, (array - high.astype(F32)).astype(BF16)


def side_by_side(query, output):
    half = query.shape[-2] // 2
    return jnp.concatenate(
        [query[..., :half, :], output[..., :half, :], query[..., half:, :], output[..., half:, :]],
        axis=-1,
    )


def in_plane(rows, cols, core):
    side = 4
    pairs = []
    for y in range(side):
        for x in range(side):
            for c in range(2):
                to = ((y + rows) % side * side + (x + cols) % side) * 2 + (c + core) % 2
                pairs.append(((y * side + x) * 2 + c, to))
    return pairs


def send(array, rows, cols, core=0):
    return lax.ppermute(array, "shard", in_plane(rows, cols, core))


def by_exchange(cotan):
    side = 4
    rows = [[(y * side + x) * 2 + c for x in range(side)] for y in range(side) for c in range(2)]
    cols = [[(y * side + x) * 2 + c for y in range(side)] for x in range(side) for c in range(2)]
    row = exchange(copies(cotan.T, side), "shard", rows)
    return exchange(copies(row, side), "shard", cols)


def by_rings(cotan):
    block = cotan.T
    below, above, across = send(block, 1, 0), send(block, 3, 0), send(block, 2, 0)
    column = jnp.stack([block, above, across, below])
    left, right = send(column, 0, 1), send(column, 0, 3)
    half = column.shape[0] // 2
    far_low, far_high = send(left[:half], 0, 1), send(right[half:], 0, 3)
    return column, right, far_low, far_high, left


def partner(array):
    return send(array, 0, 0, 1)


def gradient_kernel(factor, shard, *refs):
    acts_in, error_in, start_in, *sources = refs[:-11]
    full_out, left, acts, error, start, columns, full, given, near, done, sent = refs[-11:]
    in_rings = len(sources) > 2
    mine, theirs = sources[: len(sources) // 2], sources[len(sources) // 2 :]
    side, each = 4, columns.shape[1] // 8
    y0, x0, core = shard[0] // 8, shard[0] // 2 % side, shard[0] % 2

    def block(refs, j, k):
        if not in_rings:
            return refs[0].at[j, k]
        near, right, far_low, far_high, left = refs
        if k == 2:
            return (far_low if j < 2 else far_high).at[j % 2]
        return (near, right, None, left)[k].at[j]

    def fetch(j, k, other):
        x = (x0 + k) % side if in_rings else k
        at = (x * 2 + (1 - core if other else core)) * each
        return pltpu.make_async_copy(
            block(theirs if other else mine, j, k),
            columns.at[j, pl.ds(pl.multiple_of(at, 16), each), :],
            done.at[j, k * 2 + other],
        )

    def lanes(j):
        y = (y0 + j) % side if in_rings else j
        return pl.ds(pl.multiple_of(y * (8 * each), 128), 8 * each)

    def prior(j):
        return pltpu.make_async_copy(error_in.at[:, lanes(j)], error.at[j], near.at[j])

    def result(j):
        return pltpu.make_async_copy(full.at[j], full_out.at[:, lanes(j)], sent.at[j])

    first = pltpu.make_async_copy(acts_in, acts, given.at[0])
    second = pltpu.make_async_copy(start_in.at[factor], start, given.at[1])
    first.start()
    steps = [(k, other) for k in range(side) for other in range(2)]
    for j in range(side):
        for k, other in steps:
            fetch(j, k, other).start()
        prior(j).start()
        if j == 0:
            second.start()
    first.wait()
    total = jnp.zeros(left.shape, F32)
    for j in range(side):
        for k, other in steps:
            fetch(j, k, other).wait()
        prior(j).wait()
        if j == 0:
            second.wait()
        part = contract(acts[...], columns[j], (1, 1)) + error[j].astype(F32)
        full[j] = part
        result(j).start()
        high, low = split_high_low(part)
        rows = start[:, lanes(j)]
        total += contract(high, rows, (1, 1)) + contract(low, rows, (1, 1))
    left[...] = total
    for j in range(side):
        result(j).wait()


def full_gradient(inputs, error, factors, factor, mine, theirs, shard):
    rows, tokens = inputs.shape[::-1]
    width, rank = error.shape[-1], factors.shape[-1]
    anywhere = pl.BlockSpec(memory_space=pl.ANY)
    return pl.pallas_call(
        functools.partial(gradient_kernel, factor),
        out_shape=(
            jax.ShapeDtypeStruct((rows, width), F32),
            jax.ShapeDtypeStruct((rows, rank), F32),
        ),
        in_specs=[
            pl.BlockSpec(memory_space=pltpu.SMEM),
            *[anywhere] * (3 + len(mine) + len(theirs)),
        ],
        out_specs=(anywhere, pl.BlockSpec(memory_space=pltpu.VMEM)),
        scratch_shapes=[
            pltpu.VMEM((rows, tokens), BF16),
            pltpu.VMEM((4, rows, width // 4), BF16),
            pltpu.VMEM((rank, width), BF16),
            pltpu.VMEM((4, width // 4, tokens), BF16),
            pltpu.VMEM((4, rows, width // 4), F32),
            pltpu.SemaphoreType.DMA((2,)),
            pltpu.SemaphoreType.DMA((4,)),
            pltpu.SemaphoreType.DMA((4, 8)),
            pltpu.SemaphoreType.DMA((4,)),
        ],
    )(shard, inputs.T, error[0], jnp.swapaxes(factors, 1, 2), *mine, *theirs)


TILE = 16


def tile_of(group, block, blocks, per_shard):
    at = group * blocks + block
    return at // per_shard, at % per_shard * TILE


def term_kernel(scale, arrived, *refs):
    fulls_in, (sent, left_out, fulls, done) = refs[:-4], refs[-4:]
    copies_in = [pltpu.make_async_copy(a, fulls.at[i], done.at[i]) for i, a in enumerate(fulls_in)]
    for copy in copies_in:
        copy.start()
    total = arrived[0].astype(F32)
    for r in range(1, arrived.shape[0]):
        total += arrived[r].astype(F32)
    total = total * scale
    rank = total.shape[1] // 4
    lefts = [
        jnp.concatenate(
            [total[:, i * rank : (i + 1) * rank], total[:, (i + 2) * rank : (i + 3) * rank]], axis=0
        )
        for i in range(2)
    ]
    left_out[0] = lefts[0]
    left_out[1] = lefts[1]
    shards, depth = sent.shape[:2]
    share = depth - rank
    grams = []
    for left in lefts:
        gram = lax.dot_general(
            left, left, (((0,), (0,)), ((), ())), precision=HIGH, preferred_element_type=F32
        )
        grams.extend(split_high_low(gram))
    grams = jnp.concatenate(grams, axis=1)
    for s in range(shards):
        sent[s, share:, :] = grams
    blocks = fulls.shape[2] // 128
    per_shard = share // TILE
    for t in range(2 * rank // TILE * blocks, shards * per_shard):
        sent[t // per_shard, t % per_shard * TILE : (t % per_shard + 1) * TILE, :] = jnp.zeros(
            (TILE, 128), BF16
        )
    for i in range(2):
        copies_in[i].wait()
        high, low = split_high_low(lefts[i].T)
        both = jnp.concatenate([high, low], axis=0)
        for c in range(4):
            width = fulls.shape[2] // 4
            full_high, full_low = split_high_low(fulls[i, :, c * width : (c + 1) * width])
            product = contract(both, full_high, (1, 0))
            product = product[:rank] + product[rank:] + contract(high, full_low, (1, 0))
            product = product.astype(BF16)
            for g in range(rank // TILE):
                for b in range(width // 128):
                    s, at = tile_of(
                        i * (rank // TILE) + g, c * (width // 128) + b, blocks, per_shard
                    )
                    sent[s, at : at + TILE, :] = product[
                        g * TILE : (g + 1) * TILE, b * 128 : (b + 1) * 128
                    ]


def terms(arrived, query_full, output_full, replicas, shards):
    rows, width = query_full.shape
    rank = arrived.shape[-1] // 4
    tiles = 2 * rank // TILE * (width // 128)
    depth = -(-tiles // shards) * TILE + rank
    vmem = pl.BlockSpec(memory_space=pltpu.VMEM)
    anywhere = pl.BlockSpec(memory_space=pl.ANY)
    return pl.pallas_call(
        functools.partial(term_kernel, 1.0 / replicas),
        out_shape=(
            jax.ShapeDtypeStruct((shards, depth, 128), BF16),
            jax.ShapeDtypeStruct((2, rows, rank), F32),
        ),
        in_specs=[vmem, anywhere, anywhere],
        out_specs=(vmem, vmem),
        scratch_shapes=[
            pltpu.VMEM((2, rows, width), F32),
            pltpu.SemaphoreType.DMA((2,)),
        ],
    )(arrived, query_full, output_full)


def finish_kernel(replica, arrived, rows, query_weight, output_weight, *refs):
    fulls_in, errors_out = refs[:2], refs[2:4]
    weights_out, (fulls, cols, errors, done, sent) = refs[4:6], refs[6:]
    chunks = 4
    width = fulls.shape[2] // chunks
    here = [pl.ds(c * width, width) for c in range(chunks)]

    def prior(i, c):
        return pltpu.make_async_copy(
            fulls_in[i].at[:, here[c]], fulls.at[i, :, here[c]], done.at[i, c]
        )

    def result(i, c):
        return pltpu.make_async_copy(
            errors.at[i, :, here[c]], errors_out[i].at[0, :, here[c]], sent.at[i, c]
        )

    each = [(i, c) for i in range(2) for c in range(chunks)]
    for i, c in each:
        prior(i, c).start()
    blocks = fulls.shape[2] // 128
    groups = cols.shape[0] // TILE
    per_shard = arrived.shape[1] // TILE
    for g in range(groups):
        for b in range(blocks):
            s, at = tile_of(g, b, blocks, per_shard)
            cols[g * TILE : (g + 1) * TILE, b * 128 : (b + 1) * 128] = arrived[s, at : at + TILE, :]
    rank = cols.shape[0] // 2
    for i, c in each:
        right = cols[i * rank : (i + 1) * rank, here[c]]
        approx = contract(rows[i], jnp.concatenate([right, right], axis=0), (1, 0))
        prior(i, c).wait()
        errors[i, :, here[c]] = (fulls[i, :, here[c]] - approx).astype(BF16)
        result(i, c).start()
    span = query_weight.shape[1]
    window = 384
    at = replica[0] * span
    base = jnp.minimum(at // 128 * 128, fulls.shape[2] - window)
    own = cols[:, pl.ds(pl.multiple_of(base, 128), window)].astype(F32)
    own = pltpu.roll(own, window - (at - base), 1)[:, :span].astype(BF16)
    for i, weight in enumerate((query_weight, output_weight)):
        right = own[i * rank : (i + 1) * rank]
        approx = contract(rows[i], jnp.concatenate([right, right], axis=0), (1, 0))
        weights_out[i][...] = weight[...] - approx
    for i, c in each:
        result(i, c).wait()


def finish(arrived, rows, fulls, weights, replica):
    height, width = fulls[0].shape
    rank = rows.shape[-1] // 2
    vmem = pl.BlockSpec(memory_space=pltpu.VMEM)
    anywhere = pl.BlockSpec(memory_space=pl.ANY)
    return pl.pallas_call(
        finish_kernel,
        out_shape=(
            *[jax.ShapeDtypeStruct((1, height, width), BF16)] * 2,
            *[jax.ShapeDtypeStruct(weights[0].shape, F32)] * 2,
        ),
        in_specs=[
            pl.BlockSpec(memory_space=pltpu.SMEM),
            vmem,
            vmem,
            vmem,
            vmem,
            anywhere,
            anywhere,
        ],
        out_specs=(anywhere, anywhere, vmem, vmem),
        scratch_shapes=[
            pltpu.VMEM((2, height, width), F32),
            pltpu.VMEM((2 * rank, width), BF16),
            pltpu.VMEM((2, height, width), BF16),
            pltpu.SemaphoreType.DMA((2, 4)),
            pltpu.SemaphoreType.DMA((2, 4)),
        ],
    )(replica, arrived, rows, *weights, *fulls)


def contract(a, b, dims):
    return lax.dot_general(a, b, ((dims[:1], dims[1:]), ((), ())), preferred_element_type=F32)


def inverse_factor(gram):
    chol = jnp.linalg.cholesky(gram)
    eye = jnp.eye(gram.shape[0], dtype=F32)
    return lax.linalg.triangular_solve(chol, eye, left_side=True, lower=True)


def step(
    hidden_in,
    context_in,
    query_cotan,
    output_cotan,
    query_error,
    output_error,
    query_weight,
    output_weight,
    start_factors,
):
    replicas = lax.axis_size("dp")
    shards = lax.axis_size("shard")
    shard = lax.axis_index("shard").reshape(1)
    replica = lax.axis_index("dp").reshape(1)
    query_mine = (by_exchange(query_cotan),)
    output_mine = by_rings(output_cotan)
    column, right, far_low, far_high, left = output_mine
    column = partner(column)
    right, left = partner(right), partner(left)
    far_low, far_high = partner(far_low), partner(far_high)
    query_theirs = [partner(a) for a in query_mine]
    output_full, output_left = full_gradient(
        context_in,
        output_error,
        start_factors,
        1,
        output_mine,
        (column, right, far_low, far_high, left),
        shard,
    )
    query_full, query_left = full_gradient(
        hidden_in, query_error, start_factors, 0, query_mine, query_theirs, shard
    )

    lefts = from_everyone(side_by_side(query_left, output_left).astype(BF16), "dp")
    sent, lefts = terms(lefts, query_full, output_full, replicas, shards)
    rank = lefts.shape[-1]
    arrived = exchange(sent, "shard").astype(F32).sum(axis=0)
    share, gram_parts = arrived[:-rank], arrived[-rank:]

    shares = from_everyone(share.astype(BF16), "dp")
    share = shares.astype(F32).sum(axis=0) / F32(replicas)

    def weighted(left, gram):
        inverse = inverse_factor(gram)
        ortho = lax.dot_general(left, inverse, (((1,), (1,)), ((), ())), precision=HIGH)
        high, low = split_high_low(jnp.dot(ortho, inverse, precision=HIGH))
        return jnp.concatenate([high, low], axis=1)

    query_rows = weighted(lefts[0], gram_parts[:, :rank] + gram_parts[:, rank : 2 * rank])
    output_rows = weighted(lefts[1], gram_parts[:, 2 * rank : 3 * rank] + gram_parts[:, 3 * rank :])
    cols = from_everyone(share.astype(BF16), "shard")
    return finish(
        cols,
        jnp.stack([query_rows, output_rows]),
        (query_full, output_full),
        (query_weight, output_weight),
        replica,
    )


def solution(mesh):
    placed = (
        P("dp", "shard"),
        P("dp", "shard"),
        P("dp", "shard"),
        P("dp", "shard"),
        P("dp", "shard", None),
        P("dp", "shard", None),
        P("shard", "dp"),
        P("shard", "dp"),
        P(),
    )
    return jax.shard_map(
        step,
        mesh=mesh,
        in_specs=placed,
        out_specs=(
            P("dp", "shard", None),
            P("dp", "shard", None),
            P("shard", "dp"),
            P("shard", "dp"),
        ),
        check_vma=False,
    )
```

time: 247 us -> 247 us (level)
  Pallas kernels: 15.1 us -> 25.6 us
  matrix products: 8.3 us -> 1.42 us
  local copies, waits for them, and re-layouts: 12.8 us -> 7.41 us
  starting transfers between devices: 60.8 us -> 65.4 us
    pallas_call x2 -> x4, Pallas kernels: 15.1 us -> 25.6 us  [the longest x2 16.1 us: full_gradient(): pl.pallas_call(functools.partial(gradient_kernel, factor), out_shape=(jax...]
    dot_general x8 -> x0, matrix products: 6.95 us -> none  [the longest x4 4.41 us: contract(): lax.dot_general(a, b, ((dims[:1], dims[1:]), ((), ())), preferred_element...]
    ppermute x12 -> x13, starting transfers between devices: 37.5 us -> 41.4 us  [send(): return lax.ppermute(array, 'shard', in_plane(rows, cols, core))]
    ppermute x12 -> x13, waiting for transfers between devices: 18.1 us -> 16 us  [send(): return lax.ppermute(array, 'shard', in_plane(rows, cols, core))]
  transfers between devices with their start and end apart: 15 -> 16, of which waited for: 8 -> 8; matrix products, arithmetic and copies ran while one was open for 4% -> 2% of each run, Pallas kernels for 3% -> 3%
where the time goes in v4:
time: 247 us; the launch traced here: 246 us
  blocking collectives  78.8 us (32%)
  starting transfers between devices  65.4 us (26%)
  waiting for transfers between devices  49.6 us (20%)
  Pallas kernels  25.6 us (10%)
  other arithmetic  16.4 us (7%)
  local copies, waits for them, and re-layouts  7.41 us (3%)
    all_to_all x3, blocking collectives, exchange(): lax.all_to_all(array, axis, 0, 0, tiled=True, axis_index_groups=groups)  78.8 us
    ppermute x13, starting transfers between devices, send(): return lax.ppermute(array, 'shard', in_plane(rows, cols, core))  41.4 us
    all_to_all x3, waiting for transfers between devices, exchange(): lax.all_to_all(array, axis, 0, 0, tiled=True, axis_index_groups=groups)  33.7 us
    all_to_all x3, starting transfers between devices, exchange(): lax.all_to_all(array, axis, 0, 0, tiled=True, axis_index_groups=groups)  23.9 us
    pallas_call x2, Pallas kernels, full_gradient(): pl.pallas_call(functools.partial(gradient_kernel, factor), out_shape=(jax...  16.1 us
    ppermute x13, waiting for transfers between devices, send(): return lax.ppermute(array, 'shard', in_plane(rows, cols, core))  16 us
    another operation x6, other arithmetic, inverse_factor(): chol = jnp.linalg.cholesky(gram)  7.2 us
    another operation x4, other arithmetic, inverse_factor(): return lax.linalg.triangular_solve(chol, eye, left_side=True, lower=True)  6.17 us
  transfers between devices with their start and end apart: 16, of which 8 were waited for; matrix products, arithmetic and copies ran while one was open for 2% of the time, Pallas kernels for 3%

profile of v4, /device:TPU:1, one launch (start us, length us, event | category | flops | bytes accessed | tf_op | source)
XLA Modules:
  0.0 245.7 jit_solution(3326347889759850898)
XLA Ops:
  0.6 1.0 broadcast_in_dim.16
  1.6 12.3 %all_to_all.30 = bf16[4,80,1024]{2,1,0:T(8,128)(2,1)S(1)} all-to-all(bf16[4,80,1024]{2,1,0:T(8,128)(2,1)S(1)} %broadcast_in_dim.16), channel_id=1, replica_groups={{0,2,4,6},{1,3,5,7},{8,10,12,14},{9,11,13,15},{16,18,20,22},{17,19,21,2..., dimensions={0} | all-to-all | bytes 1310720 | tf_op jit(solution)/shard_map/all_to_all | solution.py:21
  14.2 36.2 %all_to_all.31.refs_3_ = bf16[4,4,80,1024]{3,2,1,0:T(8,128)(2,1)S(1)} all-to-all(bf16[4,4,80,1024]{3,2,1,0:T(8,128)(2,1)S(1)} %broadcast_in_dim.17), channel_id=1, replica_groups={{0,8,16,24},{1,9,17,25},{2,10,18,26},{3,11,19,27},{4,12,20,28},{5,13,21..., dimensions={0} | all-to-all | bytes 5242880 | tf_op jit(solution)/shard_map/all_to_all | solution.py:21
  50.4 5.1 %collective-permute-start = (bf16[4,4,80,1024]{3,2,1,0:T(8,128)(2,1)S(1)}, bf16[4,4,80,1024]{3,2,1,0:T(8,128)(2,1)}, u32[]{:S(2)}, u32[]{:S(2)}) collective-permute-start(bf16[4,4,80,1024]{3,2,1,0:T(8,128)(2,1)S(1)} %all_to_all.31.refs_3_), channel_id=1, source_target_pairs={{0,1},{1,0},{2,3},{3,2},{4,5},{5,4},{6,7},{7,6},{8,9},{9,8},{10,11... | collective-permute-start | bytes 7864328 | tf_op jit(solution)/shard_map/ppermute | solution.py:53
  55.6 2.4 collective-permute-start.2
  58.0 4.0 %collective-permute-start.1 = (bf16[80,1024]{1,0:T(8,128)(2,1)S(1)}, bf16[80,1024]{1,0:T(8,128)(2,1)S(1)}, u32[]{:S(2)}, u32[]{:S(2)}) collective-permute-start(bf16[80,1024]{1,0:T(8,128)(2,1)S(1)} %bitcast.55), channel_id=1, source_target_pairs={{0,24},{1,25},{2,26},{3,27},{4,28},{5,29},{6,30},{7,31},{8,0},{9,1... | collective-permute-start | bytes 491528 | tf_op jit(solution)/shard_map/ppermute | solution.py:53
  62.1 1.9 collective-permute-start.3
  64.0 0.7 collective-permute-done.2
  64.7 2.0 collective-permute-done.1
  66.7 3.6 %collective-permute-done.3 = bf16[80,1024]{1,0:T(8,128)(2,1)S(1)} collective-permute-done((bf16[80,1024]{1,0:T(8,128)(2,1)S(1)}, bf16[80,1024]{1,0:T(8,128)(2,1)S(1)}, u32[]{:S(2)}, u32[]{:S(2)}) %collective-permute-start.3) | collective-permute-done | bytes 163872 | tf_op jit(solution)/shard_map/ppermute | solution.py:53
  70.5 2.2 collective-permute-start.5
  72.7 4.3 %collective-permute-start.4 = (bf16[4,80,1024]{2,1,0:T(8,128)(2,1)S(1)}, bf16[4,80,1024]{2,1,0:T(8,128)(2,1)}, u32[]{:S(2)}, u32[]{:S(2)}) collective-permute-start(bf16[4,80,1024]{2,1,0:T(8,128)(2,1)S(1)} %pad_maximum_fusion.refs_3_), channel_id=1, source_target_pairs={{0,6},{1,7},{2,0},{3,1},{4,2},{5,3},{6,4},{7,5},{8,14},{9,15},{10,... | collective-permute-start | bytes 1966088 | tf_op jit(solution)/shard_map/ppermute | solution.py:53
  77.0 3.9 %collective-permute-start.8 = (bf16[4,80,1024]{2,1,0:T(8,128)(2,1)S(1)}, bf16[4,80,1024]{2,1,0:T(8,128)(2,1)S(1)}, u32[]{:S(2)}, u32[]{:S(2)}) collective-permute-start(bf16[4,80,1024]{2,1,0:T(8,128)(2,1)S(1)} %pad_maximum_fusion.refs_3_), channel_id=1, source_target_pairs={{0,1},{1,0},{2,3},{3,2},{4,5},{5,4},{6,7},{7,6},{8,9},{9,8},{10,11... | collective-permute-start | bytes 1966088 | tf_op jit(solution)/shard_map/ppermute | solution.py:53
  80.9 7.7 %collective-permute-done.5.refs_7_ = bf16[4,80,1024]{2,1,0:T(8,128)(2,1)} collective-permute-done((bf16[4,80,1024]{2,1,0:T(8,128)(2,1)S(1)}, bf16[4,80,1024]{2,1,0:T(8,128)(2,1)}, u32[]{:S(2)}, u32[]{:S(2)}) %collective-permute-start.5) | collective-permute-done | bytes 655392 | tf_op jit(solution)/shard_map/ppermute | solution.py:53
  88.5 1.0 slice.69
  89.5 1.9 collective-permute-start.6
  91.5 1.0 slice.70
  92.5 4.6 %collective-permute-start.7 = (bf16[2,80,1024]{2,1,0:T(8,128)(2,1)S(1)}, bf16[2,80,1024]{2,1,0:T(8,128)(2,1)}, u32[]{:S(2)}, u32[]{:S(2)}) collective-permute-start(bf16[2,80,1024]{2,1,0:T(8,128)(2,1)S(1)} %slice.70), channel_id=1, source_target_pairs={{0,6},{1,7},{2,0},{3,1},{4,2},{5,3},{6,4},{7,5},{8,14},{9,15},{10,... | collective-permute-start | bytes 983048 | tf_op jit(solution)/shard_map/ppermute | solution.py:53
  97.0 4.8 %collective-permute-start.12 = (bf16[4,80,1024]{2,1,0:T(8,128)(2,1)}, bf16[4,80,1024]{2,1,0:T(8,128)(2,1)}, u32[]{:S(2)}, u32[]{:S(2)}) collective-permute-start(bf16[4,80,1024]{2,1,0:T(8,128)(2,1)} %collective-permute-done.5.refs_7_), channel_id=1, source_target_pairs={{0,1},{1,0},{2,3},{3,2},{4,5},{5,4},{6,7},{7,6},{8,9},{9,8},{10,11... | collective-permute-start | bytes 1966088 | tf_op jit(solution)/shard_map/ppermute | solution.py:53
  101.8 0.8 copy-done.3
  102.7 1.9 collective-permute-start.9
  104.6 2.4 collective-permute-start.10
  107.0 1.9 collective-permute-start.11
  109.0 1.9 collective-permute-done.11.refs_11_
  110.9 8.1 %shard_map.121 = (f32[160,2560]{1,0:T(8,128)}, f32[160,32]{1,0:T(8,128)}) custom-call(s32[1]{0:T(128)} %bitcast.1.shard, bf16[160,1024]{1,0:T(8,128)(2,1)} %bitcast.52, bf16[160,2560]{1,0:T(8,128)(2,1)} %bitcast.50, bf16[2,32,2560]{2,1,0:T(8,128)(2,1)} %bitcast.48, bf16[4,80,1024]{2,1,0:T(8,128)(2,1)} %copy-done.1, ...), custom_call_target="tpu_custom_call" | custom-call | tf_op jit(solution)/shard_map/pallas_call | solution.py:146
  119.0 0.9 convert.16
  119.9 8.1 %shard_map.120 = (f32[160,2560]{1,0:T(8,128)}, f32[160,32]{1,0:T(8,128)}) custom-call(s32[1]{0:T(128)} %bitcast.1.shard, bf16[160,1024]{1,0:T(8,128)(2,1)} %bitcast.53, bf16[160,2560]{1,0:T(8,128)(2,1)} %bitcast.51, bf16[2,32,2560]{2,1,0:T(8,128)(2,1)} %bitcast.49, bf16[4,4,80,1024]{3,2,1,0:T(8,128)(2,1)} %copy-done, ...), custom_call_target="tpu_custom_call" | custom-call | tf_op jit(solution)/shard_map/pallas_call | solution.py:146
  127.9 0.9 convert.15
  129.0 30.4 %all_to_all.32.arrived = bf16[16,80,128]{2,1,0:T(8,128)(2,1)} all-to-all(bf16[16,80,128]{2,1,0:T(8,128)(2,1)S(1)} %broadcast_in_dim.18), channel_id=1, replica_groups=mesh['dp'=16,'shard'=32] {'dp'}, dimensions={0} | all-to-all | bytes 655360 | tf_op jit(solution)/shard_map/all_to_all | solution.py:21
  159.4 4.2 %shard_map.122 = (bf16[32,80,128]{2,1,0:T(8,128)(2,1)}, f32[2,160,32]{2,1,0:T(8,128)}) custom-call(bf16[16,80,128]{2,1,0:T(8,128)(2,1)} %all_to_all.32.arrived, f32[160,2560]{1,0:T(8,128)} %get-tuple-element.14.refs_0_, f32[160,2560]{1,0:T(8,128)} %get-tuple-element.15.refs_1_), custom_call_target="tpu_custom_call" | custom-call | tf_op jit(solution)/shard_map/pallas_call | solution.py:241
  163.6 10.2 %all-to-all-start.3 = ((bf16[32,80,128]{2,1,0:T(8,128)(2,1)}), bf16[32,80,128]{2,1,0:T(8,128)(2,1)S(1)}, u32[]{:S(2)}, u32[]{:S(2)}) async-start(bf16[32,80,128]{2,1,0:T(8,128)(2,1)} %get-tuple-element.16), calls=%async_computation.3 | async-start | bytes 1310720 | tf_op jit(solution)/shard_map/all_to_all | solution.py:21
  173.8 12.9 %all-to-all-done.3 = bf16[32,80,128]{2,1,0:T(8,128)(2,1)S(1)} async-done(((bf16[32,80,128]{2,1,0:T(8,128)(2,1)}), bf16[32,80,128]{2,1,0:T(8,128)(2,1)S(1)}, u32[]{:S(2)}, u32[]{:S(2)}) %all-to-all-start.3) | async-done | bytes 655392 | tf_op jit(solution)/shard_map/all_to_all | solution.py:21
  187.2 2.9 %cholesky.44 = f32[32,32]{1,0:T(8,128)S(1)} custom-call(f32[32,32]{1,0:T(8,128)S(1)} %fusion.15), custom_call_target="Cholesky" | custom-call | tf_op jit(solution)/shard_map/jit(cholesky)/cholesky | solution.py:340
  190.2 0.6 compare_reduce_fusion.1
  190.8 0.7 fusion.10
  191.5 2.4 custom-call.6
  194.1 2.9 %cholesky.55 = f32[32,32]{1,0:T(8,128)S(1)} custom-call(f32[32,32]{1,0:T(8,128)S(1)} %fusion.13), custom_call_target="Cholesky" | custom-call | tf_op jit(solution)/shard_map/jit(cholesky)/cholesky | solution.py:340
  197.7 0.7 fusion.11
  198.4 2.4 custom-call.7
  201.6 0.7 broadcast_in_dim.19
  202.3 5.6 %all-to-all-start.4 = ((bf16[16,48,128]{2,1,0:T(8,128)(2,1)}), bf16[16,48,128]{2,1,0:T(8,128)(2,1)S(1)}, u32[]{:S(2)}, u32[]{:S(2)}) async-start(bf16[16,48,128]{2,1,0:T(8,128)(2,1)} %broadcast_in_dim.19), calls=%async_computation.4 | async-start | bytes 393216 | tf_op jit(solution)/shard_map/all_to_all | solution.py:21
  209.0 11.3 %all-to-all-done.4 = bf16[16,48,128]{2,1,0:T(8,128)(2,1)S(1)} async-done(((bf16[16,48,128]{2,1,0:T(8,128)(2,1)}), bf16[16,48,128]{2,1,0:T(8,128)(2,1)S(1)}, u32[]{:S(2)}, u32[]{:S(2)}) %all-to-all-start.4) | async-done | bytes 196640 | tf_op jit(solution)/shard_map/all_to_all | solution.py:21
  220.4 0.8 broadcast_in_dim.20
  221.2 8.2 %all-to-all-start.5 = ((bf16[32,48,128]{2,1,0:T(8,128)(2,1)}), bf16[32,48,128]{2,1,0:T(8,128)(2,1)S(1)}, u32[]{:S(2)}, u32[]{:S(2)}) async-start(bf16[32,48,128]{2,1,0:T(8,128)(2,1)} %broadcast_in_dim.20), calls=%async_computation.5 | async-start | bytes 786432 | tf_op jit(solution)/shard_map/all_to_all | solution.py:21
  229.6 0.6 pad_maximum_fusion.1.rows
  230.2 9.4 %all-to-all-done.5.arrived = bf16[32,48,128]{2,1,0:T(8,128)(2,1)S(1)} async-done(((bf16[32,48,128]{2,1,0:T(8,128)(2,1)}), bf16[32,48,128]{2,1,0:T(8,128)(2,1)S(1)}, u32[]{:S(2)}, u32[]{:S(2)}) %all-to-all-start.5) | async-done | bytes 393248 | tf_op jit(solution)/shard_map/all_to_all | solution.py:21
  239.6 0.7 copy-done.2
  240.3 5.3 %shard_map.123 = (bf16[1,160,2560]{2,1,0:T(8,128)(2,1)}, bf16[1,160,2560]{2,1,0:T(8,128)(2,1)}, f32[160,160]{1,0:T(8,128)}, f32[160,160]{1,0:T(8,128)}) custom-call(s32[1]{0:T(128)} %bitcast.replica, bf16[32,48,128]{2,1,0:T(8,128)(2,1)} %copy-done.2, bf16[2,160,64]{2,1,0:T(8,128)(2,1)} %pad_maximum_fusion.1.rows, f32[160,160]{1,0:T(8,128)} %query_weight.1, ...), custom_call_target="tpu_custom_call" | custom-call | tf_op jit(solution)/shard_map/pallas_call | solution.py:309
  (55 shorter events, 4.1 us)
Async XLA Ops:
  14.2 41.3 %copy-start.4 = (bf16[1024,80]{0,1:T(8,128)(2,1)S(1)}, bf16[1024,80]{0,1:T(8,128)(2,1)}, u32[]{:S(2)}) copy-start(bf16[1024,80]{0,1:T(8,128)(2,1)} %param.15) | copy-start | bytes 491524
  50.4 68.6 %copy-start = (bf16[4,4,80,1024]{3,2,1,0:T(8,128)(2,1)}, bf16[4,4,80,1024]{3,2,1,0:T(8,128)(2,1)S(1)}, u32[]{:S(2)}) copy-start(bf16[4,4,80,1024]{3,2,1,0:T(8,128)(2,1)S(1)} %all_to_all.31.refs_3_) | copy-start | bytes 7864324
  50.4 69.5 %collective-permute-start = (bf16[4,4,80,1024]{3,2,1,0:T(8,128)(2,1)S(1)}, bf16[4,4,80,1024]{3,2,1,0:T(8,128)(2,1)}, u32[]{:S(2)}, u32[]{:S(2)}) collective-permute-start(bf16[4,4,80,1024]{3,2,1,0:T(8,128)(2,1)S(1)} %all_to_all.31.refs_3_), channel_id=1, source_target_pairs={{0,1},{1,0},{2,3},{3,2},{4,5},{5,4},{6,7},{7,6},{8,9},{9,8},{10,11... | collective-permute-start | bytes 7864328 | tf_op jit(solution)/shard_map/ppermute | solution.py:53
  55.6 9.1 %collective-permute-start.2 = (bf16[80,1024]{1,0:T(8,128)(2,1)S(1)}, bf16[80,1024]{1,0:T(8,128)(2,1)S(1)}, u32[]{:S(2)}, u32[]{:S(2)}) collective-permute-start(bf16[80,1024]{1,0:T(8,128)(2,1)S(1)} %bitcast.54), channel_id=1, source_target_pairs={{0,16},{1,17},{2,18},{3,19},{4,20},{5,21},{6,22},{7,23},{8,24},{9,... | collective-permute-start | bytes 491528 | tf_op jit(solution)/shard_map/ppermute | solution.py:53
  58.0 8.7 %collective-permute-start.1 = (bf16[80,1024]{1,0:T(8,128)(2,1)S(1)}, bf16[80,1024]{1,0:T(8,128)(2,1)S(1)}, u32[]{:S(2)}, u32[]{:S(2)}) collective-permute-start(bf16[80,1024]{1,0:T(8,128)(2,1)S(1)} %bitcast.55), channel_id=1, source_target_pairs={{0,24},{1,25},{2,26},{3,27},{4,28},{5,29},{6,30},{7,31},{8,0},{9,1... | collective-permute-start | bytes 491528 | tf_op jit(solution)/shard_map/ppermute | solution.py:53
  62.1 8.3 %collective-permute-start.3 = (bf16[80,1024]{1,0:T(8,128)(2,1)S(1)}, bf16[80,1024]{1,0:T(8,128)(2,1)S(1)}, u32[]{:S(2)}, u32[]{:S(2)}) collective-permute-start(bf16[80,1024]{1,0:T(8,128)(2,1)S(1)} %bitcast.56), channel_id=1, source_target_pairs={{0,8},{1,9},{2,10},{3,11},{4,12},{5,13},{6,14},{7,15},{8,16},{9,17... | collective-permute-start | bytes 491528 | tf_op jit(solution)/shard_map/ppermute | solution.py:53
  70.4 40.4 %copy-start.1 = (bf16[4,80,1024]{2,1,0:T(8,128)(2,1)}, bf16[4,80,1024]{2,1,0:T(8,128)(2,1)S(1)}, u32[]{:S(2)}) copy-start(bf16[4,80,1024]{2,1,0:T(8,128)(2,1)S(1)} %pad_maximum_fusion.refs_3_) | copy-start | bytes 1966084
  70.5 18.1 %collective-permute-start.5 = (bf16[4,80,1024]{2,1,0:T(8,128)(2,1)S(1)}, bf16[4,80,1024]{2,1,0:T(8,128)(2,1)}, u32[]{:S(2)}, u32[]{:S(2)}) collective-permute-start(bf16[4,80,1024]{2,1,0:T(8,128)(2,1)S(1)} %pad_maximum_fusion.refs_3_), channel_id=1, source_target_pairs={{0,2},{1,3},{2,4},{3,5},{4,6},{5,7},{6,0},{7,1},{8,10},{9,11},{10,... | collective-permute-start | bytes 1966088 | tf_op jit(solution)/shard_map/ppermute | solution.py:53
  72.7 18.8 %collective-permute-start.4 = (bf16[4,80,1024]{2,1,0:T(8,128)(2,1)S(1)}, bf16[4,80,1024]{2,1,0:T(8,128)(2,1)}, u32[]{:S(2)}, u32[]{:S(2)}) collective-permute-start(bf16[4,80,1024]{2,1,0:T(8,128)(2,1)S(1)} %pad_maximum_fusion.refs_3_), channel_id=1, source_target_pairs={{0,6},{1,7},{2,0},{3,1},{4,2},{5,3},{6,4},{7,5},{8,14},{9,15},{10,... | collective-permute-start | bytes 1966088 | tf_op jit(solution)/shard_map/ppermute | solution.py:53
  77.0 24.8 %collective-permute-start.8 = (bf16[4,80,1024]{2,1,0:T(8,128)(2,1)S(1)}, bf16[4,80,1024]{2,1,0:T(8,128)(2,1)S(1)}, u32[]{:S(2)}, u32[]{:S(2)}) collective-permute-start(bf16[4,80,1024]{2,1,0:T(8,128)(2,1)S(1)} %pad_maximum_fusion.refs_3_), channel_id=1, source_target_pairs={{0,1},{1,0},{2,3},{3,2},{4,5},{5,4},{6,7},{7,6},{8,9},{9,8},{10,11... | collective-permute-start | bytes 1966088 | tf_op jit(solution)/shard_map/ppermute | solution.py:53
  89.5 15.1 %collective-permute-start.6 = (bf16[2,80,1024]{2,1,0:T(8,128)(2,1)S(1)}, bf16[2,80,1024]{2,1,0:T(8,128)(2,1)}, u32[]{:S(2)}, u32[]{:S(2)}) collective-permute-start(bf16[2,80,1024]{2,1,0:T(8,128)(2,1)S(1)} %slice.69), channel_id=1, source_target_pairs={{0,2},{1,3},{2,4},{3,5},{4,6},{5,7},{6,0},{7,1},{8,10},{9,11},{10,... | collective-permute-start | bytes 983048 | tf_op jit(solution)/shard_map/ppermute | solution.py:53
  92.5 14.5 %collective-permute-start.7 = (bf16[2,80,1024]{2,1,0:T(8,128)(2,1)S(1)}, bf16[2,80,1024]{2,1,0:T(8,128)(2,1)}, u32[]{:S(2)}, u32[]{:S(2)}) collective-permute-start(bf16[2,80,1024]{2,1,0:T(8,128)(2,1)S(1)} %slice.70), channel_id=1, source_target_pairs={{0,6},{1,7},{2,0},{3,1},{4,2},{5,3},{6,4},{7,5},{8,14},{9,15},{10,... | collective-permute-start | bytes 983048 | tf_op jit(solution)/shard_map/ppermute | solution.py:53
  97.0 13.8 %collective-permute-start.12 = (bf16[4,80,1024]{2,1,0:T(8,128)(2,1)}, bf16[4,80,1024]{2,1,0:T(8,128)(2,1)}, u32[]{:S(2)}, u32[]{:S(2)}) collective-permute-start(bf16[4,80,1024]{2,1,0:T(8,128)(2,1)} %collective-permute-done.5.refs_7_), channel_id=1, source_target_pairs={{0,1},{1,0},{2,3},{3,2},{4,5},{5,4},{6,7},{7,6},{8,9},{9,8},{10,11... | collective-permute-start | bytes 1966088 | tf_op jit(solution)/shard_map/ppermute | solution.py:53
  101.8 0.8 copy-start.3
  102.7 8.2 %collective-permute-start.9 = (bf16[4,80,1024]{2,1,0:T(8,128)(2,1)}, bf16[4,80,1024]{2,1,0:T(8,128)(2,1)}, u32[]{:S(2)}, u32[]{:S(2)}) collective-permute-start(bf16[4,80,1024]{2,1,0:T(8,128)(2,1)} %collective-permute-done.4.refs_4_), channel_id=1, source_target_pairs={{0,1},{1,0},{2,3},{3,2},{4,5},{5,4},{6,7},{7,6},{8,9},{9,8},{10,11... | collective-permute-start | bytes 1966088 | tf_op jit(solution)/shard_map/ppermute | solution.py:53
  104.6 4.4 %collective-permute-start.10 = (bf16[2,80,1024]{2,1,0:T(8,128)(2,1)}, bf16[2,80,1024]{2,1,0:T(8,128)(2,1)}, u32[]{:S(2)}, u32[]{:S(2)}) collective-permute-start(bf16[2,80,1024]{2,1,0:T(8,128)(2,1)} %collective-permute-done.6.refs_5_), channel_id=1, source_target_pairs={{0,1},{1,0},{2,3},{3,2},{4,5},{5,4},{6,7},{7,6},{8,9},{9,8},{10,11... | collective-permute-start | bytes 983048 | tf_op jit(solution)/shard_map/ppermute | solution.py:53
  107.0 3.9 %collective-permute-start.11 = (bf16[2,80,1024]{2,1,0:T(8,128)(2,1)}, bf16[2,80,1024]{2,1,0:T(8,128)(2,1)}, u32[]{:S(2)}, u32[]{:S(2)}) collective-permute-start(bf16[2,80,1024]{2,1,0:T(8,128)(2,1)} %collective-permute-done.7.refs_6_), channel_id=1, source_target_pairs={{0,1},{1,0},{2,3},{3,2},{4,5},{5,4},{6,7},{7,6},{8,9},{9,8},{10,11... | collective-permute-start | bytes 983048 | tf_op jit(solution)/shard_map/ppermute | solution.py:53
  163.6 37.5 %copy-start.5 = (f32[2,160,32]{2,1,0:T(8,128)S(1)}, f32[2,160,32]{2,1,0:T(8,128)}, u32[]{:S(2)}) copy-start(f32[2,160,32]{2,1,0:T(8,128)} %get-tuple-element.17) | copy-start | bytes 122884
  163.6 23.2 %all-to-all-start.3 = ((bf16[32,80,128]{2,1,0:T(8,128)(2,1)}), bf16[32,80,128]{2,1,0:T(8,128)(2,1)S(1)}, u32[]{:S(2)}, u32[]{:S(2)}) async-start(bf16[32,80,128]{2,1,0:T(8,128)(2,1)} %get-tuple-element.16), calls=%async_computation.3 | async-start | bytes 1310720 | tf_op jit(solution)/shard_map/all_to_all | solution.py:21
  202.3 18.0 %all-to-all-start.4 = ((bf16[16,48,128]{2,1,0:T(8,128)(2,1)}), bf16[16,48,128]{2,1,0:T(8,128)(2,1)S(1)}, u32[]{:S(2)}, u32[]{:S(2)}) async-start(bf16[16,48,128]{2,1,0:T(8,128)(2,1)} %broadcast_in_dim.19), calls=%async_computation.4 | async-start | bytes 393216 | tf_op jit(solution)/shard_map/all_to_all | solution.py:21
  221.2 18.4 %all-to-all-start.5 = ((bf16[32,48,128]{2,1,0:T(8,128)(2,1)}), bf16[32,48,128]{2,1,0:T(8,128)(2,1)S(1)}, u32[]{:S(2)}, u32[]{:S(2)}) async-start(bf16[32,48,128]{2,1,0:T(8,128)(2,1)} %broadcast_in_dim.20), calls=%async_computation.5 | async-start | bytes 786432 | tf_op jit(solution)/shard_map/all_to_all | solution.py:21
  239.6 0.7 copy-start.2

commit v5 on v4

--- a/solution.py
+++ b/solution.py
@@ -28,14 +28,6 @@
 def split_high_low(array):
     high = array.astype(BF16)
     return high, (array - high.astype(F32)).astype(BF16)
-
-
-def side_by_side(query, output):
-    half = query.shape[-2] // 2
-    return jnp.concatenate(
-        [query[..., :half, :], output[..., :half, :], query[..., half:, :], output[..., half:, :]],
-        axis=-1,
-    )
 
 
 def in_plane(rows, cols, core):
@@ -76,9 +68,10 @@
 
 
 def gradient_kernel(factor, shard, *refs):
-    acts_in, error_in, start_in, *sources = refs[:-11]
-    full_out, left, acts, error, start, columns, full, given, near, done, sent = refs[-11:]
-    in_rings = len(sources) > 2
+    acts_in, error_in, start_in, *sources = refs[:-9]
+    full, left, acts, error, start, columns, given, near, done = refs[-9:]
+    in_rings = len(sources) > 3
+    other_left = None if in_rings else sources.pop()
     mine, theirs = sources[: len(sources) // 2], sources[len(sources) // 2 :]
     side, each = 4, columns.shape[1] // 8
     y0, x0, core = shard[0] // 8, shard[0] // 2 % side, shard[0] % 2
@@ -106,9 +99,6 @@
 
     def prior(j):
         return pltpu.make_async_copy(error_in.at[:, lanes(j)], error.at[j], near.at[j])
-
-    def result(j):
-        return pltpu.make_async_copy(full.at[j], full_out.at[:, lanes(j)], sent.at[j])
 
     first = pltpu.make_async_copy(acts_in, acts, given.at[0])
     second = pltpu.make_async_copy(start_in.at[factor], start, given.at[1])
@@ -121,7 +111,7 @@
         if j == 0:
             second.start()
     first.wait()
-    total = jnp.zeros(left.shape, F32)
+    total = jnp.zeros((acts.shape[0], start.shape[0]), F32)
     for j in range(side):
         for k, other in steps:
             fetch(j, k, other).wait()
@@ -129,43 +119,54 @@
         if j == 0:
             second.wait()
         part = contract(acts[...], columns[j], (1, 1)) + error[j].astype(F32)
-        full[j] = part
-        result(j).start()
+        full[:, lanes(j)] = part
         high, low = split_high_low(part)
         rows = start[:, lanes(j)]
         total += contract(high, rows, (1, 1)) + contract(low, rows, (1, 1))
-    left[...] = total
-    for j in range(side):
-        result(j).wait()
-
-
-def full_gradient(inputs, error, factors, factor, mine, theirs, shard):
+    if in_rings:
+        left[...] = total
+    else:
+        half = total.shape[0] // 2
+        packed = jnp.concatenate(
+            [total[:half], other_left[:half], total[half:], other_left[half:]], axis=1
+        ).astype(BF16)
+        for r in range(left.shape[0]):
+            left[r] = packed
+
+
+def in_vmem(*arrays):
+    return [pltpu.with_memory_space_constraint(a, pltpu.VMEM) for a in arrays]
+
+
+def in_hbm(*arrays):
+    return [pltpu.with_memory_space_constraint(a, pltpu.HBM) for a in arrays]
+
+
+def full_gradient(inputs, error, factors, factor, blocks, shard, left, *lefts):
     rows, tokens = inputs.shape[::-1]
-    width, rank = error.shape[-1], factors.shape[-1]
-    anywhere = pl.BlockSpec(memory_space=pl.ANY)
+    width = error.shape[-1]
+    vmem = pl.BlockSpec(memory_space=pltpu.VMEM)
     return pl.pallas_call(
         functools.partial(gradient_kernel, factor),
-        out_shape=(
-            jax.ShapeDtypeStruct((rows, width), F32),
-            jax.ShapeDtypeStruct((rows, rank), F32),
-        ),
+        out_shape=(pltpu.VMEM((rows, width), F32), left),
         in_specs=[
             pl.BlockSpec(memory_space=pltpu.SMEM),
-            *[anywhere] * (3 + len(mine) + len(theirs)),
+            *[pl.BlockSpec(memory_space=pltpu.HBM)] * 3,
+            *[pl.BlockSpec(memory_space=pltpu.HBM)] * len(blocks),
+            *[vmem] * len(lefts),
         ],
-        out_specs=(anywhere, pl.BlockSpec(memory_space=pltpu.VMEM)),
+        out_specs=(vmem, vmem),
         scratch_shapes=[
             pltpu.VMEM((rows, tokens), BF16),
             pltpu.VMEM((4, rows, width // 4), BF16),
-            pltpu.VMEM((rank, width), BF16),
+            pltpu.VMEM((factors.shape[-1], width), BF16),
             pltpu.VMEM((4, width // 4, tokens), BF16),
-            pltpu.VMEM((4, rows, width // 4), F32),
             pltpu.SemaphoreType.DMA((2,)),
             pltpu.SemaphoreType.DMA((4,)),
             pltpu.SemaphoreType.DMA((4, 8)),
-            pltpu.SemaphoreType.DMA((4,)),
         ],
-    )(shard, inputs.T, error[0], jnp.swapaxes(factors, 1, 2), *mine, *theirs)
+        compiler_params=pltpu.CompilerParams(vmem_limit_bytes=20 << 20),
+    )(shard, *in_hbm(inputs.T, error[0], jnp.swapaxes(factors, 1, 2), *blocks), *in_vmem(*lefts))
 
 
 TILE = 16
@@ -177,10 +178,7 @@
 
 
 def term_kernel(scale, arrived, *refs):
-    fulls_in, (sent, left_out, fulls, done) = refs[:-4], refs[-4:]
-    copies_in = [pltpu.make_async_copy(a, fulls.at[i], done.at[i]) for i, a in enumerate(fulls_in)]
-    for copy in copies_in:
-        copy.start()
+    *fulls, sent, left_out = refs
     total = arrived[0].astype(F32)
     for r in range(1, arrived.shape[0]):
         total += arrived[r].astype(F32)
@@ -205,19 +203,19 @@
     grams = jnp.concatenate(grams, axis=1)
     for s in range(shards):
         sent[s, share:, :] = grams
-    blocks = fulls.shape[2] // 128
+    full_width = fulls[0].shape[1]
+    blocks = full_width // 128
     per_shard = share // TILE
     for t in range(2 * rank // TILE * blocks, shards * per_shard):
         sent[t // per_shard, t % per_shard * TILE : (t % per_shard + 1) * TILE, :] = jnp.zeros(
             (TILE, 128), BF16
         )
     for i in range(2):
-        copies_in[i].wait()
         high, low = split_high_low(lefts[i].T)
         both = jnp.concatenate([high, low], axis=0)
         for c in range(4):
-            width = fulls.shape[2] // 4
-            full_high, full_low = split_high_low(fulls[i, :, c * width : (c + 1) * width])
+            width = full_width // 4
+            full_high, full_low = split_high_low(fulls[i][:, c * width : (c + 1) * width])
             product = contract(both, full_high, (1, 0))
             product = product[:rank] + product[rank:] + contract(high, full_low, (1, 0))
             product = product.astype(BF16)
@@ -237,33 +235,25 @@
     tiles = 2 * rank // TILE * (width // 128)
     depth = -(-tiles // shards) * TILE + rank
     vmem = pl.BlockSpec(memory_space=pltpu.VMEM)
-    anywhere = pl.BlockSpec(memory_space=pl.ANY)
     return pl.pallas_call(
         functools.partial(term_kernel, 1.0 / replicas),
         out_shape=(
             jax.ShapeDtypeStruct((shards, depth, 128), BF16),
             jax.ShapeDtypeStruct((2, rows, rank), F32),
         ),
-        in_specs=[vmem, anywhere, anywhere],
+        in_specs=[vmem] * 3,
         out_specs=(vmem, vmem),
-        scratch_shapes=[
-            pltpu.VMEM((2, rows, width), F32),
-            pltpu.SemaphoreType.DMA((2,)),
-        ],
-    )(arrived, query_full, output_full)
+        compiler_params=pltpu.CompilerParams(vmem_limit_bytes=16 << 20),
+    )(*in_vmem(arrived, query_full, output_full))
 
 
 def finish_kernel(replica, arrived, rows, query_weight, output_weight, *refs):
-    fulls_in, errors_out = refs[:2], refs[2:4]
-    weights_out, (fulls, cols, errors, done, sent) = refs[4:6], refs[6:]
+    fulls, errors_out = refs[:2], refs[2:4]
+    weights_out, (cols, errors, sent) = refs[4:6], refs[6:]
     chunks = 4
-    width = fulls.shape[2] // chunks
+    full_width = cols.shape[1]
+    width = full_width // chunks
     here = [pl.ds(c * width, width) for c in range(chunks)]
-
-    def prior(i, c):
-        return pltpu.make_async_copy(
-            fulls_in[i].at[:, here[c]], fulls.at[i, :, here[c]], done.at[i, c]
-        )
 
     def result(i, c):
         return pltpu.make_async_copy(
@@ -271,9 +261,7 @@
         )
 
     each = [(i, c) for i in range(2) for c in range(chunks)]
-    for i, c in each:
-        prior(i, c).start()
-    blocks = fulls.shape[2] // 128
+    blocks = full_width // 128
     groups = cols.shape[0] // TILE
     per_shard = arrived.shape[1] // TILE
     for g in range(groups):
@@ -284,13 +272,12 @@
     for i, c in each:
         right = cols[i * rank : (i + 1) * rank, here[c]]
         approx = contract(rows[i], jnp.concatenate([right, right], axis=0), (1, 0))
-        prior(i, c).wait()
-        errors[i, :, here[c]] = (fulls[i, :, here[c]] - approx).astype(BF16)
+        errors[i, :, here[c]] = (fulls[i][:, here[c]] - approx).astype(BF16)
         result(i, c).start()
     span = query_weight.shape[1]
     window = 384
     at = replica[0] * span
-    base = jnp.minimum(at // 128 * 128, fulls.shape[2] - window)
+    base = jnp.minimum(at // 128 * 128, full_width - window)
     own = cols[:, pl.ds(pl.multiple_of(base, 128), window)].astype(F32)
     own = pltpu.roll(own, window - (at - base), 1)[:, :span].astype(BF16)
     for i, weight in enumerate((query_weight, output_weight)):
@@ -312,24 +299,15 @@
             *[jax.ShapeDtypeStruct((1, height, width), BF16)] * 2,
             *[jax.ShapeDtypeStruct(weights[0].shape, F32)] * 2,
         ),
-        in_specs=[
-            pl.BlockSpec(memory_space=pltpu.SMEM),
-            vmem,
-            vmem,
-            vmem,
-            vmem,
-            anywhere,
-            anywhere,
-        ],
+        in_specs=[pl.BlockSpec(memory_space=pltpu.SMEM), *[vmem] * 6],
         out_specs=(anywhere, anywhere, vmem, vmem),
         scratch_shapes=[
-            pltpu.VMEM((2, height, width), F32),
             pltpu.VMEM((2 * rank, width), BF16),
             pltpu.VMEM((2, height, width), BF16),
             pltpu.SemaphoreType.DMA((2, 4)),
-            pltpu.SemaphoreType.DMA((2, 4)),
         ],
-    )(replica, arrived, rows, *weights, *fulls)
+        compiler_params=pltpu.CompilerParams(vmem_limit_bytes=16 << 20),
+    )(replica, *in_vmem(arrived), rows, *weights, *in_vmem(*fulls))
 
 
 def contract(a, b, dims):
@@ -364,22 +342,28 @@
     right, left = partner(right), partner(left)
     far_low, far_high = partner(far_low), partner(far_high)
     query_theirs = [partner(a) for a in query_mine]
+    rows, rank = output_error.shape[1], start_factors.shape[-1]
     output_full, output_left = full_gradient(
         context_in,
         output_error,
         start_factors,
         1,
-        output_mine,
-        (column, right, far_low, far_high, left),
+        (*output_mine, column, right, far_low, far_high, left),
         shard,
+        pltpu.VMEM((rows, rank), F32),
     )
-    query_full, query_left = full_gradient(
-        hidden_in, query_error, start_factors, 0, query_mine, query_theirs, shard
+    query_full, lefts = full_gradient(
+        hidden_in,
+        query_error,
+        start_factors,
+        0,
+        (*query_mine, *query_theirs),
+        shard,
+        pltpu.VMEM((replicas, rows // 2, 4 * rank), BF16),
+        output_left,
     )
 
-    lefts = from_everyone(side_by_side(query_left, output_left).astype(BF16), "dp")
-    sent, lefts = terms(lefts, query_full, output_full, replicas, shards)
-    rank = lefts.shape[-1]
+    sent, lefts = terms(exchange(lefts, "dp"), query_full, output_full, replicas, shards)
     arrived = exchange(sent, "shard").astype(F32).sum(axis=0)
     share, gram_parts = arrived[:-rank], arrived[-rank:]
 

time: 247 us -> 243 us (0.984)
  Pallas kernels: 25.6 us -> 17.8 us
  waiting for transfers between devices: 49.6 us -> 42.1 us
  local copies, waits for them, and re-layouts: 7.41 us -> 11 us
  other arithmetic: 16.4 us -> 19.6 us
  matrix products: 1.42 us -> 4.54 us
    all_to_all x3, waiting for transfers between devices: 33.7 us -> 26.4 us  [exchange(): lax.all_to_all(array, axis, 0, 0, tiled=True, axis_index_groups=groups)]
    pallas_call x1, Pallas kernels: 4.18 us -> 1.08 us  [terms(): pl.pallas_call(functools.partial(term_kernel, 1.0 / replicas), out_shape=...]
    pallas_call x2, Pallas kernels: 16.1 us -> 13.6 us  [full_gradient(): pl.pallas_call(functools.partial(gradient_kernel, factor), out_shape=(plt...]
  transfers between devices with their start and end apart: 16 -> 16, of which waited for: 8 -> 8; matrix products, arithmetic and copies ran while one was open for 2% -> 4% of each run, Pallas kernels for 3% -> 3%
where the time goes in v5:
time: 243 us; the launch traced here: 242 us
  blocking collectives  78.6 us (32%)
  starting transfers between devices  66.8 us (27%)
  waiting for transfers between devices  42.1 us (17%)
  other arithmetic  19.6 us (8%)
  Pallas kernels  17.8 us (7%)
  local copies, waits for them, and re-layouts  11 us (5%)
  matrix products  4.54 us (2%)
    all_to_all x3, blocking collectives, exchange(): lax.all_to_all(array, axis, 0, 0, tiled=True, axis_index_groups=groups)  78.6 us
    ppermute x13, starting transfers between devices, send(): return lax.ppermute(array, 'shard', in_plane(rows, cols, core))  41.6 us
    all_to_all x3, waiting for transfers between devices, exchange(): lax.all_to_all(array, axis, 0, 0, tiled=True, axis_index_groups=groups)  26.4 us
    all_to_all x3, starting transfers between devices, exchange(): lax.all_to_all(array, axis, 0, 0, tiled=True, axis_index_groups=groups)  25.1 us
    ppermute x13, waiting for transfers between devices, send(): return lax.ppermute(array, 'shard', in_plane(rows, cols, core))  15.7 us
    pallas_call x2, Pallas kernels, full_gradient(): pl.pallas_call(functools.partial(gradient_kernel, factor), out_shape=(plt...  13.6 us
    another operation x6, other arithmetic, inverse_factor(): chol = jnp.linalg.cholesky(gram)  7.2 us
    another operation x4, other arithmetic, inverse_factor(): return lax.linalg.triangular_solve(chol, eye, left_side=True, lower=True)  6.8 us
  transfers between devices with their start and end apart: 16, of which 8 were waited for; matrix products, arithmetic and copies ran while one was open for 4% of the time, Pallas kernels for 3%

profile of v5, /device:TPU:1, one launch (start us, length us, event | category | flops | bytes accessed | tf_op | source)
XLA Modules:
  0.0 241.5 jit_solution(7606731626195650111)
XLA Ops:
  0.6 1.0 broadcast_in_dim.13
  1.6 12.3 %all_to_all.30 = bf16[4,80,1024]{2,1,0:T(8,128)(2,1)S(1)} all-to-all(bf16[4,80,1024]{2,1,0:T(8,128)(2,1)S(1)} %broadcast_in_dim.13), channel_id=1, replica_groups={{0,2,4,6},{1,3,5,7},{8,10,12,14},{9,11,13,15},{16,18,20,22},{17,19,21,2..., dimensions={0} | all-to-all | bytes 1310720 | tf_op jit(solution)/shard_map/all_to_all | solution.py:21
  14.2 36.1 %all_to_all.31.refs_3_ = bf16[4,4,80,1024]{3,2,1,0:T(8,128)(2,1)} all-to-all(bf16[4,4,80,1024]{3,2,1,0:T(8,128)(2,1)S(1)} %broadcast_in_dim.14), channel_id=1, replica_groups={{0,8,16,24},{1,9,17,25},{2,10,18,26},{3,11,19,27},{4,12,20,28},{5,13,21..., dimensions={0} | all-to-all | bytes 5242880 | tf_op jit(solution)/shard_map/all_to_all | solution.py:21
  50.3 5.3 %collective-permute-start = (bf16[4,4,80,1024]{3,2,1,0:T(8,128)(2,1)}, bf16[4,4,80,1024]{3,2,1,0:T(8,128)(2,1)}, u32[]{:S(2)}, u32[]{:S(2)}) collective-permute-start(bf16[4,4,80,1024]{3,2,1,0:T(8,128)(2,1)} %all_to_all.31.refs_3_), channel_id=1, source_target_pairs={{0,1},{1,0},{2,3},{3,2},{4,5},{5,4},{6,7},{7,6},{8,9},{9,8},{10,11... | collective-permute-start | bytes 7864328 | tf_op jit(solution)/shard_map/ppermute | solution.py:45
  55.7 2.4 %collective-permute-start.2 = (bf16[80,1024]{1,0:T(8,128)(2,1)S(1)}, bf16[80,1024]{1,0:T(8,128)(2,1)S(1)}, u32[]{:S(2)}, u32[]{:S(2)}) collective-permute-start(bf16[80,1024]{1,0:T(8,128)(2,1)S(1)} %bitcast.54), channel_id=1, source_target_pairs={{0,16},{1,17},{2,18},{3,19},{4,20},{5,21},{6,22},{7,23},{8,24},{9,... | collective-permute-start | bytes 491528 | tf_op jit(solution)/shard_map/ppermute | solution.py:45
  58.1 4.0 %collective-permute-start.1 = (bf16[80,1024]{1,0:T(8,128)(2,1)S(1)}, bf16[80,1024]{1,0:T(8,128)(2,1)S(1)}, u32[]{:S(2)}, u32[]{:S(2)}) collective-permute-start(bf16[80,1024]{1,0:T(8,128)(2,1)S(1)} %bitcast.55), channel_id=1, source_target_pairs={{0,24},{1,25},{2,26},{3,27},{4,28},{5,29},{6,30},{7,31},{8,0},{9,1... | collective-permute-start | bytes 491528 | tf_op jit(solution)/shard_map/ppermute | solution.py:45
  62.2 1.9 collective-permute-start.3
  64.8 2.0 collective-permute-done.1
  66.8 3.6 %collective-permute-done.3 = bf16[80,1024]{1,0:T(8,128)(2,1)S(1)} collective-permute-done((bf16[80,1024]{1,0:T(8,128)(2,1)S(1)}, bf16[80,1024]{1,0:T(8,128)(2,1)S(1)}, u32[]{:S(2)}, u32[]{:S(2)}) %collective-permute-start.3) | collective-permute-done | bytes 163872 | tf_op jit(solution)/shard_map/ppermute | solution.py:45
  70.6 2.2 collective-permute-start.5
  72.8 4.3 %collective-permute-start.4 = (bf16[4,80,1024]{2,1,0:T(8,128)(2,1)S(1)}, bf16[4,80,1024]{2,1,0:T(8,128)(2,1)S(1)}, u32[]{:S(2)}, u32[]{:S(2)}) collective-permute-start(bf16[4,80,1024]{2,1,0:T(8,128)(2,1)S(1)} %pad_maximum_fusion.refs_3_), channel_id=1, source_target_pairs={{0,6},{1,7},{2,0},{3,1},{4,2},{5,3},{6,4},{7,5},{8,14},{9,15},{10,... | collective-permute-start | bytes 1966088 | tf_op jit(solution)/shard_map/ppermute | solution.py:45
  77.1 3.9 %collective-permute-start.8 = (bf16[4,80,1024]{2,1,0:T(8,128)(2,1)S(1)}, bf16[4,80,1024]{2,1,0:T(8,128)(2,1)S(1)}, u32[]{:S(2)}, u32[]{:S(2)}) collective-permute-start(bf16[4,80,1024]{2,1,0:T(8,128)(2,1)S(1)} %pad_maximum_fusion.refs_3_), channel_id=1, source_target_pairs={{0,1},{1,0},{2,3},{3,2},{4,5},{5,4},{6,7},{7,6},{8,9},{9,8},{10,11... | collective-permute-start | bytes 1966088 | tf_op jit(solution)/shard_map/ppermute | solution.py:45
  81.0 7.5 %collective-permute-done.5.refs_7_ = bf16[4,80,1024]{2,1,0:T(8,128)(2,1)S(1)} collective-permute-done((bf16[4,80,1024]{2,1,0:T(8,128)(2,1)S(1)}, bf16[4,80,1024]{2,1,0:T(8,128)(2,1)S(1)}, u32[]{:S(2)}, u32[]{:S(2)}) %collective-permute-start.5) | collective-permute-done | bytes 655392 | tf_op jit(solution)/shard_map/ppermute | solution.py:45
  88.6 1.9 collective-permute-start.6
  90.5 4.6 %collective-permute-start.7 = (bf16[2,80,1024]{2,1,0:T(8,128)(2,1)S(1)}, bf16[2,80,1024]{2,1,0:T(8,128)(2,1)}, u32[]{:S(2)}, u32[]{:S(2)}) collective-permute-start(bf16[2,80,1024]{2,1,0:T(8,128)(2,1)S(1)} %slice.49), channel_id=1, source_target_pairs={{0,6},{1,7},{2,0},{3,1},{4,2},{5,3},{6,4},{7,5},{8,14},{9,15},{10,... | collective-permute-start | bytes 983048 | tf_op jit(solution)/shard_map/ppermute | solution.py:45
  95.1 4.8 %collective-permute-start.12 = (bf16[4,80,1024]{2,1,0:T(8,128)(2,1)S(1)}, bf16[4,80,1024]{2,1,0:T(8,128)(2,1)}, u32[]{:S(2)}, u32[]{:S(2)}) collective-permute-start(bf16[4,80,1024]{2,1,0:T(8,128)(2,1)S(1)} %collective-permute-done.5.refs_7_), channel_id=1, source_target_pairs={{0,1},{1,0},{2,3},{3,2},{4,5},{5,4},{6,7},{7,6},{8,9},{9,8},{10,11... | collective-permute-start | bytes 1966088 | tf_op jit(solution)/shard_map/ppermute | solution.py:45
  99.9 1.9 collective-permute-start.9
  101.8 2.4 collective-permute-start.10
  104.3 1.9 collective-permute-start.11
  106.2 1.8 collective-permute-done.11.refs_11_
  108.7 6.7 %shard_map.120 = (f32[160,2560]{1,0:T(8,128)S(1)}, f32[160,32]{1,0:T(8,128)S(1)}) custom-call(s32[1]{0:T(128)} %bitcast.1.shard, bf16[160,1024]{1,0:T(8,128)(2,1)} %bitcast.52, bf16[160,2560]{1,0:T(8,128)(2,1)} %bitcast.50, bf16[2,32,2560]{2,1,0:T(8,128)(2,1)} %bitcast.48, bf16[4,80,1024]{2,1,0:T(8,128)(2,1)} %copy-done.4, bf16[4,80,1024]{2,1,0:T(8,128)(2,1)} %copy-done.6, ...), custom_call_target="tpu_custom_call" | custom-call | tf_op jit(solution)/shard_map/pallas_call | solution.py:149
  115.5 6.8 %shard_map.121 = (f32[160,2560]{1,0:T(8,128)S(1)}, bf16[16,80,128]{2,1,0:T(8,128)(2,1)S(1)}) custom-call(s32[1]{0:T(128)} %bitcast.1.shard, bf16[160,1024]{1,0:T(8,128)(2,1)} %bitcast.53, bf16[160,2560]{1,0:T(8,128)(2,1)} %bitcast.51, bf16[2,32,2560]{2,1,0:T(8,128)(2,1)} %bitcast.49, bf16[4,4,80,1024]{3,2,1,0:T(8,128)(2,1)} %all_to_all.31.refs_3_, ...), custom_call_target="tpu_custom_call" | custom-call | tf_op jit(solution)/shard_map/pallas_call | solution.py:149
  122.4 30.3 %all_to_all.32.arrived = bf16[16,80,128]{2,1,0:T(8,128)(2,1)S(1)} all-to-all(bf16[16,80,128]{2,1,0:T(8,128)(2,1)S(1)} %get-tuple-element.13), channel_id=1, replica_groups=mesh['dp'=16,'shard'=32] {'dp'}, dimensions={0} | all-to-all | bytes 655360 | tf_op jit(solution)/shard_map/all_to_all | solution.py:21
  152.7 1.1 shard_map.122
  153.7 0.8 copy-done
  155.2 10.7 %all-to-all-start.3 = ((bf16[32,80,128]{2,1,0:T(8,128)(2,1)}), bf16[32,80,128]{2,1,0:T(8,128)(2,1)}, u32[]{:S(2)}, u32[]{:S(2)}) async-start(bf16[32,80,128]{2,1,0:T(8,128)(2,1)} %copy-done), calls=%async_computation.3 | async-start | bytes 1310720 | tf_op jit(solution)/shard_map/all_to_all | solution.py:21
  166.0 13.0 %all-to-all-done.3 = bf16[32,80,128]{2,1,0:T(8,128)(2,1)} async-done(((bf16[32,80,128]{2,1,0:T(8,128)(2,1)}), bf16[32,80,128]{2,1,0:T(8,128)(2,1)}, u32[]{:S(2)}, u32[]{:S(2)}) %all-to-all-start.3) | async-done | bytes 655392 | tf_op jit(solution)/shard_map/all_to_all | solution.py:21
  179.0 1.2 convert_reduce_fusion
  181.2 2.9 %cholesky.44 = f32[32,32]{1,0:T(8,128)S(1)} custom-call(f32[32,32]{1,0:T(8,128)S(1)} %fusion.15), custom_call_target="Cholesky" | custom-call | tf_op jit(solution)/shard_map/jit(cholesky)/cholesky | solution.py:318
  185.4 3.1 %custom-call.6 = f32[1,32,32]{1,2,0:T(8,128)} custom-call(f32[1,32,32]{2,1,0:T(8,128)S(1)} %fusion.10), custom_call_target="InvertDiagBlocksLowerTriangular" | custom-call | tf_op jit(solution)/shard_map/triangular_solve/custom-call.0 | solution.py:320
  188.6 2.9 %cholesky.55 = f32[32,32]{1,0:T(8,128)S(1)} custom-call(f32[32,32]{1,0:T(8,128)S(1)} %fusion.13), custom_call_target="Cholesky" | custom-call | tf_op jit(solution)/shard_map/jit(cholesky)/cholesky | solution.py:318
  192.9 2.4 %custom-call.7 = f32[1,32,32]{1,2,0:T(8,128)S(1)} custom-call(f32[1,32,32]{2,1,0:T(8,128)S(1)} %fusion.11), custom_call_target="InvertDiagBlocksLowerTriangular" | custom-call | tf_op jit(solution)/shard_map/triangular_solve/custom-call.0 | solution.py:320
  195.6 1.2 fusion
  197.0 1.4 broadcast_in_dim.15
  198.4 5.6 %all-to-all-start.4 = ((bf16[16,48,128]{2,1,0:T(8,128)(2,1)}), bf16[16,48,128]{2,1,0:T(8,128)(2,1)}, u32[]{:S(2)}, u32[]{:S(2)}) async-start(bf16[16,48,128]{2,1,0:T(8,128)(2,1)} %broadcast_in_dim.15), calls=%async_computation.4 | async-start | bytes 393216 | tf_op jit(solution)/shard_map/all_to_all | solution.py:21
  204.0 0.9 fusion.8
  205.1 1.2 fusion.2
  206.2 0.8 fusion.18
  208.6 1.5 copy.44
  210.1 1.5 subtract_convert_fusion
  211.6 4.9 %all-to-all-done.4 = bf16[16,48,128]{2,1,0:T(8,128)(2,1)} async-done(((bf16[16,48,128]{2,1,0:T(8,128)(2,1)}), bf16[16,48,128]{2,1,0:T(8,128)(2,1)}, u32[]{:S(2)}, u32[]{:S(2)}) %all-to-all-start.4) | async-done | bytes 196640 | tf_op jit(solution)/shard_map/all_to_all | solution.py:21
  216.6 1.0 convert_reduce_fusion.1
  218.3 8.8 %all-to-all-start.5 = ((bf16[32,48,128]{2,1,0:T(8,128)(2,1)}), bf16[32,48,128]{2,1,0:T(8,128)(2,1)}, u32[]{:S(2)}, u32[]{:S(2)}) async-start(bf16[32,48,128]{2,1,0:T(8,128)(2,1)} %broadcast_in_dim.16), calls=%async_computation.5 | async-start | bytes 786432 | tf_op jit(solution)/shard_map/all_to_all | solution.py:21
  227.1 0.9 subtract_convert_fusion.1
  228.1 0.9 maximum_bitcast_fusion
  229.0 8.5 %all-to-all-done.5.arrived = bf16[32,48,128]{2,1,0:T(8,128)(2,1)} async-done(((bf16[32,48,128]{2,1,0:T(8,128)(2,1)}), bf16[32,48,128]{2,1,0:T(8,128)(2,1)}, u32[]{:S(2)}, u32[]{:S(2)}) %all-to-all-start.5) | async-done | bytes 393248 | tf_op jit(solution)/shard_map/all_to_all | solution.py:21
  237.5 0.9 copy-done.2
  238.4 3.1 %shard_map.123 = (bf16[1,160,2560]{2,1,0:T(8,128)(2,1)}, bf16[1,160,2560]{2,1,0:T(8,128)(2,1)}, f32[160,160]{1,0:T(8,128)}, f32[160,160]{1,0:T(8,128)}) custom-call(s32[1]{0:T(128)} %bitcast.replica, bf16[32,48,128]{2,1,0:T(8,128)(2,1)} %all-to-all-done.5.arrived, bf16[2,160,64]{2,1,0:T(8,128)(2,1)S(1)} %pad_maximum_fusion.1.rows, f32[160,160]{1,0:T(8,128)S(1)} %copy-done.1, ...), custom_call_target="tpu_custom_call" | custom-call | tf_op jit(solution)/shard_map/pallas_call | solution.py:296
  (59 shorter events, 9.3 us)
Async XLA Ops:
  14.2 41.4 %copy-start.10 = (bf16[1024,80]{0,1:T(8,128)(2,1)S(1)}, bf16[1024,80]{0,1:T(8,128)(2,1)}, u32[]{:S(2)}) copy-start(bf16[1024,80]{0,1:T(8,128)(2,1)} %param.15) | copy-start | bytes 491524
  50.3 65.2 %collective-permute-start = (bf16[4,4,80,1024]{3,2,1,0:T(8,128)(2,1)}, bf16[4,4,80,1024]{3,2,1,0:T(8,128)(2,1)}, u32[]{:S(2)}, u32[]{:S(2)}) collective-permute-start(bf16[4,4,80,1024]{3,2,1,0:T(8,128)(2,1)} %all_to_all.31.refs_3_), channel_id=1, source_target_pairs={{0,1},{1,0},{2,3},{3,2},{4,5},{5,4},{6,7},{7,6},{8,9},{9,8},{10,11... | collective-permute-start | bytes 7864328 | tf_op jit(solution)/shard_map/ppermute | solution.py:45
  55.7 9.1 %collective-permute-start.2 = (bf16[80,1024]{1,0:T(8,128)(2,1)S(1)}, bf16[80,1024]{1,0:T(8,128)(2,1)S(1)}, u32[]{:S(2)}, u32[]{:S(2)}) collective-permute-start(bf16[80,1024]{1,0:T(8,128)(2,1)S(1)} %bitcast.54), channel_id=1, source_target_pairs={{0,16},{1,17},{2,18},{3,19},{4,20},{5,21},{6,22},{7,23},{8,24},{9,... | collective-permute-start | bytes 491528 | tf_op jit(solution)/shard_map/ppermute | solution.py:45
  58.1 8.7 %collective-permute-start.1 = (bf16[80,1024]{1,0:T(8,128)(2,1)S(1)}, bf16[80,1024]{1,0:T(8,128)(2,1)S(1)}, u32[]{:S(2)}, u32[]{:S(2)}) collective-permute-start(bf16[80,1024]{1,0:T(8,128)(2,1)S(1)} %bitcast.55), channel_id=1, source_target_pairs={{0,24},{1,25},{2,26},{3,27},{4,28},{5,29},{6,30},{7,31},{8,0},{9,1... | collective-permute-start | bytes 491528 | tf_op jit(solution)/shard_map/ppermute | solution.py:45
  62.2 8.3 %collective-permute-start.3 = (bf16[80,1024]{1,0:T(8,128)(2,1)S(1)}, bf16[80,1024]{1,0:T(8,128)(2,1)S(1)}, u32[]{:S(2)}, u32[]{:S(2)}) collective-permute-start(bf16[80,1024]{1,0:T(8,128)(2,1)S(1)} %bitcast.56), channel_id=1, source_target_pairs={{0,8},{1,9},{2,10},{3,11},{4,12},{5,13},{6,14},{7,15},{8,16},{9,17... | collective-permute-start | bytes 491528 | tf_op jit(solution)/shard_map/ppermute | solution.py:45
  70.5 38.2 %copy-start.4 = (bf16[4,80,1024]{2,1,0:T(8,128)(2,1)}, bf16[4,80,1024]{2,1,0:T(8,128)(2,1)S(1)}, u32[]{:S(2)}) copy-start(bf16[4,80,1024]{2,1,0:T(8,128)(2,1)S(1)} %pad_maximum_fusion.refs_3_) | copy-start | bytes 1966084
  70.6 18.0 %collective-permute-start.5 = (bf16[4,80,1024]{2,1,0:T(8,128)(2,1)S(1)}, bf16[4,80,1024]{2,1,0:T(8,128)(2,1)S(1)}, u32[]{:S(2)}, u32[]{:S(2)}) collective-permute-start(bf16[4,80,1024]{2,1,0:T(8,128)(2,1)S(1)} %pad_maximum_fusion.refs_3_), channel_id=1, source_target_pairs={{0,2},{1,3},{2,4},{3,5},{4,6},{5,7},{6,0},{7,1},{8,10},{9,11},{10,... | collective-permute-start | bytes 1966088 | tf_op jit(solution)/shard_map/ppermute | solution.py:45
  72.8 17.7 %collective-permute-start.4 = (bf16[4,80,1024]{2,1,0:T(8,128)(2,1)S(1)}, bf16[4,80,1024]{2,1,0:T(8,128)(2,1)S(1)}, u32[]{:S(2)}, u32[]{:S(2)}) collective-permute-start(bf16[4,80,1024]{2,1,0:T(8,128)(2,1)S(1)} %pad_maximum_fusion.refs_3_), channel_id=1, source_target_pairs={{0,6},{1,7},{2,0},{3,1},{4,2},{5,3},{6,4},{7,5},{8,14},{9,15},{10,... | collective-permute-start | bytes 1966088 | tf_op jit(solution)/shard_map/ppermute | solution.py:45
  77.1 22.8 %collective-permute-start.8 = (bf16[4,80,1024]{2,1,0:T(8,128)(2,1)S(1)}, bf16[4,80,1024]{2,1,0:T(8,128)(2,1)S(1)}, u32[]{:S(2)}, u32[]{:S(2)}) collective-permute-start(bf16[4,80,1024]{2,1,0:T(8,128)(2,1)S(1)} %pad_maximum_fusion.refs_3_), channel_id=1, source_target_pairs={{0,1},{1,0},{2,3},{3,2},{4,5},{5,4},{6,7},{7,6},{8,9},{9,8},{10,11... | collective-permute-start | bytes 1966088 | tf_op jit(solution)/shard_map/ppermute | solution.py:45
  88.5 20.2 %copy-start.5 = (bf16[4,80,1024]{2,1,0:T(8,128)(2,1)}, bf16[4,80,1024]{2,1,0:T(8,128)(2,1)S(1)}, u32[]{:S(2)}) copy-start(bf16[4,80,1024]{2,1,0:T(8,128)(2,1)S(1)} %collective-permute-done.5.refs_7_) | copy-start | bytes 1966084
  88.6 13.3 %collective-permute-start.6 = (bf16[2,80,1024]{2,1,0:T(8,128)(2,1)S(1)}, bf16[2,80,1024]{2,1,0:T(8,128)(2,1)}, u32[]{:S(2)}, u32[]{:S(2)}) collective-permute-start(bf16[2,80,1024]{2,1,0:T(8,128)(2,1)S(1)} %slice.48), channel_id=1, source_target_pairs={{0,2},{1,3},{2,4},{3,5},{4,6},{5,7},{6,0},{7,1},{8,10},{9,11},{10,... | collective-permute-start | bytes 983048 | tf_op jit(solution)/shard_map/ppermute | solution.py:45
  90.5 17.5 %copy-start.6 = (bf16[4,80,1024]{2,1,0:T(8,128)(2,1)}, bf16[4,80,1024]{2,1,0:T(8,128)(2,1)S(1)}, u32[]{:S(2)}) copy-start(bf16[4,80,1024]{2,1,0:T(8,128)(2,1)S(1)} %collective-permute-done.4.refs_4_) | copy-start | bytes 1966084
  90.5 13.7 %collective-permute-start.7 = (bf16[2,80,1024]{2,1,0:T(8,128)(2,1)S(1)}, bf16[2,80,1024]{2,1,0:T(8,128)(2,1)}, u32[]{:S(2)}, u32[]{:S(2)}) collective-permute-start(bf16[2,80,1024]{2,1,0:T(8,128)(2,1)S(1)} %slice.49), channel_id=1, source_target_pairs={{0,6},{1,7},{2,0},{3,1},{4,2},{5,3},{6,4},{7,5},{8,14},{9,15},{10,... | collective-permute-start | bytes 983048 | tf_op jit(solution)/shard_map/ppermute | solution.py:45
  95.1 12.9 %collective-permute-start.12 = (bf16[4,80,1024]{2,1,0:T(8,128)(2,1)S(1)}, bf16[4,80,1024]{2,1,0:T(8,128)(2,1)}, u32[]{:S(2)}, u32[]{:S(2)}) collective-permute-start(bf16[4,80,1024]{2,1,0:T(8,128)(2,1)S(1)} %collective-permute-done.5.refs_7_), channel_id=1, source_target_pairs={{0,1},{1,0},{2,3},{3,2},{4,5},{5,4},{6,7},{7,6},{8,9},{9,8},{10,11... | collective-permute-start | bytes 1966088 | tf_op jit(solution)/shard_map/ppermute | solution.py:45
  99.9 8.1 %copy-start.7 = (bf16[4,80,1024]{2,1,0:T(8,128)(2,1)}, bf16[4,80,1024]{2,1,0:T(8,128)(2,1)S(1)}, u32[]{:S(2)}) copy-start(bf16[4,80,1024]{2,1,0:T(8,128)(2,1)S(1)} %collective-permute-done.8.refs_8_) | copy-start | bytes 1966084
  99.9 8.1 %collective-permute-start.9 = (bf16[4,80,1024]{2,1,0:T(8,128)(2,1)S(1)}, bf16[4,80,1024]{2,1,0:T(8,128)(2,1)}, u32[]{:S(2)}, u32[]{:S(2)}) collective-permute-start(bf16[4,80,1024]{2,1,0:T(8,128)(2,1)S(1)} %collective-permute-done.4.refs_4_), channel_id=1, source_target_pairs={{0,1},{1,0},{2,3},{3,2},{4,5},{5,4},{6,7},{7,6},{8,9},{9,8},{10,11... | collective-permute-start | bytes 1966088 | tf_op jit(solution)/shard_map/ppermute | solution.py:45
  101.8 4.4 %collective-permute-start.10 = (bf16[2,80,1024]{2,1,0:T(8,128)(2,1)}, bf16[2,80,1024]{2,1,0:T(8,128)(2,1)S(1)}, u32[]{:S(2)}, u32[]{:S(2)}) collective-permute-start(bf16[2,80,1024]{2,1,0:T(8,128)(2,1)} %collective-permute-done.6.refs_5_), channel_id=1, source_target_pairs={{0,1},{1,0},{2,3},{3,2},{4,5},{5,4},{6,7},{7,6},{8,9},{9,8},{10,11... | collective-permute-start | bytes 983048 | tf_op jit(solution)/shard_map/ppermute | solution.py:45
  104.3 3.7 %collective-permute-start.11 = (bf16[2,80,1024]{2,1,0:T(8,128)(2,1)}, bf16[2,80,1024]{2,1,0:T(8,128)(2,1)S(1)}, u32[]{:S(2)}, u32[]{:S(2)}) collective-permute-start(bf16[2,80,1024]{2,1,0:T(8,128)(2,1)} %collective-permute-done.7.refs_6_), channel_id=1, source_target_pairs={{0,1},{1,0},{2,3},{3,2},{4,5},{5,4},{6,7},{7,6},{8,9},{9,8},{10,11... | collective-permute-start | bytes 983048 | tf_op jit(solution)/shard_map/ppermute | solution.py:45
  106.2 1.8 copy-start.8
  108.0 0.7 copy-start.9
  153.7 0.8 copy-start
  154.6 0.7 copy-start.3
  155.2 23.7 %all-to-all-start.3 = ((bf16[32,80,128]{2,1,0:T(8,128)(2,1)}), bf16[32,80,128]{2,1,0:T(8,128)(2,1)}, u32[]{:S(2)}, u32[]{:S(2)}) async-start(bf16[32,80,128]{2,1,0:T(8,128)(2,1)} %copy-done), calls=%async_computation.3 | async-start | bytes 1310720 | tf_op jit(solution)/shard_map/all_to_all | solution.py:21
  166.0 71.5 %copy-start.1 = (f32[160,160]{1,0:T(8,128)S(1)}, f32[160,160]{1,0:T(8,128)}, u32[]{:S(2)}) copy-start(f32[160,160]{1,0:T(8,128)} %query_weight.1) | copy-start | bytes 307204
  198.4 18.2 %all-to-all-start.4 = ((bf16[16,48,128]{2,1,0:T(8,128)(2,1)}), bf16[16,48,128]{2,1,0:T(8,128)(2,1)}, u32[]{:S(2)}, u32[]{:S(2)}) async-start(bf16[16,48,128]{2,1,0:T(8,128)(2,1)} %broadcast_in_dim.15), calls=%async_computation.4 | async-start | bytes 393216 | tf_op jit(solution)/shard_map/all_to_all | solution.py:21
  218.3 19.1 %all-to-all-start.5 = ((bf16[32,48,128]{2,1,0:T(8,128)(2,1)}), bf16[32,48,128]{2,1,0:T(8,128)(2,1)}, u32[]{:S(2)}, u32[]{:S(2)}) async-start(bf16[32,48,128]{2,1,0:T(8,128)(2,1)} %broadcast_in_dim.16), calls=%async_computation.5 | async-start | bytes 786432 | tf_op jit(solution)/shard_map/all_to_all | solution.py:21
  237.5 0.9 copy-start.2

commit v6 on v5

--- a/solution.py
+++ b/solution.py
@@ -45,47 +45,40 @@
     return lax.ppermute(array, "shard", in_plane(rows, cols, core))
 
 
-def by_exchange(cotan):
-    side = 4
-    rows = [[(y * side + x) * 2 + c for x in range(side)] for y in range(side) for c in range(2)]
-    cols = [[(y * side + x) * 2 + c for y in range(side)] for x in range(side) for c in range(2)]
-    row = exchange(copies(cotan.T, side), "shard", rows)
-    return exchange(copies(row, side), "shard", cols)
-
-
-def by_rings(cotan):
+def ring(block, rows, cols):
+    low, high = send(block, rows, cols), send(block, 3 * rows, 3 * cols)
+    half = block.shape[0] // 2
+    far = send(low[:half], rows, cols), send(high[half:], 3 * rows, 3 * cols)
+    return block, high, *far, low
+
+
+def first_ring(cotan, rows, cols):
     block = cotan.T
-    below, above, across = send(block, 1, 0), send(block, 3, 0), send(block, 2, 0)
-    column = jnp.stack([block, above, across, below])
-    left, right = send(column, 0, 1), send(column, 0, 3)
-    half = column.shape[0] // 2
-    far_low, far_high = send(left[:half], 0, 1), send(right[half:], 0, 3)
-    return column, right, far_low, far_high, left
+    low, high = send(block, rows, cols), send(block, 3 * rows, 3 * cols)
+    far = send(block, 2 * rows, 2 * cols)
+    return jnp.stack([block, high, far, low])
 
 
 def partner(array):
     return send(array, 0, 0, 1)
 
 
-def gradient_kernel(factor, shard, *refs):
-    acts_in, error_in, start_in, *sources = refs[:-9]
-    full, left, acts, error, start, columns, given, near, done = refs[-9:]
-    in_rings = len(sources) > 3
-    other_left = None if in_rings else sources.pop()
+def gradient_kernel(across, shard, *refs):
+    acts_in, error_in, *sources = refs[:-7]
+    full, acts, error, columns, given, near, done = refs[-7:]
     mine, theirs = sources[: len(sources) // 2], sources[len(sources) // 2 :]
     side, each = 4, columns.shape[1] // 8
     y0, x0, core = shard[0] // 8, shard[0] // 2 % side, shard[0] % 2
 
     def block(refs, j, k):
-        if not in_rings:
-            return refs[0].at[j, k]
-        near, right, far_low, far_high, left = refs
-        if k == 2:
-            return (far_low if j < 2 else far_high).at[j % 2]
-        return (near, right, None, left)[k].at[j]
+        outer, inner = (k, j) if across else (j, k)
+        near, high, far_low, far_high, low = refs
+        if outer == 2:
+            return (far_low if inner < 2 else far_high).at[inner % 2]
+        return (near, high, None, low)[outer].at[inner]
 
     def fetch(j, k, other):
-        x = (x0 + k) % side if in_rings else k
+        x = (x0 + k) % side
         at = (x * 2 + (1 - core if other else core)) * each
         return pltpu.make_async_copy(
             block(theirs if other else mine, j, k),
@@ -94,44 +87,25 @@
         )
 
     def lanes(j):
-        y = (y0 + j) % side if in_rings else j
+        y = (y0 + j) % side
         return pl.ds(pl.multiple_of(y * (8 * each), 128), 8 * each)
 
     def prior(j):
         return pltpu.make_async_copy(error_in.at[:, lanes(j)], error.at[j], near.at[j])
 
     first = pltpu.make_async_copy(acts_in, acts, given.at[0])
-    second = pltpu.make_async_copy(start_in.at[factor], start, given.at[1])
     first.start()
     steps = [(k, other) for k in range(side) for other in range(2)]
     for j in range(side):
         for k, other in steps:
             fetch(j, k, other).start()
         prior(j).start()
-        if j == 0:
-            second.start()
     first.wait()
-    total = jnp.zeros((acts.shape[0], start.shape[0]), F32)
     for j in range(side):
         for k, other in steps:
             fetch(j, k, other).wait()
         prior(j).wait()
-        if j == 0:
-            second.wait()
-        part = contract(acts[...], columns[j], (1, 1)) + error[j].astype(F32)
-        full[:, lanes(j)] = part
-        high, low = split_high_low(part)
-        rows = start[:, lanes(j)]
-        total += contract(high, rows, (1, 1)) + contract(low, rows, (1, 1))
-    if in_rings:
-        left[...] = total
-    else:
-        half = total.shape[0] // 2
-        packed = jnp.concatenate(
-            [total[:half], other_left[:half], total[half:], other_left[half:]], axis=1
-        ).astype(BF16)
-        for r in range(left.shape[0]):
-            left[r] = packed
+        full[:, lanes(j)] = contract(acts[...], columns[j], (1, 1)) + error[j].astype(F32)
 
 
 def in_vmem(*arrays):
@@ -142,31 +116,67 @@
     return [pltpu.with_memory_space_constraint(a, pltpu.HBM) for a in arrays]
 
 
-def full_gradient(inputs, error, factors, factor, blocks, shard, left, *lefts):
+def full_gradient(inputs, error, blocks, shard, across):
     rows, tokens = inputs.shape[::-1]
     width = error.shape[-1]
     vmem = pl.BlockSpec(memory_space=pltpu.VMEM)
     return pl.pallas_call(
-        functools.partial(gradient_kernel, factor),
-        out_shape=(pltpu.VMEM((rows, width), F32), left),
+        functools.partial(gradient_kernel, across),
+        out_shape=pltpu.VMEM((rows, width), F32),
         in_specs=[
             pl.BlockSpec(memory_space=pltpu.SMEM),
-            *[pl.BlockSpec(memory_space=pltpu.HBM)] * 3,
-            *[pl.BlockSpec(memory_space=pltpu.HBM)] * len(blocks),
-            *[vmem] * len(lefts),
+            *[pl.BlockSpec(memory_space=pltpu.HBM)] * (2 + len(blocks)),
         ],
-        out_specs=(vmem, vmem),
+        out_specs=vmem,
         scratch_shapes=[
             pltpu.VMEM((rows, tokens), BF16),
             pltpu.VMEM((4, rows, width // 4), BF16),
-            pltpu.VMEM((factors.shape[-1], width), BF16),
             pltpu.VMEM((4, width // 4, tokens), BF16),
-            pltpu.SemaphoreType.DMA((2,)),
+            pltpu.SemaphoreType.DMA((1,)),
             pltpu.SemaphoreType.DMA((4,)),
             pltpu.SemaphoreType.DMA((4, 8)),
         ],
         compiler_params=pltpu.CompilerParams(vmem_limit_bytes=20 << 20),
-    )(shard, *in_hbm(inputs.T, error[0], jnp.swapaxes(factors, 1, 2), *blocks), *in_vmem(*lefts))
+    )(shard, *in_hbm(inputs.T, error[0], *blocks))
+
+
+def inverse_kernel(grams, lefts, rows):
+    rank = grams.shape[0]
+    lane = lax.broadcasted_iota(jnp.int32, (rank, 4 * rank), 1)
+    row = lax.broadcasted_iota(jnp.int32, (rank, 4 * rank), 0)
+    given = grams[...]
+    unit = (row[:, :rank] == lane[:, :rank]).astype(F32)
+    state = jnp.concatenate(
+        [
+            given[:, :rank] + given[:, rank : 2 * rank],
+            unit,
+            given[:, 2 * rank : 3 * rank] + given[:, 3 * rank :],
+            unit,
+        ],
+        axis=1,
+    )
+    query = lane < 2 * rank
+    for k in range(rank):
+        column = jnp.where(
+            query, state[:, k : k + 1], state[:, 2 * rank + k : 2 * rank + k + 1]
+        )
+        pivot = state[k : k + 1, :] / column[k : k + 1, :]
+        state = jnp.where(row == k, pivot, state - column * pivot)
+    for i in range(2):
+        inverse = state[:, (2 * i + 1) * rank : (2 * i + 2) * rank]
+        product = jnp.dot(lefts[i], inverse, precision=HIGH, preferred_element_type=F32)
+        rows[i] = jnp.concatenate(split_high_low(product), axis=1)
+
+
+def weighted_lefts(grams, lefts):
+    vmem = pl.BlockSpec(memory_space=pltpu.VMEM)
+    return pl.pallas_call(
+        inverse_kernel,
+        out_shape=pltpu.VMEM((*lefts.shape[:2], 2 * lefts.shape[2]), BF16),
+        in_specs=[vmem, vmem],
+        out_specs=vmem,
+        compiler_params=pltpu.CompilerParams(vmem_limit_bytes=8 << 20),
+    )(grams, lefts)
 
 
 TILE = 16
@@ -238,8 +248,8 @@
     return pl.pallas_call(
         functools.partial(term_kernel, 1.0 / replicas),
         out_shape=(
-            jax.ShapeDtypeStruct((shards, depth, 128), BF16),
-            jax.ShapeDtypeStruct((2, rows, rank), F32),
+            pltpu.HBM((shards, depth, 128), BF16),
+            pltpu.HBM((2, rows, rank), F32),
         ),
         in_specs=[vmem] * 3,
         out_specs=(vmem, vmem),
@@ -314,12 +324,6 @@
     return lax.dot_general(a, b, ((dims[:1], dims[1:]), ((), ())), preferred_element_type=F32)
 
 
-def inverse_factor(gram):
-    chol = jnp.linalg.cholesky(gram)
-    eye = jnp.eye(gram.shape[0], dtype=F32)
-    return lax.linalg.triangular_solve(chol, eye, left_side=True, lower=True)
-
-
 def step(
     hidden_in,
     context_in,
@@ -335,53 +339,71 @@
     shards = lax.axis_size("shard")
     shard = lax.axis_index("shard").reshape(1)
     replica = lax.axis_index("dp").reshape(1)
-    query_mine = (by_exchange(query_cotan),)
-    output_mine = by_rings(output_cotan)
-    column, right, far_low, far_high, left = output_mine
-    column = partner(column)
-    right, left = partner(right), partner(left)
-    far_low, far_high = partner(far_low), partner(far_high)
-    query_theirs = [partner(a) for a in query_mine]
     rows, rank = output_error.shape[1], start_factors.shape[-1]
-    output_full, output_left = full_gradient(
-        context_in,
-        output_error,
-        start_factors,
-        1,
-        (*output_mine, column, right, far_low, far_high, left),
-        shard,
-        pltpu.VMEM((rows, rank), F32),
-    )
-    query_full, lefts = full_gradient(
-        hidden_in,
-        query_error,
-        start_factors,
-        0,
-        (*query_mine, *query_theirs),
-        shard,
-        pltpu.VMEM((replicas, rows // 2, 4 * rank), BF16),
-        output_left,
-    )
-
-    sent, lefts = terms(exchange(lefts, "dp"), query_full, output_full, replicas, shards)
+    tokens, columns = query_cotan.shape
+
+    own = lax.dynamic_slice_in_dim(start_factors, shard[0] * columns, columns, 1)
+    partial = jnp.concatenate(
+        [
+            lax.dot_general(
+                own[i], cotan, (((0,), (1,)), ((), ())), preferred_element_type=F32
+            )
+            for i, cotan in enumerate((query_cotan, output_cotan))
+        ]
+    )
+    groups = partial.shape[0] // TILE
+    tiles = partial.reshape(groups, TILE, -1, 128).swapaxes(1, 2).reshape(shards, -1, 128)
+    tiles = exchange(tiles, "shard")
+    tile = tiles.sum(axis=0)
+    tiles = from_everyone(tile, "shard")
+    whole = tiles.reshape(groups, -1, TILE, 128).swapaxes(1, 2).reshape(2, rank, tokens)
+
+    query_line = first_ring(query_cotan, 0, 1)
+    output_line = first_ring(output_cotan, 1, 0)
+
+    def left_of(inputs, error, projection):
+        prior = contract(error[0], start_factors[projection], (1, 0))
+        prior = lax.optimization_barrier(prior)
+        high, low = split_high_low(whole[projection])
+        return contract(inputs.T, high, (1, 1)) + contract(inputs.T, low, (1, 1)) + prior
+
+    query_left = left_of(hidden_in, query_error, 0)
+    output_left = left_of(context_in, output_error, 1)
+    half = rows // 2
+    packed = jnp.concatenate(
+        [query_left[:half], output_left[:half], query_left[half:], output_left[half:]], axis=1
+    )
+    lefts = from_everyone(packed.astype(BF16), "dp")
+
+    output_mine = ring(output_line, 0, 1)
+    query_mine = ring(query_line, 1, 0)
+
+    def swapped(pieces):
+        near, high, far_low, far_high, low = pieces
+        near = partner(near)
+        high, low = partner(high), partner(low)
+        far_low, far_high = partner(far_low), partner(far_high)
+        return near, high, far_low, far_high, low
+
+    output_theirs = swapped(output_mine)
+    query_theirs = swapped(query_mine)
+    output_full = full_gradient(
+        context_in, output_error, (*output_mine, *output_theirs), shard, True
+    )
+    query_full = full_gradient(hidden_in, query_error, (*query_mine, *query_theirs), shard, False)
+
+    sent, lefts = terms(lefts, query_full, output_full, replicas, shards)
     arrived = exchange(sent, "shard").astype(F32).sum(axis=0)
-    share, gram_parts = arrived[:-rank], arrived[-rank:]
+    share, grams = arrived[:-rank], arrived[-rank:]
 
     shares = from_everyone(share.astype(BF16), "dp")
     share = shares.astype(F32).sum(axis=0) / F32(replicas)
 
-    def weighted(left, gram):
-        inverse = inverse_factor(gram)
-        ortho = lax.dot_general(left, inverse, (((1,), (1,)), ((), ())), precision=HIGH)
-        high, low = split_high_low(jnp.dot(ortho, inverse, precision=HIGH))
-        return jnp.concatenate([high, low], axis=1)
-
-    query_rows = weighted(lefts[0], gram_parts[:, :rank] + gram_parts[:, rank : 2 * rank])
-    output_rows = weighted(lefts[1], gram_parts[:, 2 * rank : 3 * rank] + gram_parts[:, 3 * rank :])
+    weighted = weighted_lefts(grams, lefts)
     cols = from_everyone(share.astype(BF16), "shard")
     return finish(
         cols,
-        jnp.stack([query_rows, output_rows]),
+        weighted,
         (query_full, output_full),
         (query_weight, output_weight),
         replica,

time: 243 us -> 204 us (0.84)
  starting transfers between devices: 66.8 us -> 106 us
  blocking collectives: 78.6 us -> 40.5 us
  waiting for transfers between devices: 42.1 us -> 14.8 us
  other arithmetic: 19.6 us -> 2.39 us
  Pallas kernels: 17.8 us -> 21.1 us
    all_to_all x3 -> x2, blocking collectives: 78.6 us -> 40.5 us  [exchange(): lax.all_to_all(array, axis, 0, 0, tiled=True, axis_index_groups=groups)]
    ppermute x13 -> x24, starting transfers between devices: 41.6 us -> 71.6 us  [send(): return lax.ppermute(array, 'shard', in_plane(rows, cols, core))]
    all_to_all x3 -> x4, waiting for transfers between devices: 26.4 us -> 10.9 us  [exchange(): lax.all_to_all(array, axis, 0, 0, tiled=True, axis_index_groups=groups)]
    another operation x13 -> x2, other arithmetic: 15 us -> 2.17 us  [first_ring(): return jnp.stack([block, high, far, low])]
    ppermute x13 -> x24, waiting for transfers between devices: 15.7 us -> 3.93 us  [send(): return lax.ppermute(array, 'shard', in_plane(rows, cols, core))]
    all_to_all x3 -> x4, starting transfers between devices: 25.1 us -> 34.5 us  [exchange(): lax.all_to_all(array, axis, 0, 0, tiled=True, axis_index_groups=groups)]
    slice x4 -> x10, local copies, waits for them, and re-layouts: 0.72 us -> 5.4 us  [the longest x4 5.21 us: ring(): far = (send(low[:half], rows, cols), send(high[half:], 3 * rows, 3 * cols))]
    pallas_call x2 -> x3, Pallas kernels: 13.6 us -> 15.1 us  [the longest x2 11.8 us: full_gradient(): pl.pallas_call(functools.partial(gradient_kernel, across), out_shape=pltp...]
  transfers between devices with their start and end apart: 16 -> 28, of which waited for: 8 -> 3; matrix products, arithmetic and copies ran while one was open for 4% -> 7% of each run, Pallas kernels for 3% -> 7%
where the time goes in v6:
time: 204 us; the launch traced here: 202 us
  starting transfers between devices  106 us (52%)
  blocking collectives  40.5 us (20%)
  Pallas kernels  21.1 us (10%)
  waiting for transfers between devices  14.8 us (7%)
  local copies, waits for them, and re-layouts  11.9 us (6%)
  matrix products  3.87 us (2%)
  other arithmetic  2.39 us (1%)
    ppermute x24, starting transfers between devices, send(): return lax.ppermute(array, 'shard', in_plane(rows, cols, core))  71.6 us
    all_to_all x2, blocking collectives, exchange(): lax.all_to_all(array, axis, 0, 0, tiled=True, axis_index_groups=groups)  40.5 us
    all_to_all x4, starting transfers between devices, exchange(): lax.all_to_all(array, axis, 0, 0, tiled=True, axis_index_groups=groups)  34.5 us
    pallas_call x2, Pallas kernels, full_gradient(): pl.pallas_call(functools.partial(gradient_kernel, across), out_shape=pltp...  11.8 us
    all_to_all x4, waiting for transfers between devices, exchange(): lax.all_to_all(array, axis, 0, 0, tiled=True, axis_index_groups=groups)  10.9 us
    slice x4, local copies, waits for them, and re-layouts, ring(): far = (send(low[:half], rows, cols), send(high[half:], 3 * rows, 3 * cols))  5.21 us
  transfers between devices with their start and end apart: 28, of which 3 were waited for; matrix products, arithmetic and copies ran while one was open for 7% of the time, Pallas kernels for 7%

profile of v6, /device:TPU:1, one launch (start us, length us, event | category | flops | bytes accessed | tf_op | source)
XLA Modules:
  0.0 202.3 jit_solution(8063782934886501712)
XLA Ops:
  0.7 5.6 %collective-permute-start.1 = (bf16[80,1024]{1,0:T(8,128)(2,1)}, bf16[80,1024]{1,0:T(8,128)(2,1)S(1)}, u32[]{:S(2)}, u32[]{:S(2)}) collective-permute-start(bf16[80,1024]{1,0:T(8,128)(2,1)} %bitcast.98), channel_id=1, source_target_pairs={{0,4},{1,5},{2,6},{3,7},{4,0},{5,1},{6,2},{7,3},{8,12},{9,13},{10,... | collective-permute-start | bytes 491528 | tf_op jit(solution)/shard_map/ppermute | solution.py:45
  6.3 2.8 %collective-permute-start = (bf16[80,1024]{1,0:T(8,128)(2,1)}, bf16[80,1024]{1,0:T(8,128)(2,1)}, u32[]{:S(2)}, u32[]{:S(2)}) collective-permute-start(bf16[80,1024]{1,0:T(8,128)(2,1)} %bitcast.99), channel_id=1, source_target_pairs={{0,6},{1,7},{2,0},{3,1},{4,2},{5,3},{6,4},{7,5},{8,14},{9,15},{10,... | collective-permute-start | bytes 491528 | tf_op jit(solution)/shard_map/ppermute | solution.py:45
  9.0 2.5 %collective-permute-start.2 = (bf16[80,1024]{1,0:T(8,128)(2,1)}, bf16[80,1024]{1,0:T(8,128)(2,1)}, u32[]{:S(2)}, u32[]{:S(2)}) collective-permute-start(bf16[80,1024]{1,0:T(8,128)(2,1)} %bitcast.100), channel_id=1, source_target_pairs={{0,2},{1,3},{2,4},{3,5},{4,6},{5,7},{6,0},{7,1},{8,10},{9,11},{10,... | collective-permute-start | bytes 491528 | tf_op jit(solution)/shard_map/ppermute | solution.py:45
  11.6 4.8 %collective-permute-start.13 = (bf16[80,1024]{1,0:T(8,128)(2,1)}, bf16[80,1024]{1,0:T(8,128)(2,1)S(1)}, u32[]{:S(2)}, u32[]{:S(2)}) collective-permute-start(bf16[80,1024]{1,0:T(8,128)(2,1)} %bitcast.94), channel_id=1, source_target_pairs={{0,16},{1,17},{2,18},{3,19},{4,20},{5,21},{6,22},{7,23},{8,24},{9,... | collective-permute-start | bytes 491528 | tf_op jit(solution)/shard_map/ppermute | solution.py:45
  16.4 2.7 %collective-permute-start.12 = (bf16[80,1024]{1,0:T(8,128)(2,1)}, bf16[80,1024]{1,0:T(8,128)(2,1)}, u32[]{:S(2)}, u32[]{:S(2)}) collective-permute-start(bf16[80,1024]{1,0:T(8,128)(2,1)} %bitcast.95), channel_id=1, source_target_pairs={{0,24},{1,25},{2,26},{3,27},{4,28},{5,29},{6,30},{7,31},{8,0},{9,1... | collective-permute-start | bytes 491528 | tf_op jit(solution)/shard_map/ppermute | solution.py:45
  19.1 1.1 fusion.19
  20.3 1.2 fusion.18
  22.3 8.6 %all-to-all-start = ((f32[32,16,128]{2,1,0:T(8,128)}), f32[32,16,128]{2,1,0:T(8,128)S(1)}, u32[]{:S(2)}, u32[]{:S(2)}) async-start(f32[32,16,128]{2,1,0:T(8,128)} %bitcast.4), calls=%async_computation | async-start | bytes 524288 | tf_op jit(solution)/shard_map/all_to_all | solution.py:21
  31.4 3.4 %collective-permute-start.14 = (bf16[80,1024]{1,0:T(8,128)(2,1)S(1)}, bf16[80,1024]{1,0:T(8,128)(2,1)S(1)}, u32[]{:S(2)}, u32[]{:S(2)}) collective-permute-start(bf16[80,1024]{1,0:T(8,128)(2,1)S(1)} %bitcast.96), channel_id=1, source_target_pairs={{0,8},{1,9},{2,10},{3,11},{4,12},{5,13},{6,14},{7,15},{8,16},{9,17... | collective-permute-start | bytes 491528 | tf_op jit(solution)/shard_map/ppermute | solution.py:45
  35.1 4.7 %all-to-all-done = f32[32,16,128]{2,1,0:T(8,128)S(1)} async-done(((f32[32,16,128]{2,1,0:T(8,128)}), f32[32,16,128]{2,1,0:T(8,128)S(1)}, u32[]{:S(2)}, u32[]{:S(2)}) %all-to-all-start) | async-done | bytes 262176 | tf_op jit(solution)/shard_map/all_to_all | solution.py:21
  40.6 3.8 %all-to-all-start.1 = ((f32[32,16,128]{2,1,0:T(8,128)}), f32[32,16,128]{2,1,0:T(8,128)S(1)}, u32[]{:S(2)}, u32[]{:S(2)}) async-start(f32[32,16,128]{2,1,0:T(8,128)} %broadcast_in_dim.12), calls=%async_computation.1 | async-start | bytes 524288 | tf_op jit(solution)/shard_map/all_to_all | solution.py:21
  44.4 1.0 pad_maximum_fusion.1.refs_2_
  45.5 2.2 %collective-permute-start.19 = (bf16[4,80,1024]{2,1,0:T(8,128)(2,1)S(1)}, bf16[4,80,1024]{2,1,0:T(8,128)(2,1)}, u32[]{:S(2)}, u32[]{:S(2)}) collective-permute-start(bf16[4,80,1024]{2,1,0:T(8,128)(2,1)S(1)} %pad_maximum_fusion.1.refs_2_), channel_id=1, source_target_pairs={{0,1},{1,0},{2,3},{3,2},{4,5},{5,4},{6,7},{7,6},{8,9},{9,8},{10,11... | collective-permute-start | bytes 1966088 | tf_op jit(solution)/shard_map/ppermute | solution.py:45
  47.7 3.4 %collective-permute-start.16 = (bf16[4,80,1024]{2,1,0:T(8,128)(2,1)S(1)}, bf16[4,80,1024]{2,1,0:T(8,128)(2,1)S(1)}, u32[]{:S(2)}, u32[]{:S(2)}) collective-permute-start(bf16[4,80,1024]{2,1,0:T(8,128)(2,1)S(1)} %pad_maximum_fusion.1.refs_2_), channel_id=1, source_target_pairs={{0,2},{1,3},{2,4},{3,5},{4,6},{5,7},{6,0},{7,1},{8,10},{9,11},{10,... | collective-permute-start | bytes 1966088 | tf_op jit(solution)/shard_map/ppermute | solution.py:45
  51.1 3.1 %collective-permute-start.15 = (bf16[4,80,1024]{2,1,0:T(8,128)(2,1)S(1)}, bf16[4,80,1024]{2,1,0:T(8,128)(2,1)}, u32[]{:S(2)}, u32[]{:S(2)}) collective-permute-start(bf16[4,80,1024]{2,1,0:T(8,128)(2,1)S(1)} %pad_maximum_fusion.1.refs_2_), channel_id=1, source_target_pairs={{0,6},{1,7},{2,0},{3,1},{4,2},{5,3},{6,4},{7,5},{8,14},{9,15},{10,... | collective-permute-start | bytes 1966088 | tf_op jit(solution)/shard_map/ppermute | solution.py:45
  54.3 1.1 pad_maximum_fusion.refs_2_
  55.4 3.4 %collective-permute-start.4 = (bf16[4,80,1024]{2,1,0:T(8,128)(2,1)S(1)}, bf16[4,80,1024]{2,1,0:T(8,128)(2,1)}, u32[]{:S(2)}, u32[]{:S(2)}) collective-permute-start(bf16[4,80,1024]{2,1,0:T(8,128)(2,1)S(1)} %pad_maximum_fusion.refs_2_), channel_id=1, source_target_pairs={{0,8},{1,9},{2,10},{3,11},{4,12},{5,13},{6,14},{7,15},{8,16},{9,17... | collective-permute-start | bytes 1966088 | tf_op jit(solution)/shard_map/ppermute | solution.py:45
  58.8 3.2 %collective-permute-start.3 = (bf16[4,80,1024]{2,1,0:T(8,128)(2,1)S(1)}, bf16[4,80,1024]{2,1,0:T(8,128)(2,1)}, u32[]{:S(2)}, u32[]{:S(2)}) collective-permute-start(bf16[4,80,1024]{2,1,0:T(8,128)(2,1)S(1)} %pad_maximum_fusion.refs_2_), channel_id=1, source_target_pairs={{0,24},{1,25},{2,26},{3,27},{4,28},{5,29},{6,30},{7,31},{8,0},{9,1... | collective-permute-start | bytes 1966088 | tf_op jit(solution)/shard_map/ppermute | solution.py:45
  63.1 3.9 %collective-permute-done.16.refs_6_ = bf16[4,80,1024]{2,1,0:T(8,128)(2,1)S(1)} collective-permute-done((bf16[4,80,1024]{2,1,0:T(8,128)(2,1)S(1)}, bf16[4,80,1024]{2,1,0:T(8,128)(2,1)S(1)}, u32[]{:S(2)}, u32[]{:S(2)}) %collective-permute-start.16) | collective-permute-done | bytes 655392 | tf_op jit(solution)/shard_map/ppermute | solution.py:45
  67.8 2.2 %collective-permute-start.17 = (bf16[2,80,1024]{2,1,0:T(8,128)(2,1)}, bf16[2,80,1024]{2,1,0:T(8,128)(2,1)S(1)}, u32[]{:S(2)}, u32[]{:S(2)}) collective-permute-start(bf16[2,80,1024]{2,1,0:T(8,128)(2,1)} %slice.79), channel_id=1, source_target_pairs={{0,2},{1,3},{2,4},{3,5},{4,6},{5,7},{6,0},{7,1},{8,10},{9,11},{10,... | collective-permute-start | bytes 983048 | tf_op jit(solution)/shard_map/ppermute | solution.py:45
  70.0 1.7 slice.80
  71.7 4.2 %collective-permute-start.18 = (bf16[2,80,1024]{2,1,0:T(8,128)(2,1)}, bf16[2,80,1024]{2,1,0:T(8,128)(2,1)}, u32[]{:S(2)}, u32[]{:S(2)}) collective-permute-start(bf16[2,80,1024]{2,1,0:T(8,128)(2,1)} %slice.80), channel_id=1, source_target_pairs={{0,6},{1,7},{2,0},{3,1},{4,2},{5,3},{6,4},{7,5},{8,14},{9,15},{10,... | collective-permute-start | bytes 983048 | tf_op jit(solution)/shard_map/ppermute | solution.py:45
  76.0 1.7 slice.77
  77.7 3.3 %collective-permute-start.5 = (bf16[2,80,1024]{2,1,0:T(8,128)(2,1)}, bf16[2,80,1024]{2,1,0:T(8,128)(2,1)S(1)}, u32[]{:S(2)}, u32[]{:S(2)}) collective-permute-start(bf16[2,80,1024]{2,1,0:T(8,128)(2,1)} %slice.77), channel_id=1, source_target_pairs={{0,8},{1,9},{2,10},{3,11},{4,12},{5,13},{6,14},{7,15},{8,16},{9,17... | collective-permute-start | bytes 983048 | tf_op jit(solution)/shard_map/ppermute | solution.py:45
  82.0 13.3 %all-to-all-start.2 = ((bf16[16,80,128]{2,1,0:T(8,128)(2,1)}), bf16[16,80,128]{2,1,0:T(8,128)(2,1)}, u32[]{:S(2)}, u32[]{:S(2)}) async-start(bf16[16,80,128]{2,1,0:T(8,128)(2,1)} %broadcast_in_dim.13), calls=%async_computation.2 | async-start | bytes 655360 | tf_op jit(solution)/shard_map/all_to_all | solution.py:21
  95.3 1.0 slice.78
  96.3 3.3 %collective-permute-start.6 = (bf16[2,80,1024]{2,1,0:T(8,128)(2,1)S(1)}, bf16[2,80,1024]{2,1,0:T(8,128)(2,1)S(1)}, u32[]{:S(2)}, u32[]{:S(2)}) collective-permute-start(bf16[2,80,1024]{2,1,0:T(8,128)(2,1)S(1)} %slice.78), channel_id=1, source_target_pairs={{0,24},{1,25},{2,26},{3,27},{4,28},{5,29},{6,30},{7,31},{8,0},{9,1... | collective-permute-start | bytes 983048 | tf_op jit(solution)/shard_map/ppermute | solution.py:45
  99.6 4.1 %collective-permute-start.23 = (bf16[4,80,1024]{2,1,0:T(8,128)(2,1)S(1)}, bf16[4,80,1024]{2,1,0:T(8,128)(2,1)S(1)}, u32[]{:S(2)}, u32[]{:S(2)}) collective-permute-start(bf16[4,80,1024]{2,1,0:T(8,128)(2,1)S(1)} %collective-permute-done.16.refs_6_), channel_id=1, source_target_pairs={{0,1},{1,0},{2,3},{3,2},{4,5},{5,4},{6,7},{7,6},{8,9},{9,8},{10,11... | collective-permute-start | bytes 1966088 | tf_op jit(solution)/shard_map/ppermute | solution.py:45
  103.8 1.9 collective-permute-start.20
  105.7 2.4 %collective-permute-start.21 = (bf16[2,80,1024]{2,1,0:T(8,128)(2,1)S(1)}, bf16[2,80,1024]{2,1,0:T(8,128)(2,1)S(1)}, u32[]{:S(2)}, u32[]{:S(2)}) collective-permute-start(bf16[2,80,1024]{2,1,0:T(8,128)(2,1)S(1)} %collective-permute-done.17.refs_4_), channel_id=1, source_target_pairs={{0,1},{1,0},{2,3},{3,2},{4,5},{5,4},{6,7},{7,6},{8,9},{9,8},{10,11... | collective-permute-start | bytes 983048 | tf_op jit(solution)/shard_map/ppermute | solution.py:45
  108.1 1.9 collective-permute-start.22
  110.1 2.4 %collective-permute-start.7 = (bf16[4,80,1024]{2,1,0:T(8,128)(2,1)S(1)}, bf16[4,80,1024]{2,1,0:T(8,128)(2,1)S(1)}, u32[]{:S(2)}, u32[]{:S(2)}) collective-permute-start(bf16[4,80,1024]{2,1,0:T(8,128)(2,1)S(1)} %pad_maximum_fusion.refs_2_), channel_id=1, source_target_pairs={{0,1},{1,0},{2,3},{3,2},{4,5},{5,4},{6,7},{7,6},{8,9},{9,8},{10,11... | collective-permute-start | bytes 1966088 | tf_op jit(solution)/shard_map/ppermute | solution.py:45
  112.5 1.9 collective-permute-start.11
  114.5 2.4 %collective-permute-start.8 = (bf16[4,80,1024]{2,1,0:T(8,128)(2,1)}, bf16[4,80,1024]{2,1,0:T(8,128)(2,1)S(1)}, u32[]{:S(2)}, u32[]{:S(2)}) collective-permute-start(bf16[4,80,1024]{2,1,0:T(8,128)(2,1)} %collective-permute-done.3.refs_3_), channel_id=1, source_target_pairs={{0,1},{1,0},{2,3},{3,2},{4,5},{5,4},{6,7},{7,6},{8,9},{9,8},{10,11... | collective-permute-start | bytes 1966088 | tf_op jit(solution)/shard_map/ppermute | solution.py:45
  116.9 1.9 collective-permute-start.9
  118.8 2.4 %collective-permute-start.10 = (bf16[2,80,1024]{2,1,0:T(8,128)(2,1)S(1)}, bf16[2,80,1024]{2,1,0:T(8,128)(2,1)S(1)}, u32[]{:S(2)}, u32[]{:S(2)}) collective-permute-start(bf16[2,80,1024]{2,1,0:T(8,128)(2,1)S(1)} %collective-permute-done.6.refs_5_), channel_id=1, source_target_pairs={{0,1},{1,0},{2,3},{3,2},{4,5},{5,4},{6,7},{7,6},{8,9},{9,8},{10,11... | collective-permute-start | bytes 983048 | tf_op jit(solution)/shard_map/ppermute | solution.py:45
  121.3 5.9 %shard_map.121.refs_1_ = f32[160,2560]{1,0:T(8,128)S(1)} custom-call(s32[1]{0:T(128)} %bitcast.14.shard, bf16[160,1024]{1,0:T(8,128)(2,1)} %bitcast.86, bf16[160,2560]{1,0:T(8,128)(2,1)} %bitcast.84, bf16[4,80,1024]{2,1,0:T(8,128)(2,1)} %copy-done.8, bf16[4,80,1024]{2,1,0:T(8,128)(2,1)} %collective-permute-done.15.refs_3_, bf16[2,80,1024]{2,1,0:T(8,128)(2,1)} %copy-done.19, ...), custom_call_target="tpu_custom_call" | custom-call | tf_op jit(solution)/shard_map/pallas_call | solution.py:123
  128.8 5.9 %shard_map.120.refs_0_ = f32[160,2560]{1,0:T(8,128)S(1)} custom-call(s32[1]{0:T(128)} %bitcast.14.shard, bf16[160,1024]{1,0:T(8,128)(2,1)} %bitcast.87, bf16[160,2560]{1,0:T(8,128)(2,1)} %bitcast.85, bf16[4,80,1024]{2,1,0:T(8,128)(2,1)} %copy-done.7, bf16[4,80,1024]{2,1,0:T(8,128)(2,1)} %collective-permute-done.3.refs_3_, bf16[2,80,1024]{2,1,0:T(8,128)(2,1)} %copy-done.18, ...), custom_call_target="tpu_custom_call" | custom-call | tf_op jit(solution)/shard_map/pallas_call | solution.py:123
  134.7 2.9 %shard_map.122 = (bf16[32,80,128]{2,1,0:T(8,128)(2,1)}, f32[2,160,32]{2,1,0:T(8,128)}) custom-call(bf16[16,80,128]{2,1,0:T(8,128)(2,1)} %all-to-all-done.2.arrived, f32[160,2560]{1,0:T(8,128)S(1)} %shard_map.120.refs_0_, f32[160,2560]{1,0:T(8,128)S(1)} %shard_map.121.refs_1_), custom_call_target="tpu_custom_call" | custom-call | tf_op jit(solution)/shard_map/pallas_call | solution.py:248
  137.6 16.5 %all_to_all.30 = bf16[32,80,128]{2,1,0:T(8,128)(2,1)S(1)} all-to-all(bf16[32,80,128]{2,1,0:T(8,128)(2,1)} %get-tuple-element.6), channel_id=1, replica_groups=mesh['dp'=16,'shard'=32] {'shard'}, dimensions={0} | all-to-all | bytes 1310720 | tf_op jit(solution)/shard_map/all_to_all | solution.py:21
  154.2 24.0 %all_to_all.31 = bf16[16,48,128]{2,1,0:T(8,128)(2,1)S(1)} all-to-all(bf16[16,48,128]{2,1,0:T(8,128)(2,1)S(1)} %broadcast_in_dim.14), channel_id=1, replica_groups=mesh['dp'=16,'shard'=32] {'dp'}, dimensions={0} | all-to-all | bytes 393216 | tf_op jit(solution)/shard_map/all_to_all | solution.py:21
  178.3 0.8 broadcast_in_dim.15
  179.1 8.8 %all-to-all-start.5 = ((bf16[32,48,128]{2,1,0:T(8,128)(2,1)}), bf16[32,48,128]{2,1,0:T(8,128)(2,1)}, u32[]{:S(2)}, u32[]{:S(2)}) async-start(bf16[32,48,128]{2,1,0:T(8,128)(2,1)} %broadcast_in_dim.15), calls=%async_computation.5 | async-start | bytes 786432 | tf_op jit(solution)/shard_map/all_to_all | solution.py:21
  187.9 0.9 copy-done.2
  188.8 3.3 %shard_map.123.rows = bf16[2,160,64]{2,1,0:T(8,128)(2,1)S(1)} custom-call(f32[32,128]{1,0:T(8,128)S(1)} %slice.82.grams, f32[2,160,32]{2,1,0:T(8,128)S(1)} %copy-done.2), custom_call_target="tpu_custom_call" | custom-call | tf_op jit(solution)/shard_map/pallas_call | solution.py:173
  192.1 6.1 %all-to-all-done.5.arrived = bf16[32,48,128]{2,1,0:T(8,128)(2,1)} async-done(((bf16[32,48,128]{2,1,0:T(8,128)(2,1)}), bf16[32,48,128]{2,1,0:T(8,128)(2,1)}, u32[]{:S(2)}, u32[]{:S(2)}) %all-to-all-start.5) | async-done | bytes 393248 | tf_op jit(solution)/shard_map/all_to_all | solution.py:21
  198.2 0.9 copy-done.1
  199.1 3.1 %shard_map.124 = (bf16[1,160,2560]{2,1,0:T(8,128)(2,1)}, bf16[1,160,2560]{2,1,0:T(8,128)(2,1)}, f32[160,160]{1,0:T(8,128)}, f32[160,160]{1,0:T(8,128)}) custom-call(s32[1]{0:T(128)} %bitcast.replica, bf16[32,48,128]{2,1,0:T(8,128)(2,1)} %all-to-all-done.5.arrived, bf16[2,160,64]{2,1,0:T(8,128)(2,1)S(1)} %shard_map.123.rows, f32[160,160]{1,0:T(8,128)S(1)} %copy-done, ...), custom_call_target="tpu_custom_call" | custom-call | tf_op jit(solution)/shard_map/pallas_call | solution.py:306
  (98 shorter events, 6.7 us)
Async XLA Ops:
  0.6 30.4 %copy-start.17 = (bf16[2,2560,32]{1,2,0:T(8,128)(2,1)S(1)}, bf16[2,2560,32]{1,2,0:T(8,128)(2,1)}, u32[]{:S(2)}) copy-start(bf16[2,2560,32]{1,2,0:T(8,128)(2,1)} %param.17) | copy-start | bytes 983044
  0.6 30.4 %copy-start.4 = (bf16[1,160,2560]{2,1,0:T(8,128)(2,1)S(1)}, bf16[1,160,2560]{2,1,0:T(8,128)(2,1)}, u32[]{:S(2)}) copy-start(bf16[1,160,2560]{2,1,0:T(8,128)(2,1)} %param.13) | copy-start | bytes 2457604
  0.7 50.4 %collective-permute-start.1 = (bf16[80,1024]{1,0:T(8,128)(2,1)}, bf16[80,1024]{1,0:T(8,128)(2,1)S(1)}, u32[]{:S(2)}, u32[]{:S(2)}) collective-permute-start(bf16[80,1024]{1,0:T(8,128)(2,1)} %bitcast.98), channel_id=1, source_target_pairs={{0,4},{1,5},{2,6},{3,7},{4,0},{5,1},{6,2},{7,3},{8,12},{9,13},{10,... | collective-permute-start | bytes 491528 | tf_op jit(solution)/shard_map/ppermute | solution.py:45
  6.3 48.0 %collective-permute-start = (bf16[80,1024]{1,0:T(8,128)(2,1)}, bf16[80,1024]{1,0:T(8,128)(2,1)}, u32[]{:S(2)}, u32[]{:S(2)}) collective-permute-start(bf16[80,1024]{1,0:T(8,128)(2,1)} %bitcast.99), channel_id=1, source_target_pairs={{0,6},{1,7},{2,0},{3,1},{4,2},{5,3},{6,4},{7,5},{8,14},{9,15},{10,... | collective-permute-start | bytes 491528 | tf_op jit(solution)/shard_map/ppermute | solution.py:45
  9.0 45.2 %collective-permute-start.2 = (bf16[80,1024]{1,0:T(8,128)(2,1)}, bf16[80,1024]{1,0:T(8,128)(2,1)}, u32[]{:S(2)}, u32[]{:S(2)}) collective-permute-start(bf16[80,1024]{1,0:T(8,128)(2,1)} %bitcast.100), channel_id=1, source_target_pairs={{0,2},{1,3},{2,4},{3,5},{4,6},{5,7},{6,0},{7,1},{8,10},{9,11},{10,... | collective-permute-start | bytes 491528 | tf_op jit(solution)/shard_map/ppermute | solution.py:45
  11.6 19.8 %collective-permute-start.13 = (bf16[80,1024]{1,0:T(8,128)(2,1)}, bf16[80,1024]{1,0:T(8,128)(2,1)S(1)}, u32[]{:S(2)}, u32[]{:S(2)}) collective-permute-start(bf16[80,1024]{1,0:T(8,128)(2,1)} %bitcast.94), channel_id=1, source_target_pairs={{0,16},{1,17},{2,18},{3,19},{4,20},{5,21},{6,22},{7,23},{8,24},{9,... | collective-permute-start | bytes 491528 | tf_op jit(solution)/shard_map/ppermute | solution.py:45
  16.4 28.0 %collective-permute-start.12 = (bf16[80,1024]{1,0:T(8,128)(2,1)}, bf16[80,1024]{1,0:T(8,128)(2,1)}, u32[]{:S(2)}, u32[]{:S(2)}) collective-permute-start(bf16[80,1024]{1,0:T(8,128)(2,1)} %bitcast.95), channel_id=1, source_target_pairs={{0,24},{1,25},{2,26},{3,27},{4,28},{5,29},{6,30},{7,31},{8,0},{9,1... | collective-permute-start | bytes 491528 | tf_op jit(solution)/shard_map/ppermute | solution.py:45
  20.2 11.1 %copy-start.15 = (bf16[1024,80]{0,1:T(8,128)(2,1)S(1)}, bf16[1024,80]{0,1:T(8,128)(2,1)}, u32[]{:S(2)}) copy-start(bf16[1024,80]{0,1:T(8,128)(2,1)} %param.12) | copy-start | bytes 491524
  20.3 14.5 %copy-start.3 = (bf16[1,160,2560]{2,1,0:T(8,128)(2,1)S(1)}, bf16[1,160,2560]{2,1,0:T(8,128)(2,1)}, u32[]{:S(2)}) copy-start(bf16[1,160,2560]{2,1,0:T(8,128)(2,1)} %param.14) | copy-start | bytes 2457604
  22.3 17.5 %all-to-all-start = ((f32[32,16,128]{2,1,0:T(8,128)}), f32[32,16,128]{2,1,0:T(8,128)S(1)}, u32[]{:S(2)}, u32[]{:S(2)}) async-start(f32[32,16,128]{2,1,0:T(8,128)} %bitcast.4), calls=%async_computation | async-start | bytes 524288 | tf_op jit(solution)/shard_map/all_to_all | solution.py:21
  31.3 22.9 %copy-start.16 = (bf16[1024,80]{0,1:T(8,128)(2,1)S(1)}, bf16[1024,80]{0,1:T(8,128)(2,1)}, u32[]{:S(2)}) copy-start(bf16[1024,80]{0,1:T(8,128)(2,1)} %param.11) | copy-start | bytes 491524
  31.4 13.0 %collective-permute-start.14 = (bf16[80,1024]{1,0:T(8,128)(2,1)S(1)}, bf16[80,1024]{1,0:T(8,128)(2,1)S(1)}, u32[]{:S(2)}, u32[]{:S(2)}) collective-permute-start(bf16[80,1024]{1,0:T(8,128)(2,1)S(1)} %bitcast.96), channel_id=1, source_target_pairs={{0,8},{1,9},{2,10},{3,11},{4,12},{5,13},{6,14},{7,15},{8,16},{9,17... | collective-permute-start | bytes 491528 | tf_op jit(solution)/shard_map/ppermute | solution.py:45
  40.6 21.4 %all-to-all-start.1 = ((f32[32,16,128]{2,1,0:T(8,128)}), f32[32,16,128]{2,1,0:T(8,128)S(1)}, u32[]{:S(2)}, u32[]{:S(2)}) async-start(f32[32,16,128]{2,1,0:T(8,128)} %broadcast_in_dim.12), calls=%async_computation.1 | async-start | bytes 524288 | tf_op jit(solution)/shard_map/all_to_all | solution.py:21
  44.4 17.7 %copy-start.6 = (bf16[1024,160]{0,1:T(8,128)(2,1)S(1)}, bf16[1024,160]{0,1:T(8,128)(2,1)}, u32[]{:S(2)}) copy-start(bf16[1024,160]{0,1:T(8,128)(2,1)} %param.9) | copy-start | bytes 983044
  45.5 17.1 %copy-start.8 = (bf16[4,80,1024]{2,1,0:T(8,128)(2,1)}, bf16[4,80,1024]{2,1,0:T(8,128)(2,1)S(1)}, u32[]{:S(2)}) copy-start(bf16[4,80,1024]{2,1,0:T(8,128)(2,1)S(1)} %pad_maximum_fusion.1.refs_2_) | copy-start | bytes 1966084
  45.5 54.1 %collective-permute-start.19 = (bf16[4,80,1024]{2,1,0:T(8,128)(2,1)S(1)}, bf16[4,80,1024]{2,1,0:T(8,128)(2,1)}, u32[]{:S(2)}, u32[]{:S(2)}) collective-permute-start(bf16[4,80,1024]{2,1,0:T(8,128)(2,1)S(1)} %pad_maximum_fusion.1.refs_2_), channel_id=1, source_target_pairs={{0,1},{1,0},{2,3},{3,2},{4,5},{5,4},{6,7},{7,6},{8,9},{9,8},{10,11... | collective-permute-start | bytes 1966088 | tf_op jit(solution)/shard_map/ppermute | solution.py:45
  47.7 19.3 %collective-permute-start.16 = (bf16[4,80,1024]{2,1,0:T(8,128)(2,1)S(1)}, bf16[4,80,1024]{2,1,0:T(8,128)(2,1)S(1)}, u32[]{:S(2)}, u32[]{:S(2)}) collective-permute-start(bf16[4,80,1024]{2,1,0:T(8,128)(2,1)S(1)} %pad_maximum_fusion.1.refs_2_), channel_id=1, source_target_pairs={{0,2},{1,3},{2,4},{3,5},{4,6},{5,7},{6,0},{7,1},{8,10},{9,11},{10,... | collective-permute-start | bytes 1966088 | tf_op jit(solution)/shard_map/ppermute | solution.py:45
  51.1 19.0 %collective-permute-start.15 = (bf16[4,80,1024]{2,1,0:T(8,128)(2,1)S(1)}, bf16[4,80,1024]{2,1,0:T(8,128)(2,1)}, u32[]{:S(2)}, u32[]{:S(2)}) collective-permute-start(bf16[4,80,1024]{2,1,0:T(8,128)(2,1)S(1)} %pad_maximum_fusion.1.refs_2_), channel_id=1, source_target_pairs={{0,6},{1,7},{2,0},{3,1},{4,2},{5,3},{6,4},{7,5},{8,14},{9,15},{10,... | collective-permute-start | bytes 1966088 | tf_op jit(solution)/shard_map/ppermute | solution.py:45
  54.2 8.3 %copy-start.5 = (bf16[1024,160]{0,1:T(8,128)(2,1)S(1)}, bf16[1024,160]{0,1:T(8,128)(2,1)}, u32[]{:S(2)}) copy-start(bf16[1024,160]{0,1:T(8,128)(2,1)} %param.10) | copy-start | bytes 983044
  55.4 54.7 %copy-start.7 = (bf16[4,80,1024]{2,1,0:T(8,128)(2,1)}, bf16[4,80,1024]{2,1,0:T(8,128)(2,1)S(1)}, u32[]{:S(2)}) copy-start(bf16[4,80,1024]{2,1,0:T(8,128)(2,1)S(1)} %pad_maximum_fusion.refs_2_) | copy-start | bytes 1966084
  55.4 20.6 %collective-permute-start.4 = (bf16[4,80,1024]{2,1,0:T(8,128)(2,1)S(1)}, bf16[4,80,1024]{2,1,0:T(8,128)(2,1)}, u32[]{:S(2)}, u32[]{:S(2)}) collective-permute-start(bf16[4,80,1024]{2,1,0:T(8,128)(2,1)S(1)} %pad_maximum_fusion.refs_2_), channel_id=1, source_target_pairs={{0,8},{1,9},{2,10},{3,11},{4,12},{5,13},{6,14},{7,15},{8,16},{9,17... | collective-permute-start | bytes 1966088 | tf_op jit(solution)/shard_map/ppermute | solution.py:45
  58.8 36.5 %collective-permute-start.3 = (bf16[4,80,1024]{2,1,0:T(8,128)(2,1)S(1)}, bf16[4,80,1024]{2,1,0:T(8,128)(2,1)}, u32[]{:S(2)}, u32[]{:S(2)}) collective-permute-start(bf16[4,80,1024]{2,1,0:T(8,128)(2,1)S(1)} %pad_maximum_fusion.refs_2_), channel_id=1, source_target_pairs={{0,24},{1,25},{2,26},{3,27},{4,28},{5,29},{6,30},{7,31},{8,0},{9,1... | collective-permute-start | bytes 1966088 | tf_op jit(solution)/shard_map/ppermute | solution.py:45
  67.0 32.6 %copy-start.9 = (bf16[4,80,1024]{2,1,0:T(8,128)(2,1)}, bf16[4,80,1024]{2,1,0:T(8,128)(2,1)S(1)}, u32[]{:S(2)}) copy-start(bf16[4,80,1024]{2,1,0:T(8,128)(2,1)S(1)} %collective-permute-done.16.refs_6_) | copy-start | bytes 1966084
  67.8 36.0 %collective-permute-start.17 = (bf16[2,80,1024]{2,1,0:T(8,128)(2,1)}, bf16[2,80,1024]{2,1,0:T(8,128)(2,1)S(1)}, u32[]{:S(2)}, u32[]{:S(2)}) collective-permute-start(bf16[2,80,1024]{2,1,0:T(8,128)(2,1)} %slice.79), channel_id=1, source_target_pairs={{0,2},{1,3},{2,4},{3,5},{4,6},{5,7},{6,0},{7,1},{8,10},{9,11},{10,... | collective-permute-start | bytes 983048 | tf_op jit(solution)/shard_map/ppermute | solution.py:45
  71.7 33.9 %collective-permute-start.18 = (bf16[2,80,1024]{2,1,0:T(8,128)(2,1)}, bf16[2,80,1024]{2,1,0:T(8,128)(2,1)}, u32[]{:S(2)}, u32[]{:S(2)}) collective-permute-start(bf16[2,80,1024]{2,1,0:T(8,128)(2,1)} %slice.80), channel_id=1, source_target_pairs={{0,6},{1,7},{2,0},{3,1},{4,2},{5,3},{6,4},{7,5},{8,14},{9,15},{10,... | collective-permute-start | bytes 983048 | tf_op jit(solution)/shard_map/ppermute | solution.py:45
  77.7 30.4 %collective-permute-start.5 = (bf16[2,80,1024]{2,1,0:T(8,128)(2,1)}, bf16[2,80,1024]{2,1,0:T(8,128)(2,1)S(1)}, u32[]{:S(2)}, u32[]{:S(2)}) collective-permute-start(bf16[2,80,1024]{2,1,0:T(8,128)(2,1)} %slice.77), channel_id=1, source_target_pairs={{0,8},{1,9},{2,10},{3,11},{4,12},{5,13},{6,14},{7,15},{8,16},{9,17... | collective-permute-start | bytes 983048 | tf_op jit(solution)/shard_map/ppermute | solution.py:45
  82.0 52.7 %all-to-all-start.2 = ((bf16[16,80,128]{2,1,0:T(8,128)(2,1)}), bf16[16,80,128]{2,1,0:T(8,128)(2,1)}, u32[]{:S(2)}, u32[]{:S(2)}) async-start(bf16[16,80,128]{2,1,0:T(8,128)(2,1)} %broadcast_in_dim.13), calls=%async_computation.2 | async-start | bytes 655360 | tf_op jit(solution)/shard_map/all_to_all | solution.py:21
  96.3 13.8 %collective-permute-start.6 = (bf16[2,80,1024]{2,1,0:T(8,128)(2,1)S(1)}, bf16[2,80,1024]{2,1,0:T(8,128)(2,1)S(1)}, u32[]{:S(2)}, u32[]{:S(2)}) collective-permute-start(bf16[2,80,1024]{2,1,0:T(8,128)(2,1)S(1)} %slice.78), channel_id=1, source_target_pairs={{0,24},{1,25},{2,26},{3,27},{4,28},{5,29},{6,30},{7,31},{8,0},{9,1... | collective-permute-start | bytes 983048 | tf_op jit(solution)/shard_map/ppermute | solution.py:45
  99.6 17.3 %collective-permute-start.23 = (bf16[4,80,1024]{2,1,0:T(8,128)(2,1)S(1)}, bf16[4,80,1024]{2,1,0:T(8,128)(2,1)S(1)}, u32[]{:S(2)}, u32[]{:S(2)}) collective-permute-start(bf16[4,80,1024]{2,1,0:T(8,128)(2,1)S(1)} %collective-permute-done.16.refs_6_), channel_id=1, source_target_pairs={{0,1},{1,0},{2,3},{3,2},{4,5},{5,4},{6,7},{7,6},{8,9},{9,8},{10,11... | collective-permute-start | bytes 1966088 | tf_op jit(solution)/shard_map/ppermute | solution.py:45
  103.7 17.5 %copy-start.19 = (bf16[2,80,1024]{2,1,0:T(8,128)(2,1)}, bf16[2,80,1024]{2,1,0:T(8,128)(2,1)S(1)}, u32[]{:S(2)}) copy-start(bf16[2,80,1024]{2,1,0:T(8,128)(2,1)S(1)} %collective-permute-done.17.refs_4_) | copy-start | bytes 983044
  103.8 15.1 %collective-permute-start.20 = (bf16[4,80,1024]{2,1,0:T(8,128)(2,1)}, bf16[4,80,1024]{2,1,0:T(8,128)(2,1)S(1)}, u32[]{:S(2)}, u32[]{:S(2)}) collective-permute-start(bf16[4,80,1024]{2,1,0:T(8,128)(2,1)} %collective-permute-done.15.refs_3_), channel_id=1, source_target_pairs={{0,1},{1,0},{2,3},{3,2},{4,5},{5,4},{6,7},{7,6},{8,9},{9,8},{10,11... | collective-permute-start | bytes 1966088 | tf_op jit(solution)/shard_map/ppermute | solution.py:45
  105.7 6.8 %collective-permute-start.21 = (bf16[2,80,1024]{2,1,0:T(8,128)(2,1)S(1)}, bf16[2,80,1024]{2,1,0:T(8,128)(2,1)S(1)}, u32[]{:S(2)}, u32[]{:S(2)}) collective-permute-start(bf16[2,80,1024]{2,1,0:T(8,128)(2,1)S(1)} %collective-permute-done.17.refs_4_), channel_id=1, source_target_pairs={{0,1},{1,0},{2,3},{3,2},{4,5},{5,4},{6,7},{7,6},{8,9},{9,8},{10,11... | collective-permute-start | bytes 983048 | tf_op jit(solution)/shard_map/ppermute | solution.py:45
  108.1 19.3 %copy-start.18 = (bf16[2,80,1024]{2,1,0:T(8,128)(2,1)}, bf16[2,80,1024]{2,1,0:T(8,128)(2,1)S(1)}, u32[]{:S(2)}) copy-start(bf16[2,80,1024]{2,1,0:T(8,128)(2,1)S(1)} %collective-permute-done.5.refs_4_) | copy-start | bytes 983044
  108.1 6.3 %collective-permute-start.22 = (bf16[2,80,1024]{2,1,0:T(8,128)(2,1)}, bf16[2,80,1024]{2,1,0:T(8,128)(2,1)S(1)}, u32[]{:S(2)}, u32[]{:S(2)}) collective-permute-start(bf16[2,80,1024]{2,1,0:T(8,128)(2,1)} %collective-permute-done.18.refs_5_), channel_id=1, source_target_pairs={{0,1},{1,0},{2,3},{3,2},{4,5},{5,4},{6,7},{7,6},{8,9},{9,8},{10,11... | collective-permute-start | bytes 983048 | tf_op jit(solution)/shard_map/ppermute | solution.py:45
  110.1 17.3 %copy-start.20 = (bf16[2,80,1024]{2,1,0:T(8,128)(2,1)}, bf16[2,80,1024]{2,1,0:T(8,128)(2,1)S(1)}, u32[]{:S(2)}) copy-start(bf16[2,80,1024]{2,1,0:T(8,128)(2,1)S(1)} %collective-permute-done.6.refs_5_) | copy-start | bytes 983044
  110.1 17.2 %collective-permute-start.7 = (bf16[4,80,1024]{2,1,0:T(8,128)(2,1)S(1)}, bf16[4,80,1024]{2,1,0:T(8,128)(2,1)S(1)}, u32[]{:S(2)}, u32[]{:S(2)}) collective-permute-start(bf16[4,80,1024]{2,1,0:T(8,128)(2,1)S(1)} %pad_maximum_fusion.refs_2_), channel_id=1, source_target_pairs={{0,1},{1,0},{2,3},{3,2},{4,5},{5,4},{6,7},{7,6},{8,9},{9,8},{10,11... | collective-permute-start | bytes 1966088 | tf_op jit(solution)/shard_map/ppermute | solution.py:45
  112.5 8.8 %copy-start.21 = (bf16[2,80,1024]{2,1,0:T(8,128)(2,1)}, bf16[2,80,1024]{2,1,0:T(8,128)(2,1)S(1)}, u32[]{:S(2)}) copy-start(bf16[2,80,1024]{2,1,0:T(8,128)(2,1)S(1)} %collective-permute-done.21.refs_9_) | copy-start | bytes 983044
  112.5 14.8 %collective-permute-start.11 = (bf16[4,80,1024]{2,1,0:T(8,128)(2,1)}, bf16[4,80,1024]{2,1,0:T(8,128)(2,1)S(1)}, u32[]{:S(2)}, u32[]{:S(2)}) collective-permute-start(bf16[4,80,1024]{2,1,0:T(8,128)(2,1)} %collective-permute-done.4.refs_6_), channel_id=1, source_target_pairs={{0,1},{1,0},{2,3},{3,2},{4,5},{5,4},{6,7},{7,6},{8,9},{9,8},{10,11... | collective-permute-start | bytes 1966088 | tf_op jit(solution)/shard_map/ppermute | solution.py:45
  114.5 6.8 %copy-start.22 = (bf16[2,80,1024]{2,1,0:T(8,128)(2,1)}, bf16[2,80,1024]{2,1,0:T(8,128)(2,1)S(1)}, u32[]{:S(2)}) copy-start(bf16[2,80,1024]{2,1,0:T(8,128)(2,1)S(1)} %collective-permute-done.22.refs_10_) | copy-start | bytes 983044
  114.5 12.9 %collective-permute-start.8 = (bf16[4,80,1024]{2,1,0:T(8,128)(2,1)}, bf16[4,80,1024]{2,1,0:T(8,128)(2,1)S(1)}, u32[]{:S(2)}, u32[]{:S(2)}) collective-permute-start(bf16[4,80,1024]{2,1,0:T(8,128)(2,1)} %collective-permute-done.3.refs_3_), channel_id=1, source_target_pairs={{0,1},{1,0},{2,3},{3,2},{4,5},{5,4},{6,7},{7,6},{8,9},{9,8},{10,11... | collective-permute-start | bytes 1966088 | tf_op jit(solution)/shard_map/ppermute | solution.py:45
  116.9 4.4 %copy-start.10 = (bf16[4,80,1024]{2,1,0:T(8,128)(2,1)}, bf16[4,80,1024]{2,1,0:T(8,128)(2,1)S(1)}, u32[]{:S(2)}) copy-start(bf16[4,80,1024]{2,1,0:T(8,128)(2,1)S(1)} %collective-permute-done.23.refs_11_) | copy-start | bytes 1966084
  116.9 10.4 %collective-permute-start.9 = (bf16[2,80,1024]{2,1,0:T(8,128)(2,1)S(1)}, bf16[2,80,1024]{2,1,0:T(8,128)(2,1)S(1)}, u32[]{:S(2)}, u32[]{:S(2)}) collective-permute-start(bf16[2,80,1024]{2,1,0:T(8,128)(2,1)S(1)} %collective-permute-done.5.refs_4_), channel_id=1, source_target_pairs={{0,1},{1,0},{2,3},{3,2},{4,5},{5,4},{6,7},{7,6},{8,9},{9,8},{10,11... | collective-permute-start | bytes 983048 | tf_op jit(solution)/shard_map/ppermute | solution.py:45
  118.8 2.5 %copy-start.12 = (bf16[4,80,1024]{2,1,0:T(8,128)(2,1)}, bf16[4,80,1024]{2,1,0:T(8,128)(2,1)S(1)}, u32[]{:S(2)}) copy-start(bf16[4,80,1024]{2,1,0:T(8,128)(2,1)S(1)} %collective-permute-done.20.refs_8_) | copy-start | bytes 1966084
  118.8 8.5 %collective-permute-start.10 = (bf16[2,80,1024]{2,1,0:T(8,128)(2,1)S(1)}, bf16[2,80,1024]{2,1,0:T(8,128)(2,1)S(1)}, u32[]{:S(2)}, u32[]{:S(2)}) collective-permute-start(bf16[2,80,1024]{2,1,0:T(8,128)(2,1)S(1)} %collective-permute-done.6.refs_5_), channel_id=1, source_target_pairs={{0,1},{1,0},{2,3},{3,2},{4,5},{5,4},{6,7},{7,6},{8,9},{9,8},{10,11... | collective-permute-start | bytes 983048 | tf_op jit(solution)/shard_map/ppermute | solution.py:45
  127.3 1.2 copy-start.13
  127.4 1.4 copy-start.14
  154.1 44.1 %copy-start = (f32[160,160]{1,0:T(8,128)S(1)}, f32[160,160]{1,0:T(8,128)}, u32[]{:S(2)}) copy-start(f32[160,160]{1,0:T(8,128)} %query_weight.1) | copy-start | bytes 307204
  179.1 19.1 %all-to-all-start.5 = ((bf16[32,48,128]{2,1,0:T(8,128)(2,1)}), bf16[32,48,128]{2,1,0:T(8,128)(2,1)}, u32[]{:S(2)}, u32[]{:S(2)}) async-start(bf16[32,48,128]{2,1,0:T(8,128)(2,1)} %broadcast_in_dim.15), calls=%async_computation.5 | async-start | bytes 786432 | tf_op jit(solution)/shard_map/all_to_all | solution.py:21
  (5 other events, 4.6 us)

commit v7 on v5

--- a/solution.py
+++ b/solution.py
@@ -19,10 +19,6 @@
 
 def exchange(array, axis, groups=None):
     return lax.all_to_all(array, axis, 0, 0, tiled=True, axis_index_groups=groups)
-
-
-def from_everyone(array, axis):
-    return exchange(copies(array, lax.axis_size(axis)), axis)
 
 
 def split_high_low(array):
@@ -169,12 +165,78 @@
     )(shard, *in_hbm(inputs.T, error[0], jnp.swapaxes(factors, 1, 2), *blocks), *in_vmem(*lefts))
 
 
+def inverse_kernel(grams, lefts, rows):
+    rank = grams.shape[0]
+    lane = lax.broadcasted_iota(jnp.int32, (rank, 4 * rank), 1)
+    row = lax.broadcasted_iota(jnp.int32, (rank, 4 * rank), 0)
+    given = grams[...]
+    unit = (row[:, :rank] == lane[:, :rank]).astype(F32)
+    state = jnp.concatenate(
+        [
+            given[:, :rank] + given[:, rank : 2 * rank],
+            unit,
+            given[:, 2 * rank : 3 * rank] + given[:, 3 * rank :],
+            unit,
+        ],
+        axis=1,
+    )
+    query = lane < 2 * rank
+    for k in range(rank):
+        column = jnp.where(
+            query, state[:, k : k + 1], state[:, 2 * rank + k : 2 * rank + k + 1]
+        )
+        pivot = state[k : k + 1, :] / column[k : k + 1, :]
+        state = jnp.where(row == k, pivot, state - column * pivot)
+    for i in range(2):
+        inverse = state[:, (2 * i + 1) * rank : (2 * i + 2) * rank]
+        product = jnp.dot(lefts[i], inverse, precision=HIGH, preferred_element_type=F32)
+        rows[i] = jnp.concatenate(split_high_low(product), axis=1)
+
+
+def weighted_lefts(grams, lefts):
+    vmem = pl.BlockSpec(memory_space=pltpu.VMEM)
+    return pl.pallas_call(
+        inverse_kernel,
+        out_shape=pltpu.VMEM((*lefts.shape[:2], 2 * lefts.shape[2]), BF16),
+        in_specs=[vmem, vmem],
+        out_specs=vmem,
+        compiler_params=pltpu.CompilerParams(vmem_limit_bytes=8 << 20),
+    )(grams, lefts)
+
+
 TILE = 16
 
 
 def tile_of(group, block, blocks, per_shard):
     at = group * blocks + block
     return at // per_shard, at % per_shard * TILE
+
+
+def sum_kernel(scale, arrived, copies_out, *rest):
+    total = arrived[0].astype(F32)
+    for r in range(1, arrived.shape[0]):
+        total += arrived[r].astype(F32)
+    depth = copies_out.shape[1]
+    share = (total[:depth] * scale).astype(BF16)
+    for r in range(copies_out.shape[0]):
+        copies_out[r] = share
+    for kept in rest:
+        kept[...] = total[depth:]
+
+
+def summed(arrived, receivers, depth, scale):
+    vmem = pl.BlockSpec(memory_space=pltpu.VMEM)
+    kept = arrived.shape[1] - depth
+    out = [pltpu.HBM((receivers, depth, 128), BF16)]
+    if kept:
+        out.append(pltpu.HBM((kept, 128), F32))
+    return pl.pallas_call(
+        functools.partial(sum_kernel, scale),
+        out_shape=out,
+        in_specs=[vmem],
+        out_specs=[vmem] * len(out),
+        compiler_params=pltpu.CompilerParams(vmem_limit_bytes=8 << 20),
+    )(arrived)
 
 
 def term_kernel(scale, arrived, *refs):
@@ -238,8 +300,8 @@
     return pl.pallas_call(
         functools.partial(term_kernel, 1.0 / replicas),
         out_shape=(
-            jax.ShapeDtypeStruct((shards, depth, 128), BF16),
-            jax.ShapeDtypeStruct((2, rows, rank), F32),
+            pltpu.HBM((shards, depth, 128), BF16),
+            pltpu.HBM((2, rows, rank), F32),
         ),
         in_specs=[vmem] * 3,
         out_specs=(vmem, vmem),
@@ -249,7 +311,13 @@
 
 def finish_kernel(replica, arrived, rows, query_weight, output_weight, *refs):
     fulls, errors_out = refs[:2], refs[2:4]
-    weights_out, (cols, errors, sent) = refs[4:6], refs[6:]
+    weights_out, (cols, errors, sent, weights, given) = refs[4:6], refs[6:]
+    priors = [
+        pltpu.make_async_copy(w, weights.at[i], given.at[i])
+        for i, w in enumerate((query_weight, output_weight))
+    ]
+    for prior in priors:
+        prior.start()
     chunks = 4
     full_width = cols.shape[1]
     width = full_width // chunks
@@ -280,10 +348,11 @@
     base = jnp.minimum(at // 128 * 128, full_width - window)
     own = cols[:, pl.ds(pl.multiple_of(base, 128), window)].astype(F32)
     own = pltpu.roll(own, window - (at - base), 1)[:, :span].astype(BF16)
-    for i, weight in enumerate((query_weight, output_weight)):
+    for i in range(2):
         right = own[i * rank : (i + 1) * rank]
         approx = contract(rows[i], jnp.concatenate([right, right], axis=0), (1, 0))
-        weights_out[i][...] = weight[...] - approx
+        priors[i].wait()
+        weights_out[i][...] = weights[i] - approx
     for i, c in each:
         result(i, c).wait()
 
@@ -299,25 +368,28 @@
             *[jax.ShapeDtypeStruct((1, height, width), BF16)] * 2,
             *[jax.ShapeDtypeStruct(weights[0].shape, F32)] * 2,
         ),
-        in_specs=[pl.BlockSpec(memory_space=pltpu.SMEM), *[vmem] * 6],
+        in_specs=[
+            pl.BlockSpec(memory_space=pltpu.SMEM),
+            vmem,
+            vmem,
+            *[pl.BlockSpec(memory_space=pltpu.HBM)] * 2,
+            vmem,
+            vmem,
+        ],
         out_specs=(anywhere, anywhere, vmem, vmem),
         scratch_shapes=[
             pltpu.VMEM((2 * rank, width), BF16),
             pltpu.VMEM((2, height, width), BF16),
             pltpu.SemaphoreType.DMA((2, 4)),
+            pltpu.VMEM((2, *weights[0].shape), F32),
+            pltpu.SemaphoreType.DMA((2,)),
         ],
         compiler_params=pltpu.CompilerParams(vmem_limit_bytes=16 << 20),
-    )(replica, *in_vmem(arrived), rows, *weights, *in_vmem(*fulls))
+    )(replica, arrived, *in_vmem(rows), *in_hbm(*weights), *in_vmem(*fulls))
 
 
 def contract(a, b, dims):
     return lax.dot_general(a, b, ((dims[:1], dims[1:]), ((), ())), preferred_element_type=F32)
-
-
-def inverse_factor(gram):
-    chol = jnp.linalg.cholesky(gram)
-    eye = jnp.eye(gram.shape[0], dtype=F32)
-    return lax.linalg.triangular_solve(chol, eye, left_side=True, lower=True)
 
 
 def step(
@@ -364,24 +436,15 @@
     )
 
     sent, lefts = terms(exchange(lefts, "dp"), query_full, output_full, replicas, shards)
-    arrived = exchange(sent, "shard").astype(F32).sum(axis=0)
-    share, gram_parts = arrived[:-rank], arrived[-rank:]
-
-    shares = from_everyone(share.astype(BF16), "dp")
-    share = shares.astype(F32).sum(axis=0) / F32(replicas)
-
-    def weighted(left, gram):
-        inverse = inverse_factor(gram)
-        ortho = lax.dot_general(left, inverse, (((1,), (1,)), ((), ())), precision=HIGH)
-        high, low = split_high_low(jnp.dot(ortho, inverse, precision=HIGH))
-        return jnp.concatenate([high, low], axis=1)
-
-    query_rows = weighted(lefts[0], gram_parts[:, :rank] + gram_parts[:, rank : 2 * rank])
-    output_rows = weighted(lefts[1], gram_parts[:, 2 * rank : 3 * rank] + gram_parts[:, 3 * rank :])
-    cols = from_everyone(share.astype(BF16), "shard")
+    depth = sent.shape[1] - rank
+    shares, grams = summed(exchange(sent, "shard"), replicas, depth, 1.0)
+    shares = exchange(shares, "dp")
+    weighted = weighted_lefts(grams, lefts)
+    (cols,) = summed(shares, shards, depth, 1.0 / replicas)
+    cols = exchange(cols, "shard")
     return finish(
         cols,
-        jnp.stack([query_rows, output_rows]),
+        weighted,
         (query_full, output_full),
         (query_weight, output_weight),
         replica,

time: 243 us -> 221 us (0.909)
  blocking collectives: 78.6 us -> 120 us
  waiting for transfers between devices: 42.1 us -> 22.2 us
  other arithmetic: 19.6 us -> 0.08 us
  starting transfers between devices: 66.8 us -> 50.4 us
  local copies, waits for them, and re-layouts: 11 us -> 2.1 us
  Pallas kernels: 17.8 us -> 24 us
  matrix products: 4.54 us -> 0 us
    all_to_all x3 -> x5, blocking collectives: 78.6 us -> 120 us  [exchange(): lax.all_to_all(array, axis, 0, 0, tiled=True, axis_index_groups=groups)]
    all_to_all x3 -> x1, waiting for transfers between devices: 26.4 us -> 6.32 us  [exchange(): lax.all_to_all(array, axis, 0, 0, tiled=True, axis_index_groups=groups)]
    all_to_all x3 -> x1, starting transfers between devices: 25.1 us -> 8.8 us  [exchange(): lax.all_to_all(array, axis, 0, 0, tiled=True, axis_index_groups=groups)]
    another operation x12 -> x0, other arithmetic: 14.9 us -> none  [the longest x6 7.2 us: inverse_factor(): chol = jnp.linalg.cholesky(gram)]
    pallas_call x0 -> x3, Pallas kernels: none -> 4.79 us  [the longest x1 3.25 us: weighted_lefts(): pl.pallas_call(inverse_kernel, out_shape=pltpu.VMEM((*lefts.shape[:2], 2...]
    dot_general x4 -> x0, matrix products: 3.37 us -> none  [the longest x2 2.31 us: weighted(): lax.dot_general(left, inverse, (((1,), (1,)), ((), ())), precision=HIGH)]
    unnamed x26 -> x18, local copies, waits for them, and re-layouts: 3.44 us -> 0.75 us
  transfers between devices with their start and end apart: 16 -> 14, of which waited for: 8 -> 6; matrix products, arithmetic and copies ran while one was open for 4% -> 0% of each run, Pallas kernels for 3% -> 5%
where the time goes in v7:
time: 221 us; the launch traced here: 220 us
  blocking collectives  120 us (54%)
  starting transfers between devices  50.4 us (23%)
  Pallas kernels  24 us (11%)
  waiting for transfers between devices  22.2 us (10%)
    all_to_all x5, blocking collectives, exchange(): lax.all_to_all(array, axis, 0, 0, tiled=True, axis_index_groups=groups)  120 us
    ppermute x13, starting transfers between devices, send(): return lax.ppermute(array, 'shard', in_plane(rows, cols, core))  41.6 us
    ppermute x13, waiting for transfers between devices, send(): return lax.ppermute(array, 'shard', in_plane(rows, cols, core))  15.8 us
    pallas_call x2, Pallas kernels, full_gradient(): pl.pallas_call(functools.partial(gradient_kernel, factor), out_shape=(plt...  13.6 us
    all_to_all x1, starting transfers between devices, exchange(): lax.all_to_all(array, axis, 0, 0, tiled=True, axis_index_groups=groups)  8.8 us
    all_to_all x1, waiting for transfers between devices, exchange(): lax.all_to_all(array, axis, 0, 0, tiled=True, axis_index_groups=groups)  6.32 us
  transfers between devices with their start and end apart: 14, of which 6 were waited for; matrix products, arithmetic and copies ran while one was open for 0% of the time, Pallas kernels for 5%

profile of v7, /device:TPU:1, one launch (start us, length us, event | category | flops | bytes accessed | tf_op | source)
XLA Modules:
  0.0 219.6 jit_solution(2403334369387668930)
XLA Ops:
  0.6 1.0 broadcast_in_dim.6
  1.6 12.3 %all_to_all.30 = bf16[4,80,1024]{2,1,0:T(8,128)(2,1)S(1)} all-to-all(bf16[4,80,1024]{2,1,0:T(8,128)(2,1)S(1)} %broadcast_in_dim.6), channel_id=1, replica_groups={{0,2,4,6},{1,3,5,7},{8,10,12,14},{9,11,13,15},{16,18,20,22},{17,19,21,2..., dimensions={0} | all-to-all | bytes 1310720 | tf_op jit(solution)/shard_map/all_to_all | solution.py:21
  13.9 0.3 broadcast_in_dim.7
  14.2 0.0 copy-start.8
  14.2 36.1 %all_to_all.31.refs_3_ = bf16[4,4,80,1024]{3,2,1,0:T(8,128)(2,1)} all-to-all(bf16[4,4,80,1024]{3,2,1,0:T(8,128)(2,1)S(1)} %broadcast_in_dim.7), channel_id=1, replica_groups={{0,8,16,24},{1,9,17,25},{2,10,18,26},{3,11,19,27},{4,12,20,28},{5,13,21..., dimensions={0} | all-to-all | bytes 5242880 | tf_op jit(solution)/shard_map/all_to_all | solution.py:21
  50.3 5.3 %collective-permute-start = (bf16[4,4,80,1024]{3,2,1,0:T(8,128)(2,1)}, bf16[4,4,80,1024]{3,2,1,0:T(8,128)(2,1)}, u32[]{:S(2)}, u32[]{:S(2)}) collective-permute-start(bf16[4,4,80,1024]{3,2,1,0:T(8,128)(2,1)} %all_to_all.31.refs_3_), channel_id=1, source_target_pairs={{0,1},{1,0},{2,3},{3,2},{4,5},{5,4},{6,7},{7,6},{8,9},{9,8},{10,11... | collective-permute-start | bytes 7864328 | tf_op jit(solution)/shard_map/ppermute | solution.py:41
  55.7 2.4 %collective-permute-start.2 = (bf16[80,1024]{1,0:T(8,128)(2,1)S(1)}, bf16[80,1024]{1,0:T(8,128)(2,1)S(1)}, u32[]{:S(2)}, u32[]{:S(2)}) collective-permute-start(bf16[80,1024]{1,0:T(8,128)(2,1)S(1)} %bitcast.20), channel_id=1, source_target_pairs={{0,16},{1,17},{2,18},{3,19},{4,20},{5,21},{6,22},{7,23},{8,24},{9,... | collective-permute-start | bytes 491528 | tf_op jit(solution)/shard_map/ppermute | solution.py:41
  58.1 4.0 %collective-permute-start.1 = (bf16[80,1024]{1,0:T(8,128)(2,1)S(1)}, bf16[80,1024]{1,0:T(8,128)(2,1)S(1)}, u32[]{:S(2)}, u32[]{:S(2)}) collective-permute-start(bf16[80,1024]{1,0:T(8,128)(2,1)S(1)} %bitcast.21), channel_id=1, source_target_pairs={{0,24},{1,25},{2,26},{3,27},{4,28},{5,29},{6,30},{7,31},{8,0},{9,1... | collective-permute-start | bytes 491528 | tf_op jit(solution)/shard_map/ppermute | solution.py:41
  62.2 1.9 collective-permute-start.3
  64.1 0.7 collective-permute-done.2
  64.8 2.0 collective-permute-done.1
  66.8 3.6 %collective-permute-done.3 = bf16[80,1024]{1,0:T(8,128)(2,1)S(1)} collective-permute-done((bf16[80,1024]{1,0:T(8,128)(2,1)S(1)}, bf16[80,1024]{1,0:T(8,128)(2,1)S(1)}, u32[]{:S(2)}, u32[]{:S(2)}) %collective-permute-start.3) | collective-permute-done | bytes 163872 | tf_op jit(solution)/shard_map/ppermute | solution.py:41
  70.5 0.1 pad_maximum_fusion.refs_3_
  70.5 0.0 copy-start.2
  70.6 2.2 collective-permute-start.5
  72.8 4.3 %collective-permute-start.4 = (bf16[4,80,1024]{2,1,0:T(8,128)(2,1)S(1)}, bf16[4,80,1024]{2,1,0:T(8,128)(2,1)S(1)}, u32[]{:S(2)}, u32[]{:S(2)}) collective-permute-start(bf16[4,80,1024]{2,1,0:T(8,128)(2,1)S(1)} %pad_maximum_fusion.refs_3_), channel_id=1, source_target_pairs={{0,6},{1,7},{2,0},{3,1},{4,2},{5,3},{6,4},{7,5},{8,14},{9,15},{10,... | collective-permute-start | bytes 1966088 | tf_op jit(solution)/shard_map/ppermute | solution.py:41
  77.1 3.9 %collective-permute-start.8 = (bf16[4,80,1024]{2,1,0:T(8,128)(2,1)S(1)}, bf16[4,80,1024]{2,1,0:T(8,128)(2,1)S(1)}, u32[]{:S(2)}, u32[]{:S(2)}) collective-permute-start(bf16[4,80,1024]{2,1,0:T(8,128)(2,1)S(1)} %pad_maximum_fusion.refs_3_), channel_id=1, source_target_pairs={{0,1},{1,0},{2,3},{3,2},{4,5},{5,4},{6,7},{7,6},{8,9},{9,8},{10,11... | collective-permute-start | bytes 1966088 | tf_op jit(solution)/shard_map/ppermute | solution.py:41
  81.0 7.5 %collective-permute-done.5.refs_7_ = bf16[4,80,1024]{2,1,0:T(8,128)(2,1)S(1)} collective-permute-done((bf16[4,80,1024]{2,1,0:T(8,128)(2,1)S(1)}, bf16[4,80,1024]{2,1,0:T(8,128)(2,1)S(1)}, u32[]{:S(2)}, u32[]{:S(2)}) %collective-permute-start.5) | collective-permute-done | bytes 655392 | tf_op jit(solution)/shard_map/ppermute | solution.py:41
  88.6 1.9 collective-permute-start.6
  90.5 0.0 collective-permute-done.4.refs_4_
  90.5 0.0 copy-start.4
  90.5 4.6 %collective-permute-start.7 = (bf16[2,80,1024]{2,1,0:T(8,128)(2,1)S(1)}, bf16[2,80,1024]{2,1,0:T(8,128)(2,1)}, u32[]{:S(2)}, u32[]{:S(2)}) collective-permute-start(bf16[2,80,1024]{2,1,0:T(8,128)(2,1)S(1)} %slice.9), channel_id=1, source_target_pairs={{0,6},{1,7},{2,0},{3,1},{4,2},{5,3},{6,4},{7,5},{8,14},{9,15},{10,... | collective-permute-start | bytes 983048 | tf_op jit(solution)/shard_map/ppermute | solution.py:41
  95.1 4.8 %collective-permute-start.12 = (bf16[4,80,1024]{2,1,0:T(8,128)(2,1)S(1)}, bf16[4,80,1024]{2,1,0:T(8,128)(2,1)}, u32[]{:S(2)}, u32[]{:S(2)}) collective-permute-start(bf16[4,80,1024]{2,1,0:T(8,128)(2,1)S(1)} %collective-permute-done.5.refs_7_), channel_id=1, source_target_pairs={{0,1},{1,0},{2,3},{3,2},{4,5},{5,4},{6,7},{7,6},{8,9},{9,8},{10,11... | collective-permute-start | bytes 1966088 | tf_op jit(solution)/shard_map/ppermute | solution.py:41
  99.9 0.0 collective-permute-done.8.refs_8_
  99.9 1.9 collective-permute-start.9
  101.8 0.0 collective-permute-done.6.refs_5_
  101.9 2.4 %collective-permute-start.10 = (bf16[2,80,1024]{2,1,0:T(8,128)(2,1)S(1)}, bf16[2,80,1024]{2,1,0:T(8,128)(2,1)S(1)}, u32[]{:S(2)}, u32[]{:S(2)}) collective-permute-start(bf16[2,80,1024]{2,1,0:T(8,128)(2,1)S(1)} %collective-permute-done.6.refs_5_), channel_id=1, source_target_pairs={{0,1},{1,0},{2,3},{3,2},{4,5},{5,4},{6,7},{7,6},{8,9},{9,8},{10,11... | collective-permute-start | bytes 983048 | tf_op jit(solution)/shard_map/ppermute | solution.py:41
  104.3 0.0 collective-permute-done.7.refs_6_
  104.3 1.9 collective-permute-start.11
  106.2 0.0 collective-permute-done.10.refs_10_
  106.2 1.9 collective-permute-done.11.refs_11_
  108.1 0.0 collective-permute-done.12.refs_12_
  108.1 0.0 collective-permute-done.9.refs_9_
  108.2 6.8 %shard_map.120 = (f32[160,2560]{1,0:T(8,128)S(1)}, f32[160,32]{1,0:T(8,128)S(1)}) custom-call(s32[1]{0:T(128)} %bitcast.1.shard, bf16[160,1024]{1,0:T(8,128)(2,1)} %bitcast.18, bf16[160,2560]{1,0:T(8,128)(2,1)} %bitcast.16, bf16[2,32,2560]{2,1,0:T(8,128)(2,1)} %bitcast.14, bf16[4,80,1024]{2,1,0:T(8,128)(2,1)} %copy-done.2, bf16[4,80,1024]{2,1,0:T(8,128)(2,1)} %copy-done.4, ...), custom_call_target="tpu_custom_call" | custom-call | tf_op jit(solution)/shard_map/pallas_call | solution.py:145
  115.0 0.0 collective-permute-done.refs_4_
  115.0 6.8 %shard_map.121 = (f32[160,2560]{1,0:T(8,128)S(1)}, bf16[16,80,128]{2,1,0:T(8,128)(2,1)S(1)}) custom-call(s32[1]{0:T(128)} %bitcast.1.shard, bf16[160,1024]{1,0:T(8,128)(2,1)} %bitcast.19, bf16[160,2560]{1,0:T(8,128)(2,1)} %bitcast.17, bf16[2,32,2560]{2,1,0:T(8,128)(2,1)} %bitcast.15, bf16[4,4,80,1024]{3,2,1,0:T(8,128)(2,1)} %all_to_all.31.refs_3_, ...), custom_call_target="tpu_custom_call" | custom-call | tf_op jit(solution)/shard_map/pallas_call | solution.py:145
  121.9 30.3 %all_to_all.32.arrived = bf16[16,80,128]{2,1,0:T(8,128)(2,1)S(1)} all-to-all(bf16[16,80,128]{2,1,0:T(8,128)(2,1)S(1)} %get-tuple-element.13), channel_id=1, replica_groups=mesh['dp'=16,'shard'=32] {'dp'}, dimensions={0} | all-to-all | bytes 655360 | tf_op jit(solution)/shard_map/all_to_all | solution.py:21
  152.1 1.9 shard_map.122
  154.1 23.1 %all_to_all.33.arrived = bf16[32,80,128]{2,1,0:T(8,128)(2,1)S(1)} all-to-all(bf16[32,80,128]{2,1,0:T(8,128)(2,1)} %get-tuple-element.16), channel_id=1, replica_groups=mesh['dp'=16,'shard'=32] {'shard'}, dimensions={0} | all-to-all | bytes 1310720 | tf_op jit(solution)/shard_map/all_to_all | solution.py:21
  177.2 0.7 shard_map.123
  177.9 18.0 %all_to_all.34.arrived = bf16[16,48,128]{2,1,0:T(8,128)(2,1)S(1)} all-to-all(bf16[16,48,128]{2,1,0:T(8,128)(2,1)} %get-tuple-element.17), channel_id=1, replica_groups=mesh['dp'=16,'shard'=32] {'dp'}, dimensions={0} | all-to-all | bytes 393216 | tf_op jit(solution)/shard_map/all_to_all | solution.py:21
  196.0 0.8 shard_map.124
  196.8 8.8 %all-to-all-start.5 = ((bf16[32,48,128]{2,1,0:T(8,128)(2,1)}), bf16[32,48,128]{2,1,0:T(8,128)(2,1)}, u32[]{:S(2)}, u32[]{:S(2)}) async-start(bf16[32,48,128]{2,1,0:T(8,128)(2,1)} %shard_map.124), calls=%async_computation.5 | async-start | bytes 786432 | tf_op jit(solution)/shard_map/all_to_all | solution.py:21
  205.6 0.0 copy-start.1
  205.6 0.7 copy-done.1
  206.3 3.3 %shard_map.125.rows = bf16[2,160,64]{2,1,0:T(8,128)(2,1)S(1)} custom-call(f32[32,128]{1,0:T(8,128)S(1)} %copy-done.1, f32[2,160,32]{2,1,0:T(8,128)S(1)} %copy-done), custom_call_target="tpu_custom_call" | custom-call | tf_op jit(solution)/shard_map/pallas_call | solution.py:198
  209.6 6.3 %all-to-all-done.5.arrived = bf16[32,48,128]{2,1,0:T(8,128)(2,1)} async-done(((bf16[32,48,128]{2,1,0:T(8,128)(2,1)}), bf16[32,48,128]{2,1,0:T(8,128)(2,1)}, u32[]{:S(2)}, u32[]{:S(2)}) %all-to-all-start.5) | async-done | bytes 393248 | tf_op jit(solution)/shard_map/all_to_all | solution.py:21
  215.9 3.7 %shard_map.126 = (bf16[1,160,2560]{2,1,0:T(8,128)(2,1)}, bf16[1,160,2560]{2,1,0:T(8,128)(2,1)}, f32[160,160]{1,0:T(8,128)}, f32[160,160]{1,0:T(8,128)}) custom-call(s32[1]{0:T(128)} %bitcast.replica, bf16[32,48,128]{2,1,0:T(8,128)(2,1)} %all-to-all-done.5.arrived, bf16[2,160,64]{2,1,0:T(8,128)(2,1)S(1)} %shard_map.125.rows, f32[160,160]{1,0:T(8,128)} %query_weight.1, ...), custom_call_target="tpu_custom_call" | custom-call | tf_op jit(solution)/shard_map/pallas_call | solution.py:365
  (15 shorter events, 0.1 us)
Async XLA Ops:
  14.2 41.4 %copy-start.8 = (bf16[1024,80]{0,1:T(8,128)(2,1)S(1)}, bf16[1024,80]{0,1:T(8,128)(2,1)}, u32[]{:S(2)}) copy-start(bf16[1024,80]{0,1:T(8,128)(2,1)} %param.12) | copy-start | bytes 491524
  50.3 64.7 %collective-permute-start = (bf16[4,4,80,1024]{3,2,1,0:T(8,128)(2,1)}, bf16[4,4,80,1024]{3,2,1,0:T(8,128)(2,1)}, u32[]{:S(2)}, u32[]{:S(2)}) collective-permute-start(bf16[4,4,80,1024]{3,2,1,0:T(8,128)(2,1)} %all_to_all.31.refs_3_), channel_id=1, source_target_pairs={{0,1},{1,0},{2,3},{3,2},{4,5},{5,4},{6,7},{7,6},{8,9},{9,8},{10,11... | collective-permute-start | bytes 7864328 | tf_op jit(solution)/shard_map/ppermute | solution.py:41
  55.7 9.1 %collective-permute-start.2 = (bf16[80,1024]{1,0:T(8,128)(2,1)S(1)}, bf16[80,1024]{1,0:T(8,128)(2,1)S(1)}, u32[]{:S(2)}, u32[]{:S(2)}) collective-permute-start(bf16[80,1024]{1,0:T(8,128)(2,1)S(1)} %bitcast.20), channel_id=1, source_target_pairs={{0,16},{1,17},{2,18},{3,19},{4,20},{5,21},{6,22},{7,23},{8,24},{9,... | collective-permute-start | bytes 491528 | tf_op jit(solution)/shard_map/ppermute | solution.py:41
  58.1 8.7 %collective-permute-start.1 = (bf16[80,1024]{1,0:T(8,128)(2,1)S(1)}, bf16[80,1024]{1,0:T(8,128)(2,1)S(1)}, u32[]{:S(2)}, u32[]{:S(2)}) collective-permute-start(bf16[80,1024]{1,0:T(8,128)(2,1)S(1)} %bitcast.21), channel_id=1, source_target_pairs={{0,24},{1,25},{2,26},{3,27},{4,28},{5,29},{6,30},{7,31},{8,0},{9,1... | collective-permute-start | bytes 491528 | tf_op jit(solution)/shard_map/ppermute | solution.py:41
  62.2 8.3 %collective-permute-start.3 = (bf16[80,1024]{1,0:T(8,128)(2,1)S(1)}, bf16[80,1024]{1,0:T(8,128)(2,1)S(1)}, u32[]{:S(2)}, u32[]{:S(2)}) collective-permute-start(bf16[80,1024]{1,0:T(8,128)(2,1)S(1)} %bitcast.22), channel_id=1, source_target_pairs={{0,8},{1,9},{2,10},{3,11},{4,12},{5,13},{6,14},{7,15},{8,16},{9,17... | collective-permute-start | bytes 491528 | tf_op jit(solution)/shard_map/ppermute | solution.py:41
  70.5 37.6 %copy-start.2 = (bf16[4,80,1024]{2,1,0:T(8,128)(2,1)}, bf16[4,80,1024]{2,1,0:T(8,128)(2,1)S(1)}, u32[]{:S(2)}) copy-start(bf16[4,80,1024]{2,1,0:T(8,128)(2,1)S(1)} %pad_maximum_fusion.refs_3_) | copy-start | bytes 1966084
  70.6 18.0 %collective-permute-start.5 = (bf16[4,80,1024]{2,1,0:T(8,128)(2,1)S(1)}, bf16[4,80,1024]{2,1,0:T(8,128)(2,1)S(1)}, u32[]{:S(2)}, u32[]{:S(2)}) collective-permute-start(bf16[4,80,1024]{2,1,0:T(8,128)(2,1)S(1)} %pad_maximum_fusion.refs_3_), channel_id=1, source_target_pairs={{0,2},{1,3},{2,4},{3,5},{4,6},{5,7},{6,0},{7,1},{8,10},{9,11},{10,... | collective-permute-start | bytes 1966088 | tf_op jit(solution)/shard_map/ppermute | solution.py:41
  72.8 17.7 %collective-permute-start.4 = (bf16[4,80,1024]{2,1,0:T(8,128)(2,1)S(1)}, bf16[4,80,1024]{2,1,0:T(8,128)(2,1)S(1)}, u32[]{:S(2)}, u32[]{:S(2)}) collective-permute-start(bf16[4,80,1024]{2,1,0:T(8,128)(2,1)S(1)} %pad_maximum_fusion.refs_3_), channel_id=1, source_target_pairs={{0,6},{1,7},{2,0},{3,1},{4,2},{5,3},{6,4},{7,5},{8,14},{9,15},{10,... | collective-permute-start | bytes 1966088 | tf_op jit(solution)/shard_map/ppermute | solution.py:41
  77.1 22.8 %collective-permute-start.8 = (bf16[4,80,1024]{2,1,0:T(8,128)(2,1)S(1)}, bf16[4,80,1024]{2,1,0:T(8,128)(2,1)S(1)}, u32[]{:S(2)}, u32[]{:S(2)}) collective-permute-start(bf16[4,80,1024]{2,1,0:T(8,128)(2,1)S(1)} %pad_maximum_fusion.refs_3_), channel_id=1, source_target_pairs={{0,1},{1,0},{2,3},{3,2},{4,5},{5,4},{6,7},{7,6},{8,9},{9,8},{10,11... | collective-permute-start | bytes 1966088 | tf_op jit(solution)/shard_map/ppermute | solution.py:41
  88.5 19.7 %copy-start.3 = (bf16[4,80,1024]{2,1,0:T(8,128)(2,1)}, bf16[4,80,1024]{2,1,0:T(8,128)(2,1)S(1)}, u32[]{:S(2)}) copy-start(bf16[4,80,1024]{2,1,0:T(8,128)(2,1)S(1)} %collective-permute-done.5.refs_7_) | copy-start | bytes 1966084
  88.6 13.3 %collective-permute-start.6 = (bf16[2,80,1024]{2,1,0:T(8,128)(2,1)S(1)}, bf16[2,80,1024]{2,1,0:T(8,128)(2,1)S(1)}, u32[]{:S(2)}, u32[]{:S(2)}) collective-permute-start(bf16[2,80,1024]{2,1,0:T(8,128)(2,1)S(1)} %slice.8), channel_id=1, source_target_pairs={{0,2},{1,3},{2,4},{3,5},{4,6},{5,7},{6,0},{7,1},{8,10},{9,11},{10,... | collective-permute-start | bytes 983048 | tf_op jit(solution)/shard_map/ppermute | solution.py:41
  90.5 17.7 %copy-start.4 = (bf16[4,80,1024]{2,1,0:T(8,128)(2,1)}, bf16[4,80,1024]{2,1,0:T(8,128)(2,1)S(1)}, u32[]{:S(2)}) copy-start(bf16[4,80,1024]{2,1,0:T(8,128)(2,1)S(1)} %collective-permute-done.4.refs_4_) | copy-start | bytes 1966084
  90.5 13.7 %collective-permute-start.7 = (bf16[2,80,1024]{2,1,0:T(8,128)(2,1)S(1)}, bf16[2,80,1024]{2,1,0:T(8,128)(2,1)}, u32[]{:S(2)}, u32[]{:S(2)}) collective-permute-start(bf16[2,80,1024]{2,1,0:T(8,128)(2,1)S(1)} %slice.9), channel_id=1, source_target_pairs={{0,6},{1,7},{2,0},{3,1},{4,2},{5,3},{6,4},{7,5},{8,14},{9,15},{10,... | collective-permute-start | bytes 983048 | tf_op jit(solution)/shard_map/ppermute | solution.py:41
  95.1 13.0 %collective-permute-start.12 = (bf16[4,80,1024]{2,1,0:T(8,128)(2,1)S(1)}, bf16[4,80,1024]{2,1,0:T(8,128)(2,1)}, u32[]{:S(2)}, u32[]{:S(2)}) collective-permute-start(bf16[4,80,1024]{2,1,0:T(8,128)(2,1)S(1)} %collective-permute-done.5.refs_7_), channel_id=1, source_target_pairs={{0,1},{1,0},{2,3},{3,2},{4,5},{5,4},{6,7},{7,6},{8,9},{9,8},{10,11... | collective-permute-start | bytes 1966088 | tf_op jit(solution)/shard_map/ppermute | solution.py:41
  99.9 8.3 %copy-start.5 = (bf16[4,80,1024]{2,1,0:T(8,128)(2,1)}, bf16[4,80,1024]{2,1,0:T(8,128)(2,1)S(1)}, u32[]{:S(2)}) copy-start(bf16[4,80,1024]{2,1,0:T(8,128)(2,1)S(1)} %collective-permute-done.8.refs_8_) | copy-start | bytes 1966084
  99.9 8.2 %collective-permute-start.9 = (bf16[4,80,1024]{2,1,0:T(8,128)(2,1)S(1)}, bf16[4,80,1024]{2,1,0:T(8,128)(2,1)}, u32[]{:S(2)}, u32[]{:S(2)}) collective-permute-start(bf16[4,80,1024]{2,1,0:T(8,128)(2,1)S(1)} %collective-permute-done.4.refs_4_), channel_id=1, source_target_pairs={{0,1},{1,0},{2,3},{3,2},{4,5},{5,4},{6,7},{7,6},{8,9},{9,8},{10,11... | collective-permute-start | bytes 1966088 | tf_op jit(solution)/shard_map/ppermute | solution.py:41
  101.8 6.4 %copy-start.6 = (bf16[2,80,1024]{2,1,0:T(8,128)(2,1)}, bf16[2,80,1024]{2,1,0:T(8,128)(2,1)S(1)}, u32[]{:S(2)}) copy-start(bf16[2,80,1024]{2,1,0:T(8,128)(2,1)S(1)} %collective-permute-done.6.refs_5_) | copy-start | bytes 983044
  101.9 4.4 %collective-permute-start.10 = (bf16[2,80,1024]{2,1,0:T(8,128)(2,1)S(1)}, bf16[2,80,1024]{2,1,0:T(8,128)(2,1)S(1)}, u32[]{:S(2)}, u32[]{:S(2)}) collective-permute-start(bf16[2,80,1024]{2,1,0:T(8,128)(2,1)S(1)} %collective-permute-done.6.refs_5_), channel_id=1, source_target_pairs={{0,1},{1,0},{2,3},{3,2},{4,5},{5,4},{6,7},{7,6},{8,9},{9,8},{10,11... | collective-permute-start | bytes 983048 | tf_op jit(solution)/shard_map/ppermute | solution.py:41
  104.3 3.9 %collective-permute-start.11 = (bf16[2,80,1024]{2,1,0:T(8,128)(2,1)}, bf16[2,80,1024]{2,1,0:T(8,128)(2,1)}, u32[]{:S(2)}, u32[]{:S(2)}) collective-permute-start(bf16[2,80,1024]{2,1,0:T(8,128)(2,1)} %collective-permute-done.7.refs_6_), channel_id=1, source_target_pairs={{0,1},{1,0},{2,3},{3,2},{4,5},{5,4},{6,7},{7,6},{8,9},{9,8},{10,11... | collective-permute-start | bytes 983048 | tf_op jit(solution)/shard_map/ppermute | solution.py:41
  106.2 1.9 copy-start.7
  154.1 51.5 %copy-start = (f32[2,160,32]{2,1,0:T(8,128)S(1)}, f32[2,160,32]{2,1,0:T(8,128)}, u32[]{:S(2)}) copy-start(f32[2,160,32]{2,1,0:T(8,128)} %get-tuple-element.19.lefts) | copy-start | bytes 122884
  196.8 19.1 %all-to-all-start.5 = ((bf16[32,48,128]{2,1,0:T(8,128)(2,1)}), bf16[32,48,128]{2,1,0:T(8,128)(2,1)}, u32[]{:S(2)}, u32[]{:S(2)}) async-start(bf16[32,48,128]{2,1,0:T(8,128)(2,1)} %shard_map.124), calls=%async_computation.5 | async-start | bytes 786432 | tf_op jit(solution)/shard_map/all_to_all | solution.py:21
  205.6 0.7 copy-start.1

commit v8 on v7

--- a/solution.py
+++ b/solution.py
@@ -63,71 +63,72 @@
     return send(array, 0, 0, 1)
 
 
-def gradient_kernel(factor, shard, *refs):
-    acts_in, error_in, start_in, *sources = refs[:-9]
-    full, left, acts, error, start, columns, given, near, done = refs[-9:]
-    in_rings = len(sources) > 3
-    other_left = None if in_rings else sources.pop()
-    mine, theirs = sources[: len(sources) // 2], sources[len(sources) // 2 :]
-    side, each = 4, columns.shape[1] // 8
+def gradient_kernel(shard, *refs):
+    output, query, (start_in, query_full, output_full, lefts) = refs[:12], refs[12:16], refs[16:20]
+    acts, error, start, columns, given, near, done = refs[20:]
+    side, each = 4, columns.shape[2] // 8
     y0, x0, core = shard[0] // 8, shard[0] // 2 % side, shard[0] % 2
+    jobs = [(output, output_full, 1, True), (query, query_full, 0, False)]
 
     def block(refs, j, k):
-        if not in_rings:
+        if len(refs) == 1:
             return refs[0].at[j, k]
         near, right, far_low, far_high, left = refs
         if k == 2:
             return (far_low if j < 2 else far_high).at[j % 2]
         return (near, right, None, left)[k].at[j]
 
-    def fetch(j, k, other):
+    def fetch(refs, job, in_rings, j, k, other):
         x = (x0 + k) % side if in_rings else k
         at = (x * 2 + (1 - core if other else core)) * each
+        count = (len(refs) - 2) // 2
         return pltpu.make_async_copy(
-            block(theirs if other else mine, j, k),
-            columns.at[j, pl.ds(pl.multiple_of(at, 16), each), :],
-            done.at[j, k * 2 + other],
-        )
-
-    def lanes(j):
+            block(refs[2 + count :] if other else refs[2 : 2 + count], j, k),
+            columns.at[job, j, pl.ds(pl.multiple_of(at, 16), each), :],
+            done.at[job, j, k * 2 + other],
+        )
+
+    def lanes(in_rings, j):
         y = (y0 + j) % side if in_rings else j
         return pl.ds(pl.multiple_of(y * (8 * each), 128), 8 * each)
 
-    def prior(j):
-        return pltpu.make_async_copy(error_in.at[:, lanes(j)], error.at[j], near.at[j])
-
-    first = pltpu.make_async_copy(acts_in, acts, given.at[0])
-    second = pltpu.make_async_copy(start_in.at[factor], start, given.at[1])
-    first.start()
+    def prior(refs, job, in_rings, j):
+        here = lanes(in_rings, j)
+        return pltpu.make_async_copy(refs[1].at[:, here], error.at[job, j], near.at[job, j])
+
     steps = [(k, other) for k in range(side) for other in range(2)]
-    for j in range(side):
-        for k, other in steps:
-            fetch(j, k, other).start()
-        prior(j).start()
-        if j == 0:
-            second.start()
-    first.wait()
-    total = jnp.zeros((acts.shape[0], start.shape[0]), F32)
-    for j in range(side):
-        for k, other in steps:
-            fetch(j, k, other).wait()
-        prior(j).wait()
-        if j == 0:
-            second.wait()
-        part = contract(acts[...], columns[j], (1, 1)) + error[j].astype(F32)
-        full[:, lanes(j)] = part
-        high, low = split_high_low(part)
-        rows = start[:, lanes(j)]
-        total += contract(high, rows, (1, 1)) + contract(low, rows, (1, 1))
-    if in_rings:
-        left[...] = total
-    else:
-        half = total.shape[0] // 2
-        packed = jnp.concatenate(
-            [total[:half], other_left[:half], total[half:], other_left[half:]], axis=1
-        ).astype(BF16)
-        for r in range(left.shape[0]):
-            left[r] = packed
+    first = pltpu.make_async_copy(start_in, start, given.at[2])
+    for job, (refs, _, _, in_rings) in enumerate(jobs):
+        pltpu.make_async_copy(refs[0], acts.at[job], given.at[job]).start()
+        for j in range(side):
+            for k, other in steps:
+                fetch(refs, job, in_rings, j, k, other).start()
+            prior(refs, job, in_rings, j).start()
+            if job == 0 and j == 0:
+                first.start()
+    totals = []
+    for job, (refs, full, factor, in_rings) in enumerate(jobs):
+        pltpu.make_async_copy(refs[0], acts.at[job], given.at[job]).wait()
+        total = jnp.zeros((acts.shape[1], start.shape[1]), F32)
+        for j in range(side):
+            for k, other in steps:
+                fetch(refs, job, in_rings, j, k, other).wait()
+            prior(refs, job, in_rings, j).wait()
+            if job == 0 and j == 0:
+                first.wait()
+            part = contract(acts[job], columns[job, j], (1, 1)) + error[job, j].astype(F32)
+            here = lanes(in_rings, j)
+            full[:, here] = part
+            high, low = split_high_low(part)
+            rows = start[factor, :, here]
+            total += contract(high, rows, (1, 1)) + contract(low, rows, (1, 1))
+        totals.append(total)
+    half = acts.shape[1] // 2
+    packed = jnp.concatenate(
+        [totals[1][:half], totals[0][:half], totals[1][half:], totals[0][half:]], axis=1
+    ).astype(BF16)
+    for r in range(lefts.shape[0]):
+        lefts[r] = packed
 
 
 def in_vmem(*arrays):
@@ -138,31 +139,37 @@
     return [pltpu.with_memory_space_constraint(a, pltpu.HBM) for a in arrays]
 
 
-def full_gradient(inputs, error, factors, factor, blocks, shard, left, *lefts):
-    rows, tokens = inputs.shape[::-1]
-    width = error.shape[-1]
+def full_gradients(output, query, factors, shard, replicas):
+    rows, tokens = query[0].shape[::-1]
+    width, rank = query[1].shape[-1], factors.shape[-1]
     vmem = pl.BlockSpec(memory_space=pltpu.VMEM)
+    given = [
+        a for inputs, error, *blocks in (output, query) for a in (inputs.T, error[0], *blocks)
+    ]
+    given.append(jnp.swapaxes(factors, 1, 2))
     return pl.pallas_call(
-        functools.partial(gradient_kernel, factor),
-        out_shape=(pltpu.VMEM((rows, width), F32), left),
+        gradient_kernel,
+        out_shape=(
+            pltpu.VMEM((rows, width), F32),
+            pltpu.VMEM((rows, width), F32),
+            pltpu.VMEM((replicas, rows // 2, 4 * rank), BF16),
+        ),
         in_specs=[
             pl.BlockSpec(memory_space=pltpu.SMEM),
-            *[pl.BlockSpec(memory_space=pltpu.HBM)] * 3,
-            *[pl.BlockSpec(memory_space=pltpu.HBM)] * len(blocks),
-            *[vmem] * len(lefts),
+            *[pl.BlockSpec(memory_space=pltpu.HBM)] * len(given),
         ],
-        out_specs=(vmem, vmem),
+        out_specs=(vmem, vmem, vmem),
         scratch_shapes=[
-            pltpu.VMEM((rows, tokens), BF16),
-            pltpu.VMEM((4, rows, width // 4), BF16),
-            pltpu.VMEM((factors.shape[-1], width), BF16),
-            pltpu.VMEM((4, width // 4, tokens), BF16),
-            pltpu.SemaphoreType.DMA((2,)),
-            pltpu.SemaphoreType.DMA((4,)),
-            pltpu.SemaphoreType.DMA((4, 8)),
+            pltpu.VMEM((2, rows, tokens), BF16),
+            pltpu.VMEM((2, 4, rows, width // 4), BF16),
+            pltpu.VMEM((2, rank, width), BF16),
+            pltpu.VMEM((2, 4, width // 4, tokens), BF16),
+            pltpu.SemaphoreType.DMA((3,)),
+            pltpu.SemaphoreType.DMA((2, 4)),
+            pltpu.SemaphoreType.DMA((2, 4, 8)),
         ],
-        compiler_params=pltpu.CompilerParams(vmem_limit_bytes=20 << 20),
-    )(shard, *in_hbm(inputs.T, error[0], jnp.swapaxes(factors, 1, 2), *blocks), *in_vmem(*lefts))
+        compiler_params=pltpu.CompilerParams(vmem_limit_bytes=28 << 20),
+    )(shard, *in_hbm(*given))
 
 
 def inverse_kernel(grams, lefts, rows):
@@ -414,25 +421,13 @@
     right, left = partner(right), partner(left)
     far_low, far_high = partner(far_low), partner(far_high)
     query_theirs = [partner(a) for a in query_mine]
-    rows, rank = output_error.shape[1], start_factors.shape[-1]
-    output_full, output_left = full_gradient(
-        context_in,
-        output_error,
+    rank = start_factors.shape[-1]
+    query_full, output_full, lefts = full_gradients(
+        (context_in, output_error, *output_mine, column, right, far_low, far_high, left),
+        (hidden_in, query_error, *query_mine, *query_theirs),
         start_factors,
-        1,
-        (*output_mine, column, right, far_low, far_high, left),
         shard,
-        pltpu.VMEM((rows, rank), F32),
-    )
-    query_full, lefts = full_gradient(
-        hidden_in,
-        query_error,
-        start_factors,
-        0,
-        (*query_mine, *query_theirs),
-        shard,
-        pltpu.VMEM((replicas, rows // 2, 4 * rank), BF16),
-        output_left,
+        replicas,
     )
 
     sent, lefts = terms(exchange(lefts, "dp"), query_full, output_full, replicas, shards)

time: 221 us -> 221 us (level)
    pallas_call x2 -> x1, Pallas kernels: 13.6 us -> 12.5 us  [full_gradients(): pl.pallas_call(gradient_kernel, out_shape=(pltpu.VMEM((rows, width), F32)...]
  transfers between devices with their start and end apart: 14 -> 14, of which waited for: 6 -> 6; matrix products, arithmetic and copies ran while one was open for 0% -> 1% of each run, Pallas kernels for 5% -> 1%
where the time goes in v8:
time: 221 us; the launch traced here: 220 us
  blocking collectives  120 us (54%)
  starting transfers between devices  50.2 us (23%)
  Pallas kernels  22.9 us (10%)
  waiting for transfers between devices  22.2 us (10%)
  local copies, waits for them, and re-layouts  3.9 us (2%)
    all_to_all x5, blocking collectives, exchange(): lax.all_to_all(array, axis, 0, 0, tiled=True, axis_index_groups=groups)  120 us
    ppermute x13, starting transfers between devices, send(): return lax.ppermute(array, 'shard', in_plane(rows, cols, core))  41.4 us
    ppermute x13, waiting for transfers between devices, send(): return lax.ppermute(array, 'shard', in_plane(rows, cols, core))  15.8 us
    pallas_call x1, Pallas kernels, full_gradients(): pl.pallas_call(gradient_kernel, out_shape=(pltpu.VMEM((rows, width), F32)...  12.5 us
    all_to_all x1, starting transfers between devices, exchange(): lax.all_to_all(array, axis, 0, 0, tiled=True, axis_index_groups=groups)  8.8 us
    all_to_all x1, waiting for transfers between devices, exchange(): lax.all_to_all(array, axis, 0, 0, tiled=True, axis_index_groups=groups)  6.32 us
  transfers between devices with their start and end apart: 14, of which 6 were waited for; matrix products, arithmetic and copies ran while one was open for 1% of the time, Pallas kernels for 1%

profile of v8, /device:TPU:1, one launch (start us, length us, event | category | flops | bytes accessed | tf_op | source)
XLA Modules:
  0.0 220.1 jit_solution(2761612867129234010)
XLA Ops:
  0.6 1.0 broadcast_in_dim.6
  1.6 12.3 %all_to_all.30 = bf16[4,80,1024]{2,1,0:T(8,128)(2,1)S(1)} all-to-all(bf16[4,80,1024]{2,1,0:T(8,128)(2,1)S(1)} %broadcast_in_dim.6), channel_id=1, replica_groups={{0,2,4,6},{1,3,5,7},{8,10,12,14},{9,11,13,15},{16,18,20,22},{17,19,21,2..., dimensions={0} | all-to-all | bytes 1310720 | tf_op jit(solution)/shard_map/all_to_all | solution.py:21
  13.9 0.3 broadcast_in_dim.7
  14.2 0.0 copy-start.6
  14.2 36.2 %all_to_all.31.refs_14_ = bf16[4,4,80,1024]{3,2,1,0:T(8,128)(2,1)S(1)} all-to-all(bf16[4,4,80,1024]{3,2,1,0:T(8,128)(2,1)S(1)} %broadcast_in_dim.7), channel_id=1, replica_groups={{0,8,16,24},{1,9,17,25},{2,10,18,26},{3,11,19,27},{4,12,20,28},{5,13,21..., dimensions={0} | all-to-all | bytes 5242880 | tf_op jit(solution)/shard_map/all_to_all | solution.py:21
  50.4 5.1 %collective-permute-start.12 = (bf16[4,4,80,1024]{3,2,1,0:T(8,128)(2,1)S(1)}, bf16[4,4,80,1024]{3,2,1,0:T(8,128)(2,1)}, u32[]{:S(2)}, u32[]{:S(2)}) collective-permute-start(bf16[4,4,80,1024]{3,2,1,0:T(8,128)(2,1)S(1)} %all_to_all.31.refs_14_), channel_id=1, source_target_pairs={{0,1},{1,0},{2,3},{3,2},{4,5},{5,4},{6,7},{7,6},{8,9},{9,8},{10,11... | collective-permute-start | bytes 7864328 | tf_op jit(solution)/shard_map/ppermute | solution.py:41
  55.6 2.4 %collective-permute-start.1 = (bf16[80,1024]{1,0:T(8,128)(2,1)S(1)}, bf16[80,1024]{1,0:T(8,128)(2,1)S(1)}, u32[]{:S(2)}, u32[]{:S(2)}) collective-permute-start(bf16[80,1024]{1,0:T(8,128)(2,1)S(1)} %bitcast.19), channel_id=1, source_target_pairs={{0,16},{1,17},{2,18},{3,19},{4,20},{5,21},{6,22},{7,23},{8,24},{9,... | collective-permute-start | bytes 491528 | tf_op jit(solution)/shard_map/ppermute | solution.py:41
  58.0 4.0 %collective-permute-start = (bf16[80,1024]{1,0:T(8,128)(2,1)S(1)}, bf16[80,1024]{1,0:T(8,128)(2,1)S(1)}, u32[]{:S(2)}, u32[]{:S(2)}) collective-permute-start(bf16[80,1024]{1,0:T(8,128)(2,1)S(1)} %bitcast.20), channel_id=1, source_target_pairs={{0,24},{1,25},{2,26},{3,27},{4,28},{5,29},{6,30},{7,31},{8,0},{9,1... | collective-permute-start | bytes 491528 | tf_op jit(solution)/shard_map/ppermute | solution.py:41
  62.1 1.9 collective-permute-start.2
  64.0 0.7 collective-permute-done.1
  64.7 2.0 collective-permute-done
  66.7 3.6 %collective-permute-done.2 = bf16[80,1024]{1,0:T(8,128)(2,1)S(1)} collective-permute-done((bf16[80,1024]{1,0:T(8,128)(2,1)S(1)}, bf16[80,1024]{1,0:T(8,128)(2,1)S(1)}, u32[]{:S(2)}, u32[]{:S(2)}) %collective-permute-start.2) | collective-permute-done | bytes 163872 | tf_op jit(solution)/shard_map/ppermute | solution.py:41
  70.4 0.1 pad_maximum_fusion.refs_2_
  70.4 0.0 copy-start.3
  70.5 2.2 collective-permute-start.4
  72.7 4.3 %collective-permute-start.3 = (bf16[4,80,1024]{2,1,0:T(8,128)(2,1)S(1)}, bf16[4,80,1024]{2,1,0:T(8,128)(2,1)}, u32[]{:S(2)}, u32[]{:S(2)}) collective-permute-start(bf16[4,80,1024]{2,1,0:T(8,128)(2,1)S(1)} %pad_maximum_fusion.refs_2_), channel_id=1, source_target_pairs={{0,6},{1,7},{2,0},{3,1},{4,2},{5,3},{6,4},{7,5},{8,14},{9,15},{10,... | collective-permute-start | bytes 1966088 | tf_op jit(solution)/shard_map/ppermute | solution.py:41
  77.0 3.9 %collective-permute-start.7 = (bf16[4,80,1024]{2,1,0:T(8,128)(2,1)S(1)}, bf16[4,80,1024]{2,1,0:T(8,128)(2,1)S(1)}, u32[]{:S(2)}, u32[]{:S(2)}) collective-permute-start(bf16[4,80,1024]{2,1,0:T(8,128)(2,1)S(1)} %pad_maximum_fusion.refs_2_), channel_id=1, source_target_pairs={{0,1},{1,0},{2,3},{3,2},{4,5},{5,4},{6,7},{7,6},{8,9},{9,8},{10,11... | collective-permute-start | bytes 1966088 | tf_op jit(solution)/shard_map/ppermute | solution.py:41
  80.9 7.5 %collective-permute-done.4.refs_6_ = bf16[4,80,1024]{2,1,0:T(8,128)(2,1)S(1)} collective-permute-done((bf16[4,80,1024]{2,1,0:T(8,128)(2,1)S(1)}, bf16[4,80,1024]{2,1,0:T(8,128)(2,1)S(1)}, u32[]{:S(2)}, u32[]{:S(2)}) %collective-permute-start.4) | collective-permute-done | bytes 655392 | tf_op jit(solution)/shard_map/ppermute | solution.py:41
  88.4 1.9 collective-permute-start.5
  90.4 0.0 collective-permute-done.3.refs_3_
  90.4 1.0 slice.9
  91.4 4.6 %collective-permute-start.6 = (bf16[2,80,1024]{2,1,0:T(8,128)(2,1)S(1)}, bf16[2,80,1024]{2,1,0:T(8,128)(2,1)}, u32[]{:S(2)}, u32[]{:S(2)}) collective-permute-start(bf16[2,80,1024]{2,1,0:T(8,128)(2,1)S(1)} %slice.9), channel_id=1, source_target_pairs={{0,6},{1,7},{2,0},{3,1},{4,2},{5,3},{6,4},{7,5},{8,14},{9,15},{10,... | collective-permute-start | bytes 983048 | tf_op jit(solution)/shard_map/ppermute | solution.py:41
  96.0 4.8 %collective-permute-start.11 = (bf16[4,80,1024]{2,1,0:T(8,128)(2,1)S(1)}, bf16[4,80,1024]{2,1,0:T(8,128)(2,1)}, u32[]{:S(2)}, u32[]{:S(2)}) collective-permute-start(bf16[4,80,1024]{2,1,0:T(8,128)(2,1)S(1)} %collective-permute-done.4.refs_6_), channel_id=1, source_target_pairs={{0,1},{1,0},{2,3},{3,2},{4,5},{5,4},{6,7},{7,6},{8,9},{9,8},{10,11... | collective-permute-start | bytes 1966088 | tf_op jit(solution)/shard_map/ppermute | solution.py:41
  100.7 0.0 collective-permute-done.7.refs_7_
  100.8 0.8 copy-done.5
  101.6 1.9 collective-permute-start.8
  103.5 0.0 collective-permute-done.5.refs_4_
  103.5 2.4 %collective-permute-start.9 = (bf16[2,80,1024]{2,1,0:T(8,128)(2,1)}, bf16[2,80,1024]{2,1,0:T(8,128)(2,1)}, u32[]{:S(2)}, u32[]{:S(2)}) collective-permute-start(bf16[2,80,1024]{2,1,0:T(8,128)(2,1)} %collective-permute-done.5.refs_4_), channel_id=1, source_target_pairs={{0,1},{1,0},{2,3},{3,2},{4,5},{5,4},{6,7},{7,6},{8,9},{9,8},{10,11... | collective-permute-start | bytes 983048 | tf_op jit(solution)/shard_map/ppermute | solution.py:41
  105.9 0.0 collective-permute-done.6.refs_5_
  105.9 1.9 collective-permute-start.10
  107.9 0.0 collective-permute-done.9.refs_9_
  107.9 1.9 collective-permute-done.10.refs_10_
  109.8 0.0 collective-permute-done.11.refs_11_
  109.8 0.0 collective-permute-done.8.refs_8_
  109.8 0.0 collective-permute-done.12.refs_15_
  109.8 12.5 %shard_map.120 = (f32[160,2560]{1,0:T(8,128)S(1)}, f32[160,2560]{1,0:T(8,128)S(1)}, bf16[16,80,128]{2,1,0:T(8,128)(2,1)S(1)}) custom-call(s32[1]{0:T(128)} %bitcast.1.shard, bf16[160,1024]{1,0:T(8,128)(2,1)} %bitcast.16, bf16[160,2560]{1,0:T(8,128)(2,1)} %bitcast.14, bf16[4,80,1024]{2,1,0:T(8,128)(2,1)} %copy-done.3, ...), custom_call_target="tpu_custom_call" | custom-call | tf_op jit(solution)/shard_map/pallas_call | solution.py:150
  122.4 30.3 %all_to_all.32.arrived = bf16[16,80,128]{2,1,0:T(8,128)(2,1)S(1)} all-to-all(bf16[16,80,128]{2,1,0:T(8,128)(2,1)S(1)} %get-tuple-element.11), channel_id=1, replica_groups=mesh['dp'=16,'shard'=32] {'dp'}, dimensions={0} | all-to-all | bytes 655360 | tf_op jit(solution)/shard_map/all_to_all | solution.py:21
  152.7 1.9 shard_map.121
  154.6 23.1 %all_to_all.33.arrived = bf16[32,80,128]{2,1,0:T(8,128)(2,1)S(1)} all-to-all(bf16[32,80,128]{2,1,0:T(8,128)(2,1)} %get-tuple-element.14), channel_id=1, replica_groups=mesh['dp'=16,'shard'=32] {'shard'}, dimensions={0} | all-to-all | bytes 1310720 | tf_op jit(solution)/shard_map/all_to_all | solution.py:21
  177.7 0.7 shard_map.122
  178.5 18.0 %all_to_all.34.arrived = bf16[16,48,128]{2,1,0:T(8,128)(2,1)S(1)} all-to-all(bf16[16,48,128]{2,1,0:T(8,128)(2,1)} %get-tuple-element.15), channel_id=1, replica_groups=mesh['dp'=16,'shard'=32] {'dp'}, dimensions={0} | all-to-all | bytes 393216 | tf_op jit(solution)/shard_map/all_to_all | solution.py:21
  196.5 0.8 shard_map.123
  197.3 8.8 %all-to-all-start.5 = ((bf16[32,48,128]{2,1,0:T(8,128)(2,1)}), bf16[32,48,128]{2,1,0:T(8,128)(2,1)}, u32[]{:S(2)}, u32[]{:S(2)}) async-start(bf16[32,48,128]{2,1,0:T(8,128)(2,1)} %shard_map.123), calls=%async_computation.5 | async-start | bytes 786432 | tf_op jit(solution)/shard_map/all_to_all | solution.py:21
  206.1 0.0 copy-start.1
  206.1 0.7 copy-done.1
  206.8 3.3 %shard_map.124.rows = bf16[2,160,64]{2,1,0:T(8,128)(2,1)S(1)} custom-call(f32[32,128]{1,0:T(8,128)S(1)} %copy-done.1, f32[2,160,32]{2,1,0:T(8,128)S(1)} %copy-done), custom_call_target="tpu_custom_call" | custom-call | tf_op jit(solution)/shard_map/pallas_call | solution.py:205
  210.1 6.3 %all-to-all-done.5.arrived = bf16[32,48,128]{2,1,0:T(8,128)(2,1)} async-done(((bf16[32,48,128]{2,1,0:T(8,128)(2,1)}), bf16[32,48,128]{2,1,0:T(8,128)(2,1)}, u32[]{:S(2)}, u32[]{:S(2)}) %all-to-all-start.5) | async-done | bytes 393248 | tf_op jit(solution)/shard_map/all_to_all | solution.py:21
  216.4 3.7 %shard_map.125 = (bf16[1,160,2560]{2,1,0:T(8,128)(2,1)}, bf16[1,160,2560]{2,1,0:T(8,128)(2,1)}, f32[160,160]{1,0:T(8,128)}, f32[160,160]{1,0:T(8,128)}) custom-call(s32[1]{0:T(128)} %bitcast.replica, bf16[32,48,128]{2,1,0:T(8,128)(2,1)} %all-to-all-done.5.arrived, bf16[2,160,64]{2,1,0:T(8,128)(2,1)S(1)} %shard_map.124.rows, f32[160,160]{1,0:T(8,128)} %query_weight.1, ...), custom_call_target="tpu_custom_call" | custom-call | tf_op jit(solution)/shard_map/pallas_call | solution.py:372
  (10 shorter events, 0.0 us)
Async XLA Ops:
  14.2 41.3 %copy-start.6 = (bf16[1024,80]{0,1:T(8,128)(2,1)S(1)}, bf16[1024,80]{0,1:T(8,128)(2,1)}, u32[]{:S(2)}) copy-start(bf16[1024,80]{0,1:T(8,128)(2,1)} %param.12) | copy-start | bytes 491524
  50.4 59.4 %copy-start.2 = (bf16[4,4,80,1024]{3,2,1,0:T(8,128)(2,1)}, bf16[4,4,80,1024]{3,2,1,0:T(8,128)(2,1)S(1)}, u32[]{:S(2)}) copy-start(bf16[4,4,80,1024]{3,2,1,0:T(8,128)(2,1)S(1)} %all_to_all.31.refs_14_) | copy-start | bytes 7864324
  50.4 59.4 %collective-permute-start.12 = (bf16[4,4,80,1024]{3,2,1,0:T(8,128)(2,1)S(1)}, bf16[4,4,80,1024]{3,2,1,0:T(8,128)(2,1)}, u32[]{:S(2)}, u32[]{:S(2)}) collective-permute-start(bf16[4,4,80,1024]{3,2,1,0:T(8,128)(2,1)S(1)} %all_to_all.31.refs_14_), channel_id=1, source_target_pairs={{0,1},{1,0},{2,3},{3,2},{4,5},{5,4},{6,7},{7,6},{8,9},{9,8},{10,11... | collective-permute-start | bytes 7864328 | tf_op jit(solution)/shard_map/ppermute | solution.py:41
  55.6 9.1 %collective-permute-start.1 = (bf16[80,1024]{1,0:T(8,128)(2,1)S(1)}, bf16[80,1024]{1,0:T(8,128)(2,1)S(1)}, u32[]{:S(2)}, u32[]{:S(2)}) collective-permute-start(bf16[80,1024]{1,0:T(8,128)(2,1)S(1)} %bitcast.19), channel_id=1, source_target_pairs={{0,16},{1,17},{2,18},{3,19},{4,20},{5,21},{6,22},{7,23},{8,24},{9,... | collective-permute-start | bytes 491528 | tf_op jit(solution)/shard_map/ppermute | solution.py:41
  58.0 8.7 %collective-permute-start = (bf16[80,1024]{1,0:T(8,128)(2,1)S(1)}, bf16[80,1024]{1,0:T(8,128)(2,1)S(1)}, u32[]{:S(2)}, u32[]{:S(2)}) collective-permute-start(bf16[80,1024]{1,0:T(8,128)(2,1)S(1)} %bitcast.20), channel_id=1, source_target_pairs={{0,24},{1,25},{2,26},{3,27},{4,28},{5,29},{6,30},{7,31},{8,0},{9,1... | collective-permute-start | bytes 491528 | tf_op jit(solution)/shard_map/ppermute | solution.py:41
  62.1 8.3 %collective-permute-start.2 = (bf16[80,1024]{1,0:T(8,128)(2,1)S(1)}, bf16[80,1024]{1,0:T(8,128)(2,1)S(1)}, u32[]{:S(2)}, u32[]{:S(2)}) collective-permute-start(bf16[80,1024]{1,0:T(8,128)(2,1)S(1)} %bitcast.21), channel_id=1, source_target_pairs={{0,8},{1,9},{2,10},{3,11},{4,12},{5,13},{6,14},{7,15},{8,16},{9,17... | collective-permute-start | bytes 491528 | tf_op jit(solution)/shard_map/ppermute | solution.py:41
  70.4 6.5 %copy-start.3 = (bf16[4,80,1024]{2,1,0:T(8,128)(2,1)}, bf16[4,80,1024]{2,1,0:T(8,128)(2,1)S(1)}, u32[]{:S(2)}) copy-start(bf16[4,80,1024]{2,1,0:T(8,128)(2,1)S(1)} %pad_maximum_fusion.refs_2_) | copy-start | bytes 1966084
  70.5 18.0 %collective-permute-start.4 = (bf16[4,80,1024]{2,1,0:T(8,128)(2,1)S(1)}, bf16[4,80,1024]{2,1,0:T(8,128)(2,1)S(1)}, u32[]{:S(2)}, u32[]{:S(2)}) collective-permute-start(bf16[4,80,1024]{2,1,0:T(8,128)(2,1)S(1)} %pad_maximum_fusion.refs_2_), channel_id=1, source_target_pairs={{0,2},{1,3},{2,4},{3,5},{4,6},{5,7},{6,0},{7,1},{8,10},{9,11},{10,... | collective-permute-start | bytes 1966088 | tf_op jit(solution)/shard_map/ppermute | solution.py:41
  72.7 17.7 %collective-permute-start.3 = (bf16[4,80,1024]{2,1,0:T(8,128)(2,1)S(1)}, bf16[4,80,1024]{2,1,0:T(8,128)(2,1)}, u32[]{:S(2)}, u32[]{:S(2)}) collective-permute-start(bf16[4,80,1024]{2,1,0:T(8,128)(2,1)S(1)} %pad_maximum_fusion.refs_2_), channel_id=1, source_target_pairs={{0,6},{1,7},{2,0},{3,1},{4,2},{5,3},{6,4},{7,5},{8,14},{9,15},{10,... | collective-permute-start | bytes 1966088 | tf_op jit(solution)/shard_map/ppermute | solution.py:41
  77.0 23.8 %collective-permute-start.7 = (bf16[4,80,1024]{2,1,0:T(8,128)(2,1)S(1)}, bf16[4,80,1024]{2,1,0:T(8,128)(2,1)S(1)}, u32[]{:S(2)}, u32[]{:S(2)}) collective-permute-start(bf16[4,80,1024]{2,1,0:T(8,128)(2,1)S(1)} %pad_maximum_fusion.refs_2_), channel_id=1, source_target_pairs={{0,1},{1,0},{2,3},{3,2},{4,5},{5,4},{6,7},{7,6},{8,9},{9,8},{10,11... | collective-permute-start | bytes 1966088 | tf_op jit(solution)/shard_map/ppermute | solution.py:41
  88.4 21.4 %copy-start.4 = (bf16[4,80,1024]{2,1,0:T(8,128)(2,1)}, bf16[4,80,1024]{2,1,0:T(8,128)(2,1)S(1)}, u32[]{:S(2)}) copy-start(bf16[4,80,1024]{2,1,0:T(8,128)(2,1)S(1)} %collective-permute-done.4.refs_6_) | copy-start | bytes 1966084
  88.4 15.1 %collective-permute-start.5 = (bf16[2,80,1024]{2,1,0:T(8,128)(2,1)S(1)}, bf16[2,80,1024]{2,1,0:T(8,128)(2,1)}, u32[]{:S(2)}, u32[]{:S(2)}) collective-permute-start(bf16[2,80,1024]{2,1,0:T(8,128)(2,1)S(1)} %slice.8), channel_id=1, source_target_pairs={{0,2},{1,3},{2,4},{3,5},{4,6},{5,7},{6,0},{7,1},{8,10},{9,11},{10,... | collective-permute-start | bytes 983048 | tf_op jit(solution)/shard_map/ppermute | solution.py:41
  91.4 14.6 %collective-permute-start.6 = (bf16[2,80,1024]{2,1,0:T(8,128)(2,1)S(1)}, bf16[2,80,1024]{2,1,0:T(8,128)(2,1)}, u32[]{:S(2)}, u32[]{:S(2)}) collective-permute-start(bf16[2,80,1024]{2,1,0:T(8,128)(2,1)S(1)} %slice.9), channel_id=1, source_target_pairs={{0,6},{1,7},{2,0},{3,1},{4,2},{5,3},{6,4},{7,5},{8,14},{9,15},{10,... | collective-permute-start | bytes 983048 | tf_op jit(solution)/shard_map/ppermute | solution.py:41
  96.0 13.8 %collective-permute-start.11 = (bf16[4,80,1024]{2,1,0:T(8,128)(2,1)S(1)}, bf16[4,80,1024]{2,1,0:T(8,128)(2,1)}, u32[]{:S(2)}, u32[]{:S(2)}) collective-permute-start(bf16[4,80,1024]{2,1,0:T(8,128)(2,1)S(1)} %collective-permute-done.4.refs_6_), channel_id=1, source_target_pairs={{0,1},{1,0},{2,3},{3,2},{4,5},{5,4},{6,7},{7,6},{8,9},{9,8},{10,11... | collective-permute-start | bytes 1966088 | tf_op jit(solution)/shard_map/ppermute | solution.py:41
  100.7 0.8 copy-start.5
  101.6 8.2 %collective-permute-start.8 = (bf16[4,80,1024]{2,1,0:T(8,128)(2,1)}, bf16[4,80,1024]{2,1,0:T(8,128)(2,1)}, u32[]{:S(2)}, u32[]{:S(2)}) collective-permute-start(bf16[4,80,1024]{2,1,0:T(8,128)(2,1)} %collective-permute-done.3.refs_3_), channel_id=1, source_target_pairs={{0,1},{1,0},{2,3},{3,2},{4,5},{5,4},{6,7},{7,6},{8,9},{9,8},{10,11... | collective-permute-start | bytes 1966088 | tf_op jit(solution)/shard_map/ppermute | solution.py:41
  103.5 4.4 %collective-permute-start.9 = (bf16[2,80,1024]{2,1,0:T(8,128)(2,1)}, bf16[2,80,1024]{2,1,0:T(8,128)(2,1)}, u32[]{:S(2)}, u32[]{:S(2)}) collective-permute-start(bf16[2,80,1024]{2,1,0:T(8,128)(2,1)} %collective-permute-done.5.refs_4_), channel_id=1, source_target_pairs={{0,1},{1,0},{2,3},{3,2},{4,5},{5,4},{6,7},{7,6},{8,9},{9,8},{10,11... | collective-permute-start | bytes 983048 | tf_op jit(solution)/shard_map/ppermute | solution.py:41
  105.9 3.9 %collective-permute-start.10 = (bf16[2,80,1024]{2,1,0:T(8,128)(2,1)}, bf16[2,80,1024]{2,1,0:T(8,128)(2,1)}, u32[]{:S(2)}, u32[]{:S(2)}) collective-permute-start(bf16[2,80,1024]{2,1,0:T(8,128)(2,1)} %collective-permute-done.6.refs_5_), channel_id=1, source_target_pairs={{0,1},{1,0},{2,3},{3,2},{4,5},{5,4},{6,7},{7,6},{8,9},{9,8},{10,11... | collective-permute-start | bytes 983048 | tf_op jit(solution)/shard_map/ppermute | solution.py:41
  154.6 51.5 %copy-start = (f32[2,160,32]{2,1,0:T(8,128)S(1)}, f32[2,160,32]{2,1,0:T(8,128)}, u32[]{:S(2)}) copy-start(f32[2,160,32]{2,1,0:T(8,128)} %get-tuple-element.17.lefts) | copy-start | bytes 122884
  197.3 19.1 %all-to-all-start.5 = ((bf16[32,48,128]{2,1,0:T(8,128)(2,1)}), bf16[32,48,128]{2,1,0:T(8,128)(2,1)}, u32[]{:S(2)}, u32[]{:S(2)}) async-start(bf16[32,48,128]{2,1,0:T(8,128)(2,1)} %shard_map.123), calls=%async_computation.5 | async-start | bytes 786432 | tf_op jit(solution)/shard_map/all_to_all | solution.py:21
  206.1 0.7 copy-start.1

commit v9 on v7

--- a/solution.py
+++ b/solution.py
@@ -100,12 +100,15 @@
     second = pltpu.make_async_copy(start_in.at[factor], start, given.at[1])
     first.start()
     steps = [(k, other) for k in range(side) for other in range(2)]
-    for j in range(side):
+
+    def begin(j):
         for k, other in steps:
             fetch(j, k, other).start()
         prior(j).start()
-        if j == 0:
-            second.start()
+
+    begin(0)
+    second.start()
+    begin(1)
     first.wait()
     total = jnp.zeros((acts.shape[0], start.shape[0]), F32)
     for j in range(side):
@@ -114,6 +117,8 @@
         prior(j).wait()
         if j == 0:
             second.wait()
+        if j + 2 < side:
+            begin(j + 2)
         part = contract(acts[...], columns[j], (1, 1)) + error[j].astype(F32)
         full[:, lanes(j)] = part
         high, low = split_high_low(part)

time: 221 us -> 219 us (level)
  transfers between devices with their start and end apart: 14 -> 14, of which waited for: 6 -> 6; matrix products, arithmetic and copies ran while one was open for 0% -> 0% of each run, Pallas kernels for 5% -> 4%
where the time goes in v9:
time: 219 us; the launch traced here: 218 us
  blocking collectives  120 us (55%)
  starting transfers between devices  50.4 us (23%)
  waiting for transfers between devices  22.2 us (10%)
  Pallas kernels  22.1 us (10%)
    all_to_all x5, blocking collectives, exchange(): lax.all_to_all(array, axis, 0, 0, tiled=True, axis_index_groups=groups)  120 us
    ppermute x13, starting transfers between devices, send(): return lax.ppermute(array, 'shard', in_plane(rows, cols, core))  41.6 us
    ppermute x13, waiting for transfers between devices, send(): return lax.ppermute(array, 'shard', in_plane(rows, cols, core))  15.8 us
    pallas_call x2, Pallas kernels, full_gradient(): pl.pallas_call(functools.partial(gradient_kernel, factor), out_shape=(plt...  11.7 us
    all_to_all x1, starting transfers between devices, exchange(): lax.all_to_all(array, axis, 0, 0, tiled=True, axis_index_groups=groups)  8.8 us
    all_to_all x1, waiting for transfers between devices, exchange(): lax.all_to_all(array, axis, 0, 0, tiled=True, axis_index_groups=groups)  6.32 us
  transfers between devices with their start and end apart: 14, of which 6 were waited for; matrix products, arithmetic and copies ran while one was open for 0% of the time, Pallas kernels for 4%

profile of v9, /device:TPU:1, one launch (start us, length us, event | category | flops | bytes accessed | tf_op | source)
XLA Modules:
  0.0 217.7 jit_solution(17671069918900754937)
XLA Ops:
  0.6 1.0 broadcast_in_dim.6
  1.6 12.3 %all_to_all.30 = bf16[4,80,1024]{2,1,0:T(8,128)(2,1)S(1)} all-to-all(bf16[4,80,1024]{2,1,0:T(8,128)(2,1)S(1)} %broadcast_in_dim.6), channel_id=1, replica_groups={{0,2,4,6},{1,3,5,7},{8,10,12,14},{9,11,13,15},{16,18,20,22},{17,19,21,2..., dimensions={0} | all-to-all | bytes 1310720 | tf_op jit(solution)/shard_map/all_to_all | solution.py:21
  13.9 0.3 broadcast_in_dim.7
  14.2 0.0 copy-start.8
  14.2 36.1 %all_to_all.31.refs_3_ = bf16[4,4,80,1024]{3,2,1,0:T(8,128)(2,1)} all-to-all(bf16[4,4,80,1024]{3,2,1,0:T(8,128)(2,1)S(1)} %broadcast_in_dim.7), channel_id=1, replica_groups={{0,8,16,24},{1,9,17,25},{2,10,18,26},{3,11,19,27},{4,12,20,28},{5,13,21..., dimensions={0} | all-to-all | bytes 5242880 | tf_op jit(solution)/shard_map/all_to_all | solution.py:21
  50.3 5.3 %collective-permute-start = (bf16[4,4,80,1024]{3,2,1,0:T(8,128)(2,1)}, bf16[4,4,80,1024]{3,2,1,0:T(8,128)(2,1)}, u32[]{:S(2)}, u32[]{:S(2)}) collective-permute-start(bf16[4,4,80,1024]{3,2,1,0:T(8,128)(2,1)} %all_to_all.31.refs_3_), channel_id=1, source_target_pairs={{0,1},{1,0},{2,3},{3,2},{4,5},{5,4},{6,7},{7,6},{8,9},{9,8},{10,11... | collective-permute-start | bytes 7864328 | tf_op jit(solution)/shard_map/ppermute | solution.py:41
  55.7 2.4 %collective-permute-start.2 = (bf16[80,1024]{1,0:T(8,128)(2,1)S(1)}, bf16[80,1024]{1,0:T(8,128)(2,1)S(1)}, u32[]{:S(2)}, u32[]{:S(2)}) collective-permute-start(bf16[80,1024]{1,0:T(8,128)(2,1)S(1)} %bitcast.20), channel_id=1, source_target_pairs={{0,16},{1,17},{2,18},{3,19},{4,20},{5,21},{6,22},{7,23},{8,24},{9,... | collective-permute-start | bytes 491528 | tf_op jit(solution)/shard_map/ppermute | solution.py:41
  58.1 4.0 %collective-permute-start.1 = (bf16[80,1024]{1,0:T(8,128)(2,1)S(1)}, bf16[80,1024]{1,0:T(8,128)(2,1)S(1)}, u32[]{:S(2)}, u32[]{:S(2)}) collective-permute-start(bf16[80,1024]{1,0:T(8,128)(2,1)S(1)} %bitcast.21), channel_id=1, source_target_pairs={{0,24},{1,25},{2,26},{3,27},{4,28},{5,29},{6,30},{7,31},{8,0},{9,1... | collective-permute-start | bytes 491528 | tf_op jit(solution)/shard_map/ppermute | solution.py:41
  62.2 1.9 collective-permute-start.3
  64.1 0.7 collective-permute-done.2
  64.8 2.0 collective-permute-done.1
  66.8 3.6 %collective-permute-done.3 = bf16[80,1024]{1,0:T(8,128)(2,1)S(1)} collective-permute-done((bf16[80,1024]{1,0:T(8,128)(2,1)S(1)}, bf16[80,1024]{1,0:T(8,128)(2,1)S(1)}, u32[]{:S(2)}, u32[]{:S(2)}) %collective-permute-start.3) | collective-permute-done | bytes 163872 | tf_op jit(solution)/shard_map/ppermute | solution.py:41
  70.5 0.1 pad_maximum_fusion.refs_3_
  70.5 0.0 copy-start.2
  70.6 2.2 %collective-permute-start.5 = (bf16[4,80,1024]{2,1,0:T(8,128)(2,1)S(1)}, bf16[4,80,1024]{2,1,0:T(8,128)(2,1)S(1)}, u32[]{:S(2)}, u32[]{:S(2)}) collective-permute-start(bf16[4,80,1024]{2,1,0:T(8,128)(2,1)S(1)} %pad_maximum_fusion.refs_3_), channel_id=1, source_target_pairs={{0,2},{1,3},{2,4},{3,5},{4,6},{5,7},{6,0},{7,1},{8,10},{9,11},{10,... | collective-permute-start | bytes 1966088 | tf_op jit(solution)/shard_map/ppermute | solution.py:41
  72.8 4.3 %collective-permute-start.4 = (bf16[4,80,1024]{2,1,0:T(8,128)(2,1)S(1)}, bf16[4,80,1024]{2,1,0:T(8,128)(2,1)S(1)}, u32[]{:S(2)}, u32[]{:S(2)}) collective-permute-start(bf16[4,80,1024]{2,1,0:T(8,128)(2,1)S(1)} %pad_maximum_fusion.refs_3_), channel_id=1, source_target_pairs={{0,6},{1,7},{2,0},{3,1},{4,2},{5,3},{6,4},{7,5},{8,14},{9,15},{10,... | collective-permute-start | bytes 1966088 | tf_op jit(solution)/shard_map/ppermute | solution.py:41
  77.1 3.9 %collective-permute-start.8 = (bf16[4,80,1024]{2,1,0:T(8,128)(2,1)S(1)}, bf16[4,80,1024]{2,1,0:T(8,128)(2,1)S(1)}, u32[]{:S(2)}, u32[]{:S(2)}) collective-permute-start(bf16[4,80,1024]{2,1,0:T(8,128)(2,1)S(1)} %pad_maximum_fusion.refs_3_), channel_id=1, source_target_pairs={{0,1},{1,0},{2,3},{3,2},{4,5},{5,4},{6,7},{7,6},{8,9},{9,8},{10,11... | collective-permute-start | bytes 1966088 | tf_op jit(solution)/shard_map/ppermute | solution.py:41
  81.0 7.5 %collective-permute-done.5.refs_7_ = bf16[4,80,1024]{2,1,0:T(8,128)(2,1)S(1)} collective-permute-done((bf16[4,80,1024]{2,1,0:T(8,128)(2,1)S(1)}, bf16[4,80,1024]{2,1,0:T(8,128)(2,1)S(1)}, u32[]{:S(2)}, u32[]{:S(2)}) %collective-permute-start.5) | collective-permute-done | bytes 655392 | tf_op jit(solution)/shard_map/ppermute | solution.py:41
  88.6 1.9 collective-permute-start.6
  90.5 0.0 collective-permute-done.4.refs_4_
  90.5 0.0 copy-start.4
  90.5 4.6 %collective-permute-start.7 = (bf16[2,80,1024]{2,1,0:T(8,128)(2,1)S(1)}, bf16[2,80,1024]{2,1,0:T(8,128)(2,1)}, u32[]{:S(2)}, u32[]{:S(2)}) collective-permute-start(bf16[2,80,1024]{2,1,0:T(8,128)(2,1)S(1)} %slice.9), channel_id=1, source_target_pairs={{0,6},{1,7},{2,0},{3,1},{4,2},{5,3},{6,4},{7,5},{8,14},{9,15},{10,... | collective-permute-start | bytes 983048 | tf_op jit(solution)/shard_map/ppermute | solution.py:41
  95.1 4.8 %collective-permute-start.12 = (bf16[4,80,1024]{2,1,0:T(8,128)(2,1)S(1)}, bf16[4,80,1024]{2,1,0:T(8,128)(2,1)}, u32[]{:S(2)}, u32[]{:S(2)}) collective-permute-start(bf16[4,80,1024]{2,1,0:T(8,128)(2,1)S(1)} %collective-permute-done.5.refs_7_), channel_id=1, source_target_pairs={{0,1},{1,0},{2,3},{3,2},{4,5},{5,4},{6,7},{7,6},{8,9},{9,8},{10,11... | collective-permute-start | bytes 1966088 | tf_op jit(solution)/shard_map/ppermute | solution.py:41
  99.9 0.0 collective-permute-done.8.refs_8_
  99.9 1.9 collective-permute-start.9
  101.8 0.0 collective-permute-done.6.refs_5_
  101.9 2.4 %collective-permute-start.10 = (bf16[2,80,1024]{2,1,0:T(8,128)(2,1)S(1)}, bf16[2,80,1024]{2,1,0:T(8,128)(2,1)S(1)}, u32[]{:S(2)}, u32[]{:S(2)}) collective-permute-start(bf16[2,80,1024]{2,1,0:T(8,128)(2,1)S(1)} %collective-permute-done.6.refs_5_), channel_id=1, source_target_pairs={{0,1},{1,0},{2,3},{3,2},{4,5},{5,4},{6,7},{7,6},{8,9},{9,8},{10,11... | collective-permute-start | bytes 983048 | tf_op jit(solution)/shard_map/ppermute | solution.py:41
  104.3 0.0 collective-permute-done.7.refs_6_
  104.3 1.9 collective-permute-start.11
  106.2 0.0 collective-permute-done.10.refs_10_
  106.2 1.9 collective-permute-done.11.refs_11_
  108.1 0.0 collective-permute-done.12.refs_12_
  108.1 0.0 collective-permute-done.9.refs_9_
  108.2 5.8 %shard_map.120 = (f32[160,2560]{1,0:T(8,128)S(1)}, f32[160,32]{1,0:T(8,128)S(1)}) custom-call(s32[1]{0:T(128)} %bitcast.1.shard, bf16[160,1024]{1,0:T(8,128)(2,1)} %bitcast.18, bf16[160,2560]{1,0:T(8,128)(2,1)} %bitcast.16, bf16[2,32,2560]{2,1,0:T(8,128)(2,1)} %bitcast.14, bf16[4,80,1024]{2,1,0:T(8,128)(2,1)} %copy-done.2, bf16[4,80,1024]{2,1,0:T(8,128)(2,1)} %copy-done.4, ...), custom_call_target="tpu_custom_call" | custom-call | tf_op jit(solution)/shard_map/pallas_call | solution.py:150
  114.0 0.0 collective-permute-done.refs_4_
  114.0 5.9 %shard_map.121 = (f32[160,2560]{1,0:T(8,128)S(1)}, bf16[16,80,128]{2,1,0:T(8,128)(2,1)S(1)}) custom-call(s32[1]{0:T(128)} %bitcast.1.shard, bf16[160,1024]{1,0:T(8,128)(2,1)} %bitcast.19, bf16[160,2560]{1,0:T(8,128)(2,1)} %bitcast.17, bf16[2,32,2560]{2,1,0:T(8,128)(2,1)} %bitcast.15, bf16[4,4,80,1024]{3,2,1,0:T(8,128)(2,1)} %all_to_all.31.refs_3_, ...), custom_call_target="tpu_custom_call" | custom-call | tf_op jit(solution)/shard_map/pallas_call | solution.py:150
  120.0 30.3 %all_to_all.32.arrived = bf16[16,80,128]{2,1,0:T(8,128)(2,1)S(1)} all-to-all(bf16[16,80,128]{2,1,0:T(8,128)(2,1)S(1)} %get-tuple-element.13), channel_id=1, replica_groups=mesh['dp'=16,'shard'=32] {'dp'}, dimensions={0} | all-to-all | bytes 655360 | tf_op jit(solution)/shard_map/all_to_all | solution.py:21
  150.3 1.9 shard_map.122
  152.2 23.1 %all_to_all.33.arrived = bf16[32,80,128]{2,1,0:T(8,128)(2,1)S(1)} all-to-all(bf16[32,80,128]{2,1,0:T(8,128)(2,1)} %get-tuple-element.16), channel_id=1, replica_groups=mesh['dp'=16,'shard'=32] {'shard'}, dimensions={0} | all-to-all | bytes 1310720 | tf_op jit(solution)/shard_map/all_to_all | solution.py:21
  175.3 0.7 shard_map.123
  176.1 18.0 %all_to_all.34.arrived = bf16[16,48,128]{2,1,0:T(8,128)(2,1)S(1)} all-to-all(bf16[16,48,128]{2,1,0:T(8,128)(2,1)} %get-tuple-element.17), channel_id=1, replica_groups=mesh['dp'=16,'shard'=32] {'dp'}, dimensions={0} | all-to-all | bytes 393216 | tf_op jit(solution)/shard_map/all_to_all | solution.py:21
  194.1 0.8 shard_map.124
  194.9 8.8 %all-to-all-start.5 = ((bf16[32,48,128]{2,1,0:T(8,128)(2,1)}), bf16[32,48,128]{2,1,0:T(8,128)(2,1)}, u32[]{:S(2)}, u32[]{:S(2)}) async-start(bf16[32,48,128]{2,1,0:T(8,128)(2,1)} %shard_map.124), calls=%async_computation.5 | async-start | bytes 786432 | tf_op jit(solution)/shard_map/all_to_all | solution.py:21
  203.7 0.0 copy-start.1
  203.7 0.7 copy-done.1
  204.5 3.3 %shard_map.125.rows = bf16[2,160,64]{2,1,0:T(8,128)(2,1)S(1)} custom-call(f32[32,128]{1,0:T(8,128)S(1)} %copy-done.1, f32[2,160,32]{2,1,0:T(8,128)S(1)} %copy-done), custom_call_target="tpu_custom_call" | custom-call | tf_op jit(solution)/shard_map/pallas_call | solution.py:203
  207.7 6.3 %all-to-all-done.5.arrived = bf16[32,48,128]{2,1,0:T(8,128)(2,1)} async-done(((bf16[32,48,128]{2,1,0:T(8,128)(2,1)}), bf16[32,48,128]{2,1,0:T(8,128)(2,1)}, u32[]{:S(2)}, u32[]{:S(2)}) %all-to-all-start.5) | async-done | bytes 393248 | tf_op jit(solution)/shard_map/all_to_all | solution.py:21
  214.0 3.7 %shard_map.126 = (bf16[1,160,2560]{2,1,0:T(8,128)(2,1)}, bf16[1,160,2560]{2,1,0:T(8,128)(2,1)}, f32[160,160]{1,0:T(8,128)}, f32[160,160]{1,0:T(8,128)}) custom-call(s32[1]{0:T(128)} %bitcast.replica, bf16[32,48,128]{2,1,0:T(8,128)(2,1)} %all-to-all-done.5.arrived, bf16[2,160,64]{2,1,0:T(8,128)(2,1)S(1)} %shard_map.125.rows, f32[160,160]{1,0:T(8,128)} %query_weight.1, ...), custom_call_target="tpu_custom_call" | custom-call | tf_op jit(solution)/shard_map/pallas_call | solution.py:370
  (15 shorter events, 0.1 us)
Async XLA Ops:
  14.2 41.4 %copy-start.8 = (bf16[1024,80]{0,1:T(8,128)(2,1)S(1)}, bf16[1024,80]{0,1:T(8,128)(2,1)}, u32[]{:S(2)}) copy-start(bf16[1024,80]{0,1:T(8,128)(2,1)} %param.12) | copy-start | bytes 491524
  50.3 63.7 %collective-permute-start = (bf16[4,4,80,1024]{3,2,1,0:T(8,128)(2,1)}, bf16[4,4,80,1024]{3,2,1,0:T(8,128)(2,1)}, u32[]{:S(2)}, u32[]{:S(2)}) collective-permute-start(bf16[4,4,80,1024]{3,2,1,0:T(8,128)(2,1)} %all_to_all.31.refs_3_), channel_id=1, source_target_pairs={{0,1},{1,0},{2,3},{3,2},{4,5},{5,4},{6,7},{7,6},{8,9},{9,8},{10,11... | collective-permute-start | bytes 7864328 | tf_op jit(solution)/shard_map/ppermute | solution.py:41
  55.7 9.1 %collective-permute-start.2 = (bf16[80,1024]{1,0:T(8,128)(2,1)S(1)}, bf16[80,1024]{1,0:T(8,128)(2,1)S(1)}, u32[]{:S(2)}, u32[]{:S(2)}) collective-permute-start(bf16[80,1024]{1,0:T(8,128)(2,1)S(1)} %bitcast.20), channel_id=1, source_target_pairs={{0,16},{1,17},{2,18},{3,19},{4,20},{5,21},{6,22},{7,23},{8,24},{9,... | collective-permute-start | bytes 491528 | tf_op jit(solution)/shard_map/ppermute | solution.py:41
  58.1 8.7 %collective-permute-start.1 = (bf16[80,1024]{1,0:T(8,128)(2,1)S(1)}, bf16[80,1024]{1,0:T(8,128)(2,1)S(1)}, u32[]{:S(2)}, u32[]{:S(2)}) collective-permute-start(bf16[80,1024]{1,0:T(8,128)(2,1)S(1)} %bitcast.21), channel_id=1, source_target_pairs={{0,24},{1,25},{2,26},{3,27},{4,28},{5,29},{6,30},{7,31},{8,0},{9,1... | collective-permute-start | bytes 491528 | tf_op jit(solution)/shard_map/ppermute | solution.py:41
  62.2 8.3 %collective-permute-start.3 = (bf16[80,1024]{1,0:T(8,128)(2,1)S(1)}, bf16[80,1024]{1,0:T(8,128)(2,1)S(1)}, u32[]{:S(2)}, u32[]{:S(2)}) collective-permute-start(bf16[80,1024]{1,0:T(8,128)(2,1)S(1)} %bitcast.22), channel_id=1, source_target_pairs={{0,8},{1,9},{2,10},{3,11},{4,12},{5,13},{6,14},{7,15},{8,16},{9,17... | collective-permute-start | bytes 491528 | tf_op jit(solution)/shard_map/ppermute | solution.py:41
  70.5 37.6 %copy-start.2 = (bf16[4,80,1024]{2,1,0:T(8,128)(2,1)}, bf16[4,80,1024]{2,1,0:T(8,128)(2,1)S(1)}, u32[]{:S(2)}) copy-start(bf16[4,80,1024]{2,1,0:T(8,128)(2,1)S(1)} %pad_maximum_fusion.refs_3_) | copy-start | bytes 1966084
  70.6 18.0 %collective-permute-start.5 = (bf16[4,80,1024]{2,1,0:T(8,128)(2,1)S(1)}, bf16[4,80,1024]{2,1,0:T(8,128)(2,1)S(1)}, u32[]{:S(2)}, u32[]{:S(2)}) collective-permute-start(bf16[4,80,1024]{2,1,0:T(8,128)(2,1)S(1)} %pad_maximum_fusion.refs_3_), channel_id=1, source_target_pairs={{0,2},{1,3},{2,4},{3,5},{4,6},{5,7},{6,0},{7,1},{8,10},{9,11},{10,... | collective-permute-start | bytes 1966088 | tf_op jit(solution)/shard_map/ppermute | solution.py:41
  72.8 17.7 %collective-permute-start.4 = (bf16[4,80,1024]{2,1,0:T(8,128)(2,1)S(1)}, bf16[4,80,1024]{2,1,0:T(8,128)(2,1)S(1)}, u32[]{:S(2)}, u32[]{:S(2)}) collective-permute-start(bf16[4,80,1024]{2,1,0:T(8,128)(2,1)S(1)} %pad_maximum_fusion.refs_3_), channel_id=1, source_target_pairs={{0,6},{1,7},{2,0},{3,1},{4,2},{5,3},{6,4},{7,5},{8,14},{9,15},{10,... | collective-permute-start | bytes 1966088 | tf_op jit(solution)/shard_map/ppermute | solution.py:41
  77.1 22.8 %collective-permute-start.8 = (bf16[4,80,1024]{2,1,0:T(8,128)(2,1)S(1)}, bf16[4,80,1024]{2,1,0:T(8,128)(2,1)S(1)}, u32[]{:S(2)}, u32[]{:S(2)}) collective-permute-start(bf16[4,80,1024]{2,1,0:T(8,128)(2,1)S(1)} %pad_maximum_fusion.refs_3_), channel_id=1, source_target_pairs={{0,1},{1,0},{2,3},{3,2},{4,5},{5,4},{6,7},{7,6},{8,9},{9,8},{10,11... | collective-permute-start | bytes 1966088 | tf_op jit(solution)/shard_map/ppermute | solution.py:41
  88.5 19.7 %copy-start.3 = (bf16[4,80,1024]{2,1,0:T(8,128)(2,1)}, bf16[4,80,1024]{2,1,0:T(8,128)(2,1)S(1)}, u32[]{:S(2)}) copy-start(bf16[4,80,1024]{2,1,0:T(8,128)(2,1)S(1)} %collective-permute-done.5.refs_7_) | copy-start | bytes 1966084
  88.6 13.3 %collective-permute-start.6 = (bf16[2,80,1024]{2,1,0:T(8,128)(2,1)S(1)}, bf16[2,80,1024]{2,1,0:T(8,128)(2,1)S(1)}, u32[]{:S(2)}, u32[]{:S(2)}) collective-permute-start(bf16[2,80,1024]{2,1,0:T(8,128)(2,1)S(1)} %slice.8), channel_id=1, source_target_pairs={{0,2},{1,3},{2,4},{3,5},{4,6},{5,7},{6,0},{7,1},{8,10},{9,11},{10,... | collective-permute-start | bytes 983048 | tf_op jit(solution)/shard_map/ppermute | solution.py:41
  90.5 17.7 %copy-start.4 = (bf16[4,80,1024]{2,1,0:T(8,128)(2,1)}, bf16[4,80,1024]{2,1,0:T(8,128)(2,1)S(1)}, u32[]{:S(2)}) copy-start(bf16[4,80,1024]{2,1,0:T(8,128)(2,1)S(1)} %collective-permute-done.4.refs_4_) | copy-start | bytes 1966084
  90.5 13.7 %collective-permute-start.7 = (bf16[2,80,1024]{2,1,0:T(8,128)(2,1)S(1)}, bf16[2,80,1024]{2,1,0:T(8,128)(2,1)}, u32[]{:S(2)}, u32[]{:S(2)}) collective-permute-start(bf16[2,80,1024]{2,1,0:T(8,128)(2,1)S(1)} %slice.9), channel_id=1, source_target_pairs={{0,6},{1,7},{2,0},{3,1},{4,2},{5,3},{6,4},{7,5},{8,14},{9,15},{10,... | collective-permute-start | bytes 983048 | tf_op jit(solution)/shard_map/ppermute | solution.py:41
  95.1 13.0 %collective-permute-start.12 = (bf16[4,80,1024]{2,1,0:T(8,128)(2,1)S(1)}, bf16[4,80,1024]{2,1,0:T(8,128)(2,1)}, u32[]{:S(2)}, u32[]{:S(2)}) collective-permute-start(bf16[4,80,1024]{2,1,0:T(8,128)(2,1)S(1)} %collective-permute-done.5.refs_7_), channel_id=1, source_target_pairs={{0,1},{1,0},{2,3},{3,2},{4,5},{5,4},{6,7},{7,6},{8,9},{9,8},{10,11... | collective-permute-start | bytes 1966088 | tf_op jit(solution)/shard_map/ppermute | solution.py:41
  99.9 8.3 %copy-start.5 = (bf16[4,80,1024]{2,1,0:T(8,128)(2,1)}, bf16[4,80,1024]{2,1,0:T(8,128)(2,1)S(1)}, u32[]{:S(2)}) copy-start(bf16[4,80,1024]{2,1,0:T(8,128)(2,1)S(1)} %collective-permute-done.8.refs_8_) | copy-start | bytes 1966084
  99.9 8.2 %collective-permute-start.9 = (bf16[4,80,1024]{2,1,0:T(8,128)(2,1)S(1)}, bf16[4,80,1024]{2,1,0:T(8,128)(2,1)}, u32[]{:S(2)}, u32[]{:S(2)}) collective-permute-start(bf16[4,80,1024]{2,1,0:T(8,128)(2,1)S(1)} %collective-permute-done.4.refs_4_), channel_id=1, source_target_pairs={{0,1},{1,0},{2,3},{3,2},{4,5},{5,4},{6,7},{7,6},{8,9},{9,8},{10,11... | collective-permute-start | bytes 1966088 | tf_op jit(solution)/shard_map/ppermute | solution.py:41
  101.8 6.4 %copy-start.6 = (bf16[2,80,1024]{2,1,0:T(8,128)(2,1)}, bf16[2,80,1024]{2,1,0:T(8,128)(2,1)S(1)}, u32[]{:S(2)}) copy-start(bf16[2,80,1024]{2,1,0:T(8,128)(2,1)S(1)} %collective-permute-done.6.refs_5_) | copy-start | bytes 983044
  101.9 4.4 %collective-permute-start.10 = (bf16[2,80,1024]{2,1,0:T(8,128)(2,1)S(1)}, bf16[2,80,1024]{2,1,0:T(8,128)(2,1)S(1)}, u32[]{:S(2)}, u32[]{:S(2)}) collective-permute-start(bf16[2,80,1024]{2,1,0:T(8,128)(2,1)S(1)} %collective-permute-done.6.refs_5_), channel_id=1, source_target_pairs={{0,1},{1,0},{2,3},{3,2},{4,5},{5,4},{6,7},{7,6},{8,9},{9,8},{10,11... | collective-permute-start | bytes 983048 | tf_op jit(solution)/shard_map/ppermute | solution.py:41
  104.3 3.9 %collective-permute-start.11 = (bf16[2,80,1024]{2,1,0:T(8,128)(2,1)}, bf16[2,80,1024]{2,1,0:T(8,128)(2,1)}, u32[]{:S(2)}, u32[]{:S(2)}) collective-permute-start(bf16[2,80,1024]{2,1,0:T(8,128)(2,1)} %collective-permute-done.7.refs_6_), channel_id=1, source_target_pairs={{0,1},{1,0},{2,3},{3,2},{4,5},{5,4},{6,7},{7,6},{8,9},{9,8},{10,11... | collective-permute-start | bytes 983048 | tf_op jit(solution)/shard_map/ppermute | solution.py:41
  106.2 1.9 copy-start.7
  152.2 51.5 %copy-start = (f32[2,160,32]{2,1,0:T(8,128)S(1)}, f32[2,160,32]{2,1,0:T(8,128)}, u32[]{:S(2)}) copy-start(f32[2,160,32]{2,1,0:T(8,128)} %get-tuple-element.19.lefts) | copy-start | bytes 122884
  194.9 19.1 %all-to-all-start.5 = ((bf16[32,48,128]{2,1,0:T(8,128)(2,1)}), bf16[32,48,128]{2,1,0:T(8,128)(2,1)}, u32[]{:S(2)}, u32[]{:S(2)}) async-start(bf16[32,48,128]{2,1,0:T(8,128)(2,1)} %shard_map.124), calls=%async_computation.5 | async-start | bytes 786432 | tf_op jit(solution)/shard_map/all_to_all | solution.py:21
  203.7 0.7 copy-start.1
